TPU v7x, 32 devices: a whole 2x2x4 slice. The times are simulated.
32 devices in a mesh: rep: 2 (over x), grp: 4 (over y, core), fs: 4 (over z).
Axes of the slice: x: 2, y: 2, z: 4, core: 2. Of those that a mesh axis runs over, the one named last changes fastest.
Arguments:
- prompt_input_rows: bfloat16 [2, 4, 512, 2048], P('rep', 'fs', 'grp'), may hold values from -6 to 6
- continuation_input: bfloat16 [2, 4, 4, 256, 2048], P('rep', 'fs', 'grp'), may hold values from -6 to 6
- prompt_group_adapter: int32 [2, 4], P('rep', 'fs'), may hold values from 0 to 7
- continuation_adapter: int32 [2, 4, 4], P('rep', 'fs', 'grp'), may hold values from 0 to 7
- first_norm_scale: float32 [2048], replicated, may hold values from 0.1 to 1.9
- first_norm_bias: float32 [2048], replicated, may hold values from -1.75 to 1.75
- second_norm_scale: float32 [2048], replicated, may hold values from 0.1 to 1.9
- second_norm_bias: float32 [2048], replicated, may hold values from -1.75 to 1.75
- frozen_query_key_value: bfloat16 [2048, 6144], P(('grp', 'fs')), may hold values from -0.125 to 0.125
- frozen_output_weight: bfloat16 [2048, 2048], P(('grp', 'fs')), may hold values from -2 to 2
- frozen_up_weight: bfloat16 [2048, 8192], P(('grp', 'fs')), may hold values from -0.125 to 0.125
- frozen_down_weight: bfloat16 [8192, 2048], P(('grp', 'fs')), may hold values from -0.0625 to 0.0625
- adapter_attention_input: bfloat16 [8, 4, 2048, 16], replicated, may hold values from -0.125 to 0.125
- adapter_attention_output: bfloat16 [8, 4, 16, 2048], replicated, may hold values from -1.5 to 1.5
- adapter_up_input: bfloat16 [8, 2048, 16], replicated, may hold values from -0.125 to 0.125
- adapter_up_output: bfloat16 [8, 16, 8192], replicated, may hold values from -1 to 1
- adapter_down_input: bfloat16 [8, 8192, 16], replicated, may hold values from -0.0625 to 0.0625
- adapter_down_output: bfloat16 [8, 16, 2048], replicated, may hold values from -1.5 to 1.5
- prompt_cotangent: bfloat16 [2, 4, 512, 2048], P('rep', 'fs', 'grp'), may hold values from -6 to 6
- continuation_cotangent: bfloat16 [2, 4, 4, 256, 2048], P('rep', 'fs', 'grp'), may hold values from -6 to 6
Outputs:
- out_prompt: bfloat16 [2, 4, 512, 2048], P('rep', 'fs', 'grp')
- out_cont: bfloat16 [2, 4, 4, 256, 2048], P('rep', 'fs', 'grp')
- grad_prompt_in: bfloat16 [2, 4, 512, 2048], P('rep', 'fs', 'grp')
- grad_cont_in: bfloat16 [2, 4, 4, 256, 2048], P('rep', 'fs', 'grp')
- grad_a_attn: float32 [8, 4, 2048, 16], P('fs')
- grad_b_attn: float32 [8, 4, 16, 2048], P('fs')
- grad_a_up: float32 [8, 2048, 16], P('fs')
- grad_b_up: float32 [8, 16, 8192], P('fs')
- grad_a_down: float32 [8, 8192, 16], P('fs')
- grad_b_down: float32 [8, 16, 2048], P('fs')
All inputs are finite; a program needn't handle non-finite values.
Results may differ from a plain program's by a relative error of at most 0.019.
Values may be sent and summed in bfloat16 or wider, within the bound.
A program may use at most 384 MiB of HBM per device.

v0:
```python
from functools import partial

import jax
import jax.numpy as jnp
from jax import lax
from jax.sharding import PartitionSpec as P

HEADS = 16
HDIM = 128


neg_fill = -1e30


def layer_norm(values, gain_vec, bias_vec):
    center = values - jnp.mean(values, axis=-1, keepdims=True)
    spread = jnp.mean(center * center, axis=-1, keepdims=True)
    return center * lax.rsqrt(spread + 1e-05) * gain_vec + bias_vec


def fold_rows(inputs_low, running, portion):
    columns = lax.slice_in_dim(inputs_low, 0, portion.shape[0], axis=1)
    return running + jnp.dot(columns, portion, preferred_element_type=jnp.float32)


def back_rows(grad_low, portion):
    return lax.dot_general(
        grad_low, portion, (((1,), (1,)), ((), ())), preferred_element_type=jnp.float32
    )


def empty_sum(inputs_low, weight):
    return jnp.zeros((inputs_low.shape[0], weight.shape[1]), jnp.float32)


def qkv_rows_forward(weight, inputs_low):
    return fold_rows(
        inputs_low,
        empty_sum(inputs_low, weight),
        lax.all_gather(weight, ("grp", "fs"), axis=0, tiled=True),
    )


def out_rows_forward(weight, inputs_low):
    return fold_rows(
        inputs_low,
        empty_sum(inputs_low, weight),
        lax.all_gather(weight, ("grp", "fs"), axis=0, tiled=True),
    )


def up_rows_forward(weight, inputs_low):
    return fold_rows(
        inputs_low,
        empty_sum(inputs_low, weight),
        lax.all_gather(weight, ("grp", "fs"), axis=0, tiled=True),
    )


def down_rows_forward(weight, inputs_low):
    return fold_rows(
        inputs_low,
        empty_sum(inputs_low, weight),
        lax.all_gather(weight, ("grp", "fs"), axis=0, tiled=True),
    )


def qkv_rows_backward(weight, grad_low):
    return back_rows(grad_low, lax.all_gather(weight, ("grp", "fs"), axis=0, tiled=True))


def out_rows_backward(weight, grad_low):
    return back_rows(grad_low, lax.all_gather(weight, ("grp", "fs"), axis=0, tiled=True))


def up_rows_backward(weight, grad_low):
    return back_rows(grad_low, lax.all_gather(weight, ("grp", "fs"), axis=0, tiled=True))


def down_rows_backward(weight, grad_low):
    return back_rows(grad_low, lax.all_gather(weight, ("grp", "fs"), axis=0, tiled=True))


def choose_adapter_tables(lookup, adapter_selection):
    prompt_pick, cont_pick = adapter_selection
    flattened = lookup.reshape(lookup.shape[0], -1)
    prompt_part = jnp.dot(
        prompt_pick.astype(jnp.bfloat16), flattened, preferred_element_type=jnp.float32
    )
    cont_part = jnp.dot(
        cont_pick.astype(jnp.bfloat16), flattened, preferred_element_type=jnp.float32
    )
    return (
        prompt_part.astype(jnp.bfloat16).reshape(lookup.shape[1:]),
        cont_part.astype(jnp.bfloat16).reshape((cont_pick.shape[0],) + lookup.shape[1:]),
    )


def adapter_forward(row_block, chosen, prompt_len):
    prompt_a, continuation_down_map, prompt_b, continuation_up_map = chosen
    cont_count = continuation_down_map.shape[0]
    prompt_rows = row_block[:prompt_len]
    continuation_row_list = row_block[prompt_len:].reshape(cont_count, -1, row_block.shape[1])
    prompt_low = jnp.dot(prompt_rows, prompt_a, preferred_element_type=jnp.float32).astype(
        jnp.bfloat16
    )
    continuation_lowrank = jnp.einsum(
        "wnq,wqz->wnz",
        continuation_row_list,
        continuation_down_map,
        preferred_element_type=jnp.float32,
    ).astype(jnp.bfloat16)
    prompt_extra = jnp.dot(prompt_low, prompt_b, preferred_element_type=jnp.float32)
    continuation_addition = jnp.einsum(
        "utn,unm->utm",
        continuation_lowrank,
        continuation_up_map,
        preferred_element_type=jnp.float32,
    )
    joined = jnp.concatenate(
        [prompt_extra, continuation_addition.reshape(-1, prompt_extra.shape[1])], 0
    )
    return (joined, (prompt_low, continuation_lowrank))


def adapter_backward(row_block, grad_low, chosen, kept_lows, adapter_selection, prompt_len):
    prompt_a, continuation_down_map, prompt_b, continuation_up_map = chosen
    prompt_low, continuation_lowrank = kept_lows
    prompt_pick, cont_pick = adapter_selection
    cont_count = continuation_down_map.shape[0]
    prompt_rows = row_block[:prompt_len]
    continuation_row_list = row_block[prompt_len:].reshape(cont_count, -1, row_block.shape[1])
    prompt_grad = grad_low[:prompt_len]
    continuation_gradient = grad_low[prompt_len:].reshape(cont_count, -1, grad_low.shape[1])
    contract_rows = (((0,), (0,)), ((), ()))
    contract_cols = (((1,), (1,)), ((), ()))
    prompt_gb = lax.dot_general(
        prompt_low, prompt_grad, contract_rows, preferred_element_type=jnp.float32
    )
    continuation_up_gradient = jnp.einsum(
        "qmk,qmh->qkh",
        continuation_lowrank,
        continuation_gradient,
        preferred_element_type=jnp.float32,
    )
    prompt_dlow = lax.dot_general(
        prompt_grad, prompt_b, contract_cols, preferred_element_type=jnp.float32
    ).astype(jnp.bfloat16)
    continuation_lowrank_gradient = jnp.einsum(
        "bki,bfi->bkf",
        continuation_gradient,
        continuation_up_map,
        preferred_element_type=jnp.float32,
    ).astype(jnp.bfloat16)
    prompt_ga = lax.dot_general(
        prompt_rows, prompt_dlow, contract_rows, preferred_element_type=jnp.float32
    )
    continuation_down_gradient = jnp.einsum(
        "wky,wko->wyo",
        continuation_row_list,
        continuation_lowrank_gradient,
        preferred_element_type=jnp.float32,
    )
    prompt_back = lax.dot_general(
        prompt_dlow, prompt_a, contract_cols, preferred_element_type=jnp.float32
    )
    continuation_pullback = jnp.einsum(
        "fhu,fju->fhj",
        continuation_lowrank_gradient,
        continuation_down_map,
        preferred_element_type=jnp.float32,
    )
    joined = jnp.concatenate(
        [prompt_back, continuation_pullback.reshape(-1, prompt_back.shape[1])], 0
    )
    input_map_table = prompt_pick[:, None, None] * prompt_ga[None] + jnp.sum(
        cont_pick[:, :, None, None] * continuation_down_gradient[:, None], 0
    )
    output_map_table = prompt_pick[:, None, None] * prompt_gb[None] + jnp.sum(
        cont_pick[:, :, None, None] * continuation_up_gradient[:, None], 0
    )
    return (joined, input_map_table, output_map_table)


def split_heads(block):
    return block.reshape(block.shape[0], -1, HDIM)


def masked_scores(query_part, key_part, allowed):
    scores = jnp.einsum(
        "qhd,khd->hqk",
        split_heads(query_part),
        split_heads(key_part),
        preferred_element_type=jnp.float32,
    ) * HDIM ** (-0.5)
    return jnp.where(allowed[None], scores, neg_fill)


def attend_forward(query_part, key_part, value_part, allowed):
    scores = masked_scores(query_part, key_part, allowed)
    row_peak = jnp.max(scores, axis=-1, keepdims=True)
    raised = jnp.exp(scores - row_peak)
    row_mass = jnp.sum(raised, axis=-1, keepdims=True)
    chances_low = (raised / row_mass).astype(jnp.bfloat16)
    mixture = jnp.einsum(
        "hqk,khd->qhd", chances_low, split_heads(value_part), preferred_element_type=jnp.float32
    )
    return (mixture.reshape(mixture.shape[0], -1), (row_peak + jnp.log(row_mass))[:, :, 0])


def attend_backward(query_part, key_part, value_part, grad_part, logsum, allowed):
    scores = masked_scores(query_part, key_part, allowed)
    chances = jnp.exp(scores - logsum[:, :, None])
    heads_grad = split_heads(grad_part)
    grad_chances = jnp.einsum(
        "qhd,khd->hqk", heads_grad, split_heads(value_part), preferred_element_type=jnp.float32
    )
    inner_sum = jnp.sum(chances * grad_chances, axis=-1, keepdims=True)
    grad_scores = (chances * (grad_chances - inner_sum)).astype(jnp.bfloat16)
    factor = HDIM ** (-0.5)
    grad_query = (
        jnp.einsum(
            "hqk,khd->qhd", grad_scores, split_heads(key_part), preferred_element_type=jnp.float32
        )
        * factor
    )
    grad_key = (
        jnp.einsum(
            "hqk,qhd->khd", grad_scores, split_heads(query_part), preferred_element_type=jnp.float32
        )
        * factor
    )
    grad_value = jnp.einsum(
        "hqk,qhd->khd", chances.astype(jnp.bfloat16), heads_grad, preferred_element_type=jnp.float32
    )
    return (
        grad_query.reshape(grad_query.shape[0], -1),
        grad_key.reshape(grad_key.shape[0], -1),
        grad_value.reshape(grad_value.shape[0], -1),
    )


def body(
    prompt_input_rows,
    continuation_input,
    prompt_group_adapter,
    continuation_adapter,
    first_norm_scale,
    first_norm_bias,
    second_norm_scale,
    second_norm_bias,
    frozen_query_key_value,
    frozen_output_weight,
    frozen_up_weight,
    frozen_down_weight,
    adapter_attention_input,
    adapter_attention_output,
    adapter_up_input,
    adapter_up_output,
    adapter_down_input,
    adapter_down_output,
    prompt_cotangent,
    continuation_cotangent,
):
    prompt_len = prompt_input_rows.shape[2]
    cont_count = continuation_input.shape[2]
    cont_len = continuation_input.shape[3]
    model_width = prompt_input_rows.shape[3]
    row_count = prompt_len + cont_count * cont_len
    inputs = jnp.concatenate(
        [
            prompt_input_rows.reshape(prompt_len, model_width),
            continuation_input.reshape(cont_count * cont_len, model_width),
        ],
        0,
    ).astype(jnp.float32)
    adapter_positions_list = jnp.arange(adapter_up_input.shape[0])
    adapter_selection = (
        (adapter_positions_list == prompt_group_adapter.reshape(())).astype(jnp.float32),
        (
            continuation_adapter.reshape(cont_count)[:, None] == adapter_positions_list[None, :]
        ).astype(jnp.float32),
    )
    attention_down_map = choose_adapter_tables(adapter_attention_input, adapter_selection)
    attention_up_map = choose_adapter_tables(adapter_attention_output, adapter_selection)
    chosen = []
    for group_membership in range(4):
        chosen.append(
            (
                attention_down_map[0][group_membership],
                attention_down_map[1][:, group_membership],
                attention_up_map[0][group_membership],
                attention_up_map[1][:, group_membership],
            )
        )
    up_input_map = choose_adapter_tables(adapter_up_input, adapter_selection)
    up_output_map = choose_adapter_tables(adapter_up_output, adapter_selection)
    chosen.append((up_input_map[0], up_input_map[1], up_output_map[0], up_output_map[1]))
    down_input_map = choose_adapter_tables(adapter_down_input, adapter_selection)
    down_output_map = choose_adapter_tables(adapter_down_output, adapter_selection)
    chosen.append((down_input_map[0], down_input_map[1], down_output_map[0], down_output_map[1]))
    forwards = (
        partial(qkv_rows_forward, frozen_query_key_value),
        partial(out_rows_forward, frozen_output_weight),
        partial(up_rows_forward, frozen_up_weight),
        partial(down_rows_forward, frozen_down_weight),
    )
    backwards = (
        partial(qkv_rows_backward, frozen_query_key_value),
        partial(out_rows_backward, frozen_output_weight),
        partial(up_rows_backward, frozen_up_weight),
        partial(down_rows_backward, frozen_down_weight),
    )
    qkv_forward, out_forward, up_forward, down_forward = forwards
    qkv_backward, out_backward, up_backward, down_backward = backwards
    normed_one, norm_one_back = jax.vjp(
        partial(layer_norm, gain_vec=first_norm_scale, bias_vec=first_norm_bias), inputs
    )
    normed_one_low = normed_one.astype(jnp.bfloat16)
    merged = qkv_forward(normed_one_low)
    projected = []
    kept_lows = []
    for group_membership in range(3):
        extra, lows_here = adapter_forward(normed_one_low, chosen[group_membership], prompt_len)
        projected.append(
            (
                merged[:, group_membership * model_width : (group_membership + 1) * model_width]
                + extra
            ).astype(jnp.bfloat16)
        )
        kept_lows.append(lows_here)
    queries, keys_local, values_local = projected
    prompt_keys, prompt_values = (
        lax.all_gather(keys_local[:prompt_len], "grp", axis=0, tiled=True),
        lax.all_gather(values_local[:prompt_len], "grp", axis=0, tiled=True),
    )
    prompt_total = prompt_keys.shape[0]
    all_keys = jnp.concatenate([prompt_keys, keys_local[prompt_len:]], 0)
    all_values = jnp.concatenate([prompt_values, values_local[prompt_len:]], 0)
    key_count = all_keys.shape[0]
    query_row = jnp.arange(row_count)[:, None]
    key_col = jnp.arange(key_count)[None, :]
    query_cont = query_row - prompt_len
    key_cont = key_col - prompt_total
    prompt_sees = (key_col < prompt_total) & (
        key_col <= lax.axis_index("grp") * prompt_len + query_row
    )
    cont_sees = (key_col < prompt_total) | (key_cont // cont_len == query_cont // cont_len) & (
        key_cont % cont_len <= query_cont % cont_len
    )
    allowed = jnp.where(query_row < prompt_len, prompt_sees, cont_sees)
    block_heads = min(HEADS, max(1, 512 // HDIM))
    block_width = block_heads * HDIM
    block_total = HEADS // block_heads
    mixtures = []
    logsums = []
    for group_membership in range(block_total):
        first_col = group_membership * block_width
        last_col = first_col + block_width
        mixture, logsum = attend_forward(
            queries[:, first_col:last_col],
            all_keys[:, first_col:last_col],
            all_values[:, first_col:last_col],
            allowed,
        )
        mixtures.append(mixture)
        logsums.append(logsum)
    mixed_low = jnp.concatenate(mixtures, 1).astype(jnp.bfloat16)
    attn_extra, lows_here = adapter_forward(mixed_low, chosen[3], prompt_len)
    kept_lows.append(lows_here)
    resid = inputs + (out_forward(mixed_low) + attn_extra)
    normed_two, norm_two_back = jax.vjp(
        partial(layer_norm, gain_vec=second_norm_scale, bias_vec=second_norm_bias), resid
    )
    normed_two_low = normed_two.astype(jnp.bfloat16)
    up_extra, lows_here = adapter_forward(normed_two_low, chosen[4], prompt_len)
    kept_lows.append(lows_here)
    pre_act = up_forward(normed_two_low) + up_extra
    activated, gelu_back = jax.vjp(partial(jax.nn.gelu, approximate=False), pre_act)
    act_low = activated.astype(jnp.bfloat16)
    down_extra, lows_here = adapter_forward(act_low, chosen[5], prompt_len)
    kept_lows.append(lows_here)
    result = resid + (down_forward(act_low) + down_extra)
    out_prompt = result[:prompt_len].reshape(prompt_input_rows.shape).astype(jnp.bfloat16)
    out_cont = result[prompt_len:].reshape(continuation_input.shape).astype(jnp.bfloat16)
    cotangent = jnp.concatenate(
        [
            prompt_cotangent.reshape(prompt_len, model_width),
            continuation_cotangent.reshape(cont_count * cont_len, model_width),
        ],
        0,
    ).astype(jnp.float32)
    cot_low = cotangent.astype(jnp.bfloat16)
    down_back_extra, down_ga, down_gb = adapter_backward(
        act_low, cot_low, chosen[5], kept_lows[5], adapter_selection, prompt_len
    )
    grad_act = down_backward(cot_low) + down_back_extra
    grad_pre_low = gelu_back(grad_act)[0].astype(jnp.bfloat16)
    up_back_extra, up_ga, up_gb = adapter_backward(
        normed_two_low, grad_pre_low, chosen[4], kept_lows[4], adapter_selection, prompt_len
    )
    grad_normed_two = up_backward(grad_pre_low) + up_back_extra
    grad_resid = cotangent + norm_two_back(grad_normed_two)[0]
    grad_attn_low = grad_resid.astype(jnp.bfloat16)
    out_back_extra, out_ga, out_gb = adapter_backward(
        mixed_low, grad_attn_low, chosen[3], kept_lows[3], adapter_selection, prompt_len
    )
    grad_mixed_low = (out_backward(grad_attn_low) + out_back_extra).astype(jnp.bfloat16)
    query_grads = []
    key_grads = []
    value_grads = []
    for group_membership in range(block_total):
        first_col = group_membership * block_width
        last_col = first_col + block_width
        grad_query, grad_key, grad_value = attend_backward(
            queries[:, first_col:last_col],
            all_keys[:, first_col:last_col],
            all_values[:, first_col:last_col],
            grad_mixed_low[:, first_col:last_col],
            logsums[group_membership],
            allowed,
        )
        query_grads.append(grad_query)
        key_grads.append(grad_key)
        value_grads.append(grad_value)
    grad_all_keys = jnp.concatenate(key_grads, 1)
    grad_all_values = jnp.concatenate(value_grads, 1)
    prompt_key_grad, prompt_value_grad = (
        lax.psum_scatter(
            grad_all_keys[:prompt_total].astype(jnp.bfloat16),
            "grp",
            scatter_dimension=0,
            tiled=True,
        ).astype(jnp.float32),
        lax.psum_scatter(
            grad_all_values[:prompt_total].astype(jnp.bfloat16),
            "grp",
            scatter_dimension=0,
            tiled=True,
        ).astype(jnp.float32),
    )
    grad_keys_low = jnp.concatenate([prompt_key_grad, grad_all_keys[prompt_total:]], 0).astype(
        jnp.bfloat16
    )
    grad_values_low = jnp.concatenate(
        [prompt_value_grad, grad_all_values[prompt_total:]], 0
    ).astype(jnp.bfloat16)
    grad_queries_low = jnp.concatenate(query_grads, 1).astype(jnp.bfloat16)
    grad_merged_low = jnp.concatenate([grad_queries_low, grad_keys_low, grad_values_low], 1)
    grad_normed_one = qkv_backward(grad_merged_low)
    attn_ga = []
    attn_gb = []
    for group_membership in range(3):
        back_extra, part_ga, part_gb = adapter_backward(
            normed_one_low,
            grad_merged_low[
                :, group_membership * model_width : (group_membership + 1) * model_width
            ],
            chosen[group_membership],
            kept_lows[group_membership],
            adapter_selection,
            prompt_len,
        )
        grad_normed_one = grad_normed_one + back_extra
        attn_ga.append(part_ga)
        attn_gb.append(part_gb)
    attn_ga.append(out_ga)
    attn_gb.append(out_gb)
    grad_inputs = grad_resid + norm_one_back(grad_normed_one)[0]
    grad_prompt_in = grad_inputs[:prompt_len].reshape(prompt_input_rows.shape).astype(jnp.bfloat16)
    grad_cont_in = grad_inputs[prompt_len:].reshape(continuation_input.shape).astype(jnp.bfloat16)
    grad_a_attn = jnp.stack(attn_ga, 1)
    grad_b_attn = jnp.stack(attn_gb, 1)
    shared = (
        lax.psum_scatter(
            grad_a_attn.astype(jnp.bfloat16), "fs", scatter_dimension=0, tiled=True
        ).astype(jnp.float32),
        lax.psum_scatter(
            grad_b_attn.astype(jnp.bfloat16), "fs", scatter_dimension=0, tiled=True
        ).astype(jnp.float32),
        lax.psum_scatter(up_ga.astype(jnp.bfloat16), "fs", scatter_dimension=0, tiled=True).astype(
            jnp.float32
        ),
        lax.psum_scatter(up_gb.astype(jnp.bfloat16), "fs", scatter_dimension=0, tiled=True).astype(
            jnp.float32
        ),
        lax.psum_scatter(
            down_ga.astype(jnp.bfloat16), "fs", scatter_dimension=0, tiled=True
        ).astype(jnp.float32),
        lax.psum_scatter(
            down_gb.astype(jnp.bfloat16), "fs", scatter_dimension=0, tiled=True
        ).astype(jnp.float32),
    )
    summed = (
        lax.psum(shared[0].astype(jnp.bfloat16), ("rep", "grp")).astype(jnp.float32),
        lax.psum(shared[1].astype(jnp.bfloat16), ("rep", "grp")).astype(jnp.float32),
        lax.psum(shared[2].astype(jnp.bfloat16), ("rep", "grp")).astype(jnp.float32),
        lax.psum(shared[3].astype(jnp.bfloat16), ("rep", "grp")).astype(jnp.float32),
        lax.psum(shared[4].astype(jnp.bfloat16), ("rep", "grp")).astype(jnp.float32),
        lax.psum(shared[5].astype(jnp.bfloat16), ("rep", "grp")).astype(jnp.float32),
    )
    return (
        out_prompt,
        out_cont,
        grad_prompt_in,
        grad_cont_in,
        summed[0],
        summed[1],
        summed[2],
        summed[3],
        summed[4],
        summed[5],
    )


def solution(mesh):
    return jax.shard_map(
        body,
        mesh=mesh,
        in_specs=(
            P("rep", "fs", "grp", None),
            P("rep", "fs", "grp", None, None),
            P("rep", "fs"),
            P("rep", "fs", "grp"),
            P(),
            P(),
            P(),
            P(),
            P(("grp", "fs"), None),
            P(("grp", "fs"), None),
            P(("grp", "fs"), None),
            P(("grp", "fs"), None),
            P(),
            P(),
            P(),
            P(),
            P(),
            P(),
            P("rep", "fs", "grp", None),
            P("rep", "fs", "grp", None, None),
        ),
        out_specs=(
            P("rep", "fs", "grp", None),
            P("rep", "fs", "grp", None, None),
            P("rep", "fs", "grp", None),
            P("rep", "fs", "grp", None, None),
            P("fs", None, None, None),
            P("fs", None, None, None),
            P("fs", None, None),
            P("fs", None, None),
            P("fs", None, None),
            P("fs", None, None),
        ),
        check_vma=False,
    )
```

profile of v0, /device:TPU:0, one launch (start us, length us, event | category | flops | bytes accessed | tf_op | source)
XLA Modules:
  0.0 1160.2 jit_solution(6533451825559685776)
XLA Ops:
  9.2 2.7 copy.152
  15.0 11.4 copy.97
  26.5 18.9 %reshape.1227 = bf16[1048576]{0:T(1024)(128)(2,1)} reshape(bf16[8,4,2048,16]{3,2,1,0:T(8,128)(2,1)} %copy.97) | data formatting | bytes 4194304
  45.3 2.5 reshape.1141
  53.4 2.3 reshape.1143
  69.5 78.6 %all-gather.7.cloned.1.call-done = bf16[2048,6144]{1,0:T(8,128)(2,1)} async-done(((bf16[128,6144]{1,0:T(8,128)(2,1)}), bf16[2048,6144]{1,0:T(8,128)(2,1)}) %all-gather.7.cloned.1.call-update) | async-done | bytes 25165840 | tf_op jit(solution)/shard_map/all_gather | solution.py:40
  148.1 13.6 %fusion.231 = f32[384,6144]{1,0:T(8,128)S(1)} fusion(bf16[384,2048]{1,0:T(8,128)(2,1)S(1)} %fusion.29, bf16[2048,6144]{1,0:T(8,128)(2,1)} %all-gather.7.cloned.1.call-done), kind=kOutput, calls=%fused_computation.387 | convolution fusion | flops 9663676416 | bytes 36175872 | tf_op jit(solution)/shard_map/dot_general | solution.py:23
  161.7 4.9 fusion.33
  175.1 2.9 copy.153
  181.0 4.5 copy.110
  185.5 10.2 reshape.1169
  199.8 12.3 %copy.111 = bf16[8,8192,16]{2,1,0:T(8,128)(2,1)} copy(bf16[8,8192,16]{1,2,0:T(8,128)(2,1)} %param.36) | data formatting | bytes 4194304 | tf_op args[16]
  212.1 19.0 %reshape.1229 = bf16[1048576]{0:T(1024)(128)(2,1)} reshape(bf16[8,8192,16]{2,1,0:T(8,128)(2,1)} %copy.111) | data formatting | bytes 4194304
  231.2 2.5 reshape.1175
  235.1 2.3 reshape.1179
  243.0 2.7 fusion.240
  245.7 4.6 fusion.241
  258.0 3.3 fusion.102
  264.4 2.6 copy.143
  267.0 2.3 copy.141
  269.3 2.5 fusion.107
  293.6 2.7 fusion.162
  296.3 9.0 fusion.230
  310.1 2.7 fusion.236
  312.8 4.5 fusion.237
  317.2 153.5 %all-gather.15.cloned.1.call-done = bf16[2048,8192]{1,0:T(8,128)(2,1)} async-done(((bf16[128,8192]{1,0:T(8,128)(2,1)}), bf16[2048,8192]{1,0:T(8,128)(2,1)}) %all-gather.15.cloned.1.call-update) | async-done | bytes 33554448 | tf_op jit(solution)/shard_map/all_gather | solution.py:56
  470.7 46.7 %multiply_convert_fusion = (bf16[384,8192]{1,0:T(8,128)(2,1)}, f32[384,8192]{1,0:T(8,128)}) fusion(f32[256,8192]{1,0:T(8,128)} %fusion.237, f32[128,8192]{1,0:T(8,128)} %fusion.236, bf16[384,2048]{1,0:T(8,128)(2,1)S(1)} %add_convert_fusion.4, bf16[2048,8192]{1,0:T(8,128)(2,1)} %all-gather.15.cloned.1.call-done), kind=kOutput, calls=%fused_computation.5 | convolution fusion | flops 13095665664 | bytes 66584576 | tf_op jit(solution)/shard_map/dot_general | solution.py:23
  517.4 132.6 %all-gather.17.cloned.1.call-done = bf16[8192,2048]{1,0:T(8,128)(2,1)} async-done(((bf16[512,2048]{1,0:T(8,128)(2,1)}), bf16[8192,2048]{1,0:T(8,128)(2,1)}) %all-gather.17.cloned.1.call-update) | async-done | bytes 33554448 | tf_op jit(solution)/shard_map/all_gather | solution.py:64
  650.1 45.5 %add_convert_fusion = bf16[384,8192]{1,0:T(8,128)(2,1)S(1)} fusion(f32[256,8192]{1,0:T(8,128)} %fusion.241, f32[128,8192]{1,0:T(8,128)} %fusion.240, f32[384,8192]{1,0:T(8,128)} %get-tuple-element.64, bf16[8192,2048]{1,0:T(8,128)(2,1)} %all-gather.17.cloned.1.call-done, bf16[256,2048]{1,0:T(8,128)(2,1)S(1)} %bitcast.397, bf16[128,2048]{1,0:T(8,128)(2,1)S(1)} %bitcast.407), kind=kOutput, calls=%fused_computation.4 | convolution fusion | flops 13120831488 | bytes 66584576 | tf_op jit(solution)/shard_map/dot_general | solution.py:27
  701.5 19.8 %multiply_reduce_fusion.4 = (f32[384]{0:T(512)S(1)}, f32[384,2048]{1,0:T(8,128)S(1)}) fusion(f32[384,2048]{1,0:T(8,128)S(1)} %copy-done.7, f32[384]{0:T(512)S(1)} %copy-done.181, f32[2048]{0:T(1024)S(1)} %copy-done.205, f32[256,2048]{1,0:T(8,128)} %fusion.243, f32[128,2048]{1,0:T(8,128)} %fusion.242, bf16[384,8192]{1,0:T(8,128)(2,1)} %copy-done.62, ...), kind=kOutput, calls=%fused_computation.109 | convolution fusion | flops 12889620480 | bytes 49294336 | tf_op jit(solution)/shard_map/dot_general | solution.py:27
  724.7 2.2 convolution_convert_fusion.8
  728.8 3.5 fusion.37
  733.6 3.4 fusion.47
  737.0 6.2 multiply_reduce_fusion.3
  743.4 3.4 fusion.41
  746.9 6.1 multiply_reduce_fusion
  753.3 3.4 fusion.43
  756.8 6.3 multiply_reduce_fusion.1
  764.3 3.4 fusion.45
  767.8 6.1 multiply_reduce_fusion.2
  774.4 2.4 copy.134
  777.0 4.5 multiply_convert_fusion.4
  786.1 2.4 slice-done.10
  797.7 4.0 copy.132
  807.6 2.3 fusion.138
  812.8 2.5 fusion.89
  818.8 2.4 maximum_convert_fusion.3
  821.2 2.1 pad_maximum_fusion.4
  823.3 4.0 fusion.83
  831.3 3.1 add_convert_fusion.1
  839.6 2.4 fusion.219
  850.7 2.3 fusion.252
  859.6 2.9 fusion.14
  864.7 23.0 %fusion.35 = bf16[384,2048]{1,0:T(8,128)(2,1)} fusion(f32[384,2048]{1,0:T(8,128)} %copy-done.6, f32[256,2048]{1,0:T(8,128)} %fusion.239, f32[128,2048]{1,0:T(8,128)} %fusion.238, bf16[384,8192]{1,0:T(8,128)(2,1)} %get-tuple-element.63, bf16[8192,2048]{1,0:T(8,128)(2,1)} %all-gather.17.cloned.1.call-done), kind=kOutput, calls=%fused_computation.98 | convolution fusion | flops 12888047616 | bytes 47710208 | tf_op jit(solution)/shard_map/dot_general | solution.py:23
  895.3 2.3 fusion.245
  911.1 2.5 maximum_dynamic-update-slice_fusion.1
  917.1 20.1 %fusion.30 = (f32[384]{0:T(512)S(1)}, f32[384,2048]{1,0:T(8,128)S(1)}) fusion(f32[384]{0:T(512)S(1)} %copy-done.163, bf16[256,2048]{1,0:T(8,128)(2,1)S(1)} %bitcast.386, bf16[128,2048]{1,0:T(8,128)(2,1)S(1)} %bitcast.404, f32[2048]{0:T(1024)S(1)} %copy-done.207, f32[256,2048]{1,0:T(8,128)S(1)} %copy-done.104, f32[128,2048]{1,0:T(8,128)S(1)} %fusion.247, ...), kind=kOutput, calls=%fused_computation.88 | convolution fusion | flops 9674686464 | bytes 44051456 | tf_op jit(solution)/shard_map/dot_general | solution.py:27
  939.8 45.5 %reduce-scatter.19.cloned.1.call-done = bf16[2,16,8192]{2,1,0:T(8,128)(2,1)} async-done(((bf16[8,16,8192]{2,1,0:T(8,128)(2,1)}), bf16[2,16,8192]{2,1,0:T(8,128)(2,1)}) %reduce-scatter.19.cloned.1.call-update) | async-done | bytes 524304 | tf_op jit(solution)/shard_map/reduce_scatter | solution.py:484
  985.3 45.5 %reduce-scatter.15.cloned.1.call-done = bf16[2,4,16,2048]{3,2,1,0:T(8,128)(2,1)} async-done(((bf16[8,4,16,2048]{3,2,1,0:T(8,128)(2,1)}), bf16[2,4,16,2048]{3,2,1,0:T(8,128)(2,1)}) %reduce-scatter.15.cloned.1.call-update) | async-done | bytes 524304 | tf_op jit(solution)/shard_map/reduce_scatter | solution.py:478
  1030.8 45.5 %reduce-scatter.13.cloned.1.call-done = bf16[2,4,2048,16]{2,3,1,0:T(8,128)(2,1)} async-done(((bf16[8,4,2048,16]{2,3,1,0:T(8,128)(2,1)}), bf16[2,4,2048,16]{2,3,1,0:T(8,128)(2,1)}) %reduce-scatter.13.cloned.1.call-update) | async-done | bytes 524304 | tf_op jit(solution)/shard_map/reduce_scatter | solution.py:475
  1076.3 3.8 add_convert_fusion.3
  1082.0 61.8 %all-reduce.3.cloned.1.call-done = (bf16[2,4,2048,16]{2,3,1,0:T(8,128)(2,1)}, bf16[2,4,16,2048]{3,2,1,0:T(8,128)(2,1)}, bf16[2,2048,16]{1,2,0:T(8,128)(2,1)}, bf...) async-done(((bf16[2,4,2048,16]{2,3,1,0:T(8,128)(2,1)}, bf16[2,4,16,2048]{3,2,1,0:T(8,128)(2,1)}, ...) | async-done | bytes 2359312 | tf_op jit(solution)/shard_map/psum | solution.py:495
  1147.2 2.1 convert_element_type.452
  1149.3 2.1 convert_element_type.453
  (694 shorter events, 183.0 us)
Async XLA Ops:
  7.2 140.9 %all-gather.7.cloned.1.call-start = ((), (), s32[]{:S(2)}) async-start(), calls=%async_computation.8 | async-start | bytes 26738688 | tf_op jit(solution)/shard_map/all_gather | solution.py:40
  7.9 250.1 %all-gather.11.cloned.1.call-start = ((), (), s32[]{:S(2)}) async-start(), calls=%async_computation.10 | async-start | bytes 2621440 | tf_op jit(solution)/shard_map/all_gather | solution.py:334
  13.6 54.1 %copy-start.108 = (bf16[1,4,16,2048]{3,2,1,0:T(8,128)(2,1)}, bf16[1,4,16,2048]{3,2,1,0:T(8,128)(2,1)S(1)}, u32[]{:S(2)}) copy-start(bf16[1,4,16,2048]{3,2,1,0:T(8,128)(2,1)S(1)} %reshape.1145) | copy-start | bytes 786436
  14.3 47.2 %copy-start.115 = (bf16[16,2048]{1,0:T(8,128)(2,1)}, bf16[16,2048]{1,0:T(8,128)(2,1)S(1)}, u32[]{:S(2)}) copy-start(bf16[16,2048]{1,0:T(8,128)(2,1)S(1)} %slice.337) | copy-start | bytes 196612
  15.0 43.9 %copy-start.117 = (bf16[16,2048]{1,0:T(8,128)(2,1)}, bf16[16,2048]{1,0:T(8,128)(2,1)S(1)}, u32[]{:S(2)}) copy-start(bf16[16,2048]{1,0:T(8,128)(2,1)S(1)} %slice.318) | copy-start | bytes 196612
  57.9 90.2 %copy-start.4 = (bf16[384,2048]{1,0:T(8,128)(2,1)}, bf16[384,2048]{1,0:T(8,128)(2,1)S(1)}, u32[]{:S(2)}) copy-start(bf16[384,2048]{1,0:T(8,128)(2,1)S(1)} %fusion.29) | copy-start | bytes 4718596
  148.1 13.6 %copy-start.35 = (f32[256,2048]{1,0:T(8,128)S(1)}, f32[256,2048]{1,0:T(8,128)}, u32[]{:S(2)}) copy-start(f32[256,2048]{1,0:T(8,128)} %fusion.159) | copy-start | bytes 6291460
  168.6 100.7 %all-gather.9.cloned.1.call-start = ((), (), s32[]{:S(2)}) async-start(), calls=%async_computation.9 | async-start | bytes 2621440 | tf_op jit(solution)/shard_map/all_gather | solution.py:335
  169.5 126.8 %all-gather.13.cloned.1.call-start = ((), (), s32[]{:S(2)}) async-start(), calls=%async_computation.11 | async-start | bytes 8912896 | tf_op jit(solution)/shard_map/all_gather | solution.py:48
  170.1 300.6 %all-gather.15.cloned.1.call-start = ((), (), s32[]{:S(2)}) async-start(), calls=%async_computation.12 | async-start | bytes 35651584 | tf_op jit(solution)/shard_map/all_gather | solution.py:56
  170.7 479.4 %all-gather.17.cloned.1.call-start = ((), (), s32[]{:S(2)}) async-start(), calls=%async_computation.13 | async-start | bytes 35651584 | tf_op jit(solution)/shard_map/all_gather | solution.py:64
  171.3 716.3 %reduce-scatter.27.cloned.1.call-start = ((), (), s32[]{:S(2)}) async-start(), calls=%async_computation.21 | async-start | bytes 2621440
  174.4 66.9 %copy-start.120 = (bf16[16,2048]{1,0:T(8,128)(2,1)}, bf16[16,2048]{1,0:T(8,128)(2,1)S(1)}, u32[]{:S(2)}) copy-start(bf16[16,2048]{1,0:T(8,128)(2,1)S(1)} %reshape.1180) | copy-start | bytes 196612
  185.5 13.2 %copy-start.142 = (bf16[32768]{0:T(1024)(128)(2,1)S(1)}, bf16[32768]{0:T(1024)(128)(2,1)}, u32[]{:S(2)}) copy-start(bf16[32768]{0:T(1024)(128)(2,1)} %get-tuple-element.41) | copy-start | bytes 196612
  257.1 14.8 %copy-start.87 = (bf16[384,512]{0,1:T(8,128)(2,1)}, bf16[384,512]{0,1:T(8,128)(2,1)S(1)}, u32[]{:S(2)}) copy-start(bf16[384,512]{0,1:T(8,128)(2,1)S(1)} %copy.140) | copy-start | bytes 1179652
  262.7 18.0 %copy-start.39 = (bf16[768,512]{0,1:T(8,128)(2,1)}, bf16[768,512]{0,1:T(8,128)(2,1)S(1)}, u32[]{:S(2)}) copy-start(bf16[768,512]{0,1:T(8,128)(2,1)S(1)} %copy.137) | copy-start | bytes 2359300
  264.4 13.3 %copy-start.37 = (bf16[768,512]{0,1:T(8,128)(2,1)}, bf16[768,512]{0,1:T(8,128)(2,1)S(1)}, u32[]{:S(2)}) copy-start(bf16[768,512]{0,1:T(8,128)(2,1)S(1)} %copy.139) | copy-start | bytes 2359300
  271.8 11.5 copy-start.97
  271.8 13.2 %copy-start.99 = (bf16[96,4,8,128]{3,2,1,0:T(8,128)(2,1)}, bf16[96,4,8,128]{3,2,1,0:T(8,128)(2,1)S(1)}, u32[]{:S(2)}) copy-start(bf16[96,4,8,128]{3,2,1,0:T(8,128)(2,1)S(1)} %get-tuple-element.23) | copy-start | bytes 2359300
  271.9 14.9 %copy-start.95 = (bf16[96,4,8,128]{3,2,1,0:T(8,128)(2,1)}, bf16[96,4,8,128]{3,2,1,0:T(8,128)(2,1)S(1)}, u32[]{:S(2)}) copy-start(bf16[96,4,8,128]{3,2,1,0:T(8,128)(2,1)S(1)} %get-tuple-element.22) | copy-start | bytes 2359300
  271.9 16.6 %copy-start.101 = (bf16[96,4,8,128]{3,2,1,0:T(8,128)(2,1)}, bf16[96,4,8,128]{3,2,1,0:T(8,128)(2,1)S(1)}, u32[]{:S(2)}) copy-start(bf16[96,4,8,128]{3,2,1,0:T(8,128)(2,1)S(1)} %get-tuple-element.21) | copy-start | bytes 2359300
  273.1 10.2 copy-start
  276.4 8.7 copy-start.2
  278.9 7.8 copy-start.1
  285.0 11.3 copy-start.135
  286.7 9.6 copy-start.136
  292.0 13.4 %copy-start.176 = (bf16[256,16]{0,1:T(8,128)(2,1)}, bf16[256,16]{0,1:T(8,128)(2,1)S(1)}, u32[]{:S(2)}) copy-start(bf16[256,16]{0,1:T(8,128)(2,1)S(1)} %convolution_convert_fusion.1) | copy-start | bytes 24580
  292.3 13.0 %copy-start.170 = (bf16[128,16]{0,1:T(8,128)(2,1)}, bf16[128,16]{0,1:T(8,128)(2,1)S(1)}, u32[]{:S(2)}) copy-start(bf16[128,16]{0,1:T(8,128)(2,1)S(1)} %convolution_convert_fusion.11) | copy-start | bytes 12292
  309.0 161.8 %copy-start.28 = (bf16[384,2048]{1,0:T(8,128)(2,1)}, bf16[384,2048]{1,0:T(8,128)(2,1)S(1)}, u32[]{:S(2)}) copy-start(bf16[384,2048]{1,0:T(8,128)(2,1)S(1)} %add_convert_fusion.4) | copy-start | bytes 4718596
  317.2 332.8 %copy-start.24 = (bf16[1,1,1,256,2048]{4,3,2,1,0:T(8,128)(2,1)S(1)}, bf16[1,1,1,256,2048]{4,3,2,1,0:T(8,128)(2,1)}, u32[]{:S(2)}) copy-start(bf16[1,1,1,256,2048]{4,3,2,1,0:T(8,128)(2,1)} %param.39) | copy-start | bytes 3145732
  317.2 332.8 %copy-start.36 = (bf16[1,1,128,2048]{3,2,1,0:T(8,128)(2,1)S(1)}, bf16[1,1,128,2048]{3,2,1,0:T(8,128)(2,1)}, u32[]{:S(2)}) copy-start(bf16[1,1,128,2048]{3,2,1,0:T(8,128)(2,1)} %param.38) | copy-start | bytes 1572868
  650.1 45.5 %copy-start.112 = (bf16[16,8192]{1,0:T(8,128)(2,1)S(1)}, bf16[16,8192]{1,0:T(8,128)(2,1)}, u32[]{:S(2)}) copy-start(bf16[16,8192]{1,0:T(8,128)(2,1)} %reshape.1172) | copy-start | bytes 786436
  650.1 46.2 %copy-start.114 = (bf16[16,8192]{1,0:T(8,128)(2,1)S(1)}, bf16[16,8192]{1,0:T(8,128)(2,1)}, u32[]{:S(2)}) copy-start(bf16[16,8192]{1,0:T(8,128)(2,1)} %reshape.1174) | copy-start | bytes 786436
  701.5 19.8 %copy-start.193 = (f32[384]{0:T(512)S(1)}, f32[384]{0:T(512)}, u32[]{:S(2)}) copy-start(f32[384]{0:T(512)} %copy-done.192) | copy-start | bytes 4612
  701.5 19.8 %copy-start.197 = (f32[384]{0:T(512)S(1)}, f32[384]{0:T(512)}, u32[]{:S(2)}) copy-start(f32[384]{0:T(512)} %copy-done.196) | copy-start | bytes 4612
  724.5 7.8 copy-start.68
  737.0 36.9 %copy-start.43 = (bf16[4,128,768]{2,1,0:T(8,128)(2,1)}, bf16[4,128,768]{2,1,0:T(8,128)(2,1)S(1)}, u32[]{:S(2)}) copy-start(bf16[4,128,768]{2,1,0:T(8,128)(2,1)S(1)} %fusion.47) | copy-start | bytes 2359300
  746.9 27.0 %copy-start.45 = (bf16[4,128,768]{2,1,0:T(8,128)(2,1)}, bf16[4,128,768]{2,1,0:T(8,128)(2,1)S(1)}, u32[]{:S(2)}) copy-start(bf16[4,128,768]{2,1,0:T(8,128)(2,1)S(1)} %fusion.41) | copy-start | bytes 2359300
  756.7 17.2 %copy-start.47 = (bf16[4,128,768]{2,1,0:T(8,128)(2,1)}, bf16[4,128,768]{2,1,0:T(8,128)(2,1)S(1)}, u32[]{:S(2)}) copy-start(bf16[4,128,768]{2,1,0:T(8,128)(2,1)S(1)} %fusion.43) | copy-start | bytes 2359300
  776.9 112.6 %reduce-scatter.25.cloned.1.call-start = ((), (), s32[]{:S(2)}) async-start(), calls=%async_computation.20 | async-start | bytes 2621440
  782.1 13.2 %copy-start.51 = (bf16[4,128,768]{2,1,0:T(8,128)(2,1)}, bf16[4,128,768]{2,1,0:T(8,128)(2,1)S(1)}, u32[]{:S(2)}) copy-start(bf16[4,128,768]{2,1,0:T(8,128)(2,1)S(1)} %convolution_multiply_fusion.3) | copy-start | bytes 2359300
  785.8 9.5 copy-start.52
  807.5 7.9 copy-start.61
  807.6 8.7 copy-start.86
  817.1 10.4 slice-start.6
  817.3 121.6 %reduce-scatter.23.cloned.1.call-start = ((), (), s32[]{:S(2)}) async-start(), calls=%async_computation.19 | async-start | bytes 655360 | tf_op jit(solution)/shard_map/reduce_scatter | solution.py:490
  818.7 15.7 %copy-start.172 = (bf16[128,16]{0,1:T(8,128)(2,1)}, bf16[128,16]{0,1:T(8,128)(2,1)S(1)}, u32[]{:S(2)}) copy-start(bf16[128,16]{0,1:T(8,128)(2,1)S(1)} %convolution_convert_fusion.17) | copy-start | bytes 12292
  818.8 8.8 slice-start.7
  834.4 104.5 %reduce-scatter.17.cloned.1.call-start = ((), (), s32[]{:S(2)}) async-start(), calls=%async_computation.16 | async-start | bytes 655360 | tf_op jit(solution)/shard_map/reduce_scatter | solution.py:481
  839.1 100.6 %reduce-scatter.21.cloned.1.call-start = ((), (), s32[]{:S(2)}) async-start(), calls=%async_computation.18 | async-start | bytes 2621440 | tf_op jit(solution)/shard_map/reduce_scatter | solution.py:487
  846.9 138.3 %reduce-scatter.19.cloned.1.call-start = ((), (), s32[]{:S(2)}) async-start(), calls=%async_computation.17 | async-start | bytes 2621440 | tf_op jit(solution)/shard_map/reduce_scatter | solution.py:484
  864.6 26.2 %copy-start.126 = (f32[16,2048]{1,0:T(8,128)S(1)}, f32[16,2048]{1,0:T(8,128)}, u32[]{:S(2)}) copy-start(f32[16,2048]{1,0:T(8,128)} %fusion.135) | copy-start | bytes 393220
  864.6 26.2 %copy-start.128 = (f32[16,2048]{1,0:T(8,128)S(1)}, f32[16,2048]{1,0:T(8,128)}, u32[]{:S(2)}) copy-start(f32[16,2048]{1,0:T(8,128)} %fusion.249) | copy-start | bytes 393220
  864.6 26.2 %copy-start.131 = (f32[16,2048]{1,0:T(8,128)S(1)}, f32[16,2048]{1,0:T(8,128)}, u32[]{:S(2)}) copy-start(f32[16,2048]{1,0:T(8,128)} %fusion.95) | copy-start | bytes 393220
  864.6 26.2 %copy-start.132 = (f32[16,2048]{1,0:T(8,128)S(1)}, f32[16,2048]{1,0:T(8,128)}, u32[]{:S(2)}) copy-start(f32[16,2048]{1,0:T(8,128)} %fusion.254) | copy-start | bytes 393220
  864.6 166.2 %reduce-scatter.15.cloned.1.call-start = ((), (), s32[]{:S(2)}) async-start(), calls=%async_computation.15 | async-start | bytes 2621440 | tf_op jit(solution)/shard_map/reduce_scatter | solution.py:478
  894.0 182.2 %reduce-scatter.13.cloned.1.call-start = ((), (), s32[]{:S(2)}) async-start(), calls=%async_computation.14 | async-start | bytes 2621440 | tf_op jit(solution)/shard_map/reduce_scatter | solution.py:475
  908.2 235.6 %all-reduce.3.cloned.1.call-start = ((), (), s32[]{:S(2)}) async-start(), calls=%async_computation.22 | async-start | bytes 4718592 | tf_op jit(solution)/shard_map/psum | solution.py:495
  917.1 20.2 %copy-start.191 = (f32[384]{0:T(512)S(1)}, f32[384]{0:T(512)}, u32[]{:S(2)}) copy-start(f32[384]{0:T(512)} %copy-done.190) | copy-start | bytes 4612
  917.1 20.2 %copy-start.179 = (f32[384]{0:T(512)S(1)}, f32[384]{0:T(512)}, u32[]{:S(2)}) copy-start(f32[384]{0:T(512)} %copy-done.178) | copy-start | bytes 4612
  937.3 139.0 %copy-start.9 = (f32[384,2048]{1,0:T(8,128)S(1)}, f32[384,2048]{1,0:T(8,128)}, u32[]{:S(2)}) copy-start(f32[384,2048]{1,0:T(8,128)} %copy-done.8) | copy-start | bytes 9437188
  937.3 139.0 %copy-start.195 = (f32[384]{0:T(512)S(1)}, f32[384]{0:T(512)}, u32[]{:S(2)}) copy-start(f32[384]{0:T(512)} %copy-done.194) | copy-start | bytes 4612
  1143.8 7.6 copy-start.124
  1143.8 8.6 copy-start.123
  (177 other events, 676.3 us)
Sparse Core Ops, SparseCore 0:
  9.6 138.4 all-gather.6
  168.7 22.5 all-gather.10
  193.5 22.5 all-gather.8
  218.2 74.8 all-gather.12
  294.5 176.1 all-gather.14
  472.1 177.9 all-gather.16
  777.0 31.4 reduce-scatter.26
  817.4 31.2 reduce-scatter.24
  850.9 21.6 reduce-scatter.22
  875.4 19.8 reduce-scatter.16
  897.6 42.1 reduce-scatter.20
  942.0 43.1 reduce-scatter.18
  987.5 43.1 reduce-scatter.14
  1033.0 43.1 reduce-scatter.12
  1080.1 63.7 all-reduce.2
where the time goes:
time: 1170 us; the launch traced here: 1160 us
  waiting for transfers between devices  566 us (48%)
  matrix products  344 us (29%)
  local copies, waits for them, and re-layouts  162 us (14%)
  other arithmetic  68 us (6%)
  between operations  18.2 us (2%)
    all_gather x1, waiting for transfers between devices, up_rows_forward(): lax.all_gather(weight, ('grp', 'fs'), axis=0, tiled=True)  153 us
    all_gather x1, waiting for transfers between devices, down_rows_forward(): lax.all_gather(weight, ('grp', 'fs'), axis=0, tiled=True)  133 us
    unnamed x468, local copies, waits for them, and re-layouts  104 us
    dot_general x4, matrix products, fold_rows(): jnp.dot(columns, portion, preferred_element_type=jnp.float32)  92.3 us
    dot_general x4, matrix products, back_rows(): lax.dot_general(grad_low, portion, (((1,), (1,)), ((), ())), preferred_el...  88.9 us
    all_gather x1, waiting for transfers between devices, qkv_rows_forward(): lax.all_gather(weight, ('grp', 'fs'), axis=0, tiled=True)  78.6 us
    psum x1, waiting for transfers between devices, body(): lax.psum(shared[0].astype(jnp.bfloat16), ('rep', 'grp')).astype(jnp.float32)  61.8 us
    reduce_scatter x1, waiting for transfers between devices, body(): lax.psum_scatter(grad_b_attn.astype(jnp.bfloat16), 'fs', scatter_dimensio...  45.5 us
  transfers between devices with their start and end apart: 15, of which 8 were waited for; matrix products, arithmetic and copies ran while one was open for 35% of the time, Pallas kernels for 0%

commit v1 on v0

v1 whole, which is shorter than its diff:
```python
import functools
import math

import jax
import jax.numpy as jnp
from jax import lax
from jax.experimental import pallas as pl
from jax.experimental.pallas import tpu as pltpu
from jax.sharding import PartitionSpec as P

HEADS = 16
HDIM = 128
RANK = 16
NEG_FILL = -1e30
BF = jnp.bfloat16
F32 = jnp.float32
MESH = pl.DeviceIdType.MESH
BLOCK = 512


def mm(a, b):
    return jnp.dot(a, b, preferred_element_type=F32)


def mm_nt(a, b):
    return lax.dot_general(a, b, (((1,), (1,)), ((), ())), preferred_element_type=F32)


def mm_tn(a, b):
    return lax.dot_general(a, b, (((0,), (0,)), ((), ())), preferred_element_type=F32)


def norm_stats(values):
    center = values - jnp.mean(values, axis=-1, keepdims=True)
    spread = jnp.mean(center * center, axis=-1, keepdims=True)
    rstd = lax.rsqrt(spread + 1e-05)
    return center * rstd, rstd


def norm_back(hat, rstd, gain, grad):
    e = grad * gain
    return (
        e - jnp.mean(e, axis=-1, keepdims=True) - hat * jnp.mean(e * hat, axis=-1, keepdims=True)
    ) * rstd


def split_heads(block):
    return block.reshape(block.shape[0], -1, HDIM)


def masked_scores(query_part, key_part, allowed):
    scores = jnp.einsum(
        "qhd,khd->hqk",
        split_heads(query_part),
        split_heads(key_part),
        preferred_element_type=F32,
    ) * HDIM ** (-0.5)
    return jnp.where(allowed[None], scores, NEG_FILL)


def attend_forward(query_part, key_part, value_part, allowed):
    scores = masked_scores(query_part, key_part, allowed)
    row_peak = jnp.max(scores, axis=-1, keepdims=True)
    raised = jnp.exp(scores - row_peak)
    row_mass = jnp.sum(raised, axis=-1, keepdims=True)
    chances_low = (raised / row_mass).astype(BF)
    mixture = jnp.einsum(
        "hqk,khd->qhd", chances_low, split_heads(value_part), preferred_element_type=F32
    )
    return (mixture.reshape(mixture.shape[0], -1), (row_peak + jnp.log(row_mass))[:, :, 0])


def attend_backward(query_part, key_part, value_part, grad_part, logsum, allowed):
    scores = masked_scores(query_part, key_part, allowed)
    chances = jnp.exp(scores - logsum[:, :, None])
    heads_grad = split_heads(grad_part)
    grad_chances = jnp.einsum(
        "qhd,khd->hqk", heads_grad, split_heads(value_part), preferred_element_type=F32
    )
    inner_sum = jnp.sum(chances * grad_chances, axis=-1, keepdims=True)
    grad_scores = (chances * (grad_chances - inner_sum)).astype(BF)
    factor = HDIM ** (-0.5)
    grad_query = (
        jnp.einsum("hqk,khd->qhd", grad_scores, split_heads(key_part), preferred_element_type=F32)
        * factor
    )
    grad_key = (
        jnp.einsum("hqk,qhd->khd", grad_scores, split_heads(query_part), preferred_element_type=F32)
        * factor
    )
    grad_value = jnp.einsum(
        "hqk,qhd->khd", chances.astype(BF), heads_grad, preferred_element_type=F32
    )
    return (
        grad_query.reshape(grad_query.shape[0], -1),
        grad_key.reshape(grad_key.shape[0], -1),
        grad_value.reshape(grad_value.shape[0], -1),
    )


def pick_rows(table, ids):
    return jnp.concatenate(
        [lax.dynamic_index_in_dim(table, i, 0, keepdims=False) for i in ids], 0
    )


def spread_rows(grads, order, ids):
    owner = jnp.repeat(jnp.stack(ids), RANK)
    rank = jnp.arange(RANK * len(ids)) % RANK
    hot = (order[:, None] == (owner * RANK + rank)[None, :]).astype(BF)
    return mm(hot, grads.astype(BF)).astype(BF)


class Gather:
    def __init__(self, n_fs, count, src, dst, sems, lag=2, away=48):
        (self.zs, self.zr, self.ys, self.yr, self.xs, self.xr) = sems[:6]
        (self.cs, self.cr, self.ds, self.dr, self.loc) = sems[6:]
        self.nz, self.count, self.src, self.dst = n_fs, count, src, dst
        self.lag, self.slots, self.last = lag, 2 * lag, n_fs + 2
        self.rows = src.shape[1]
        rep, grp = lax.axis_index("rep"), lax.axis_index("grp")
        self.z = lax.axis_index("fs")
        self.y, self.c, plane = grp // 2, grp % 2, rep % 2
        self.far_rep = rep + 1 - 2 * plane
        self.far_core = self.y * 2 + 1 - self.c
        self.far_row = (1 - self.y) * 2 + self.c
        self.own = grp * n_fs + self.z
        self.away, self.stay = away, self.rows - away
        self.in_first = pl.multiple_of(away * plane, 8)
        self.out_first = pl.multiple_of(self.stay * plane, 8)
        self.far_first = pl.multiple_of(self.stay * (1 - plane), 8)

    @staticmethod
    def semaphores(n_fs, lag=2):
        slots, dma = 2 * lag, pltpu.SemaphoreType.DMA
        return (
            [dma((2 * slots, 2, n_fs)), dma((2 * slots, n_fs))]
            + [dma((slots, n_fs))] * 2
            + [dma((slots, 2 * n_fs))] * 6
            + [dma((slots,))]
        )

    def barrier(self):
        sem = pltpu.get_barrier_semaphore()

        def greet(**where):
            pl.semaphore_signal(sem, 1, device_id=where, device_id_type=MESH)

        greet(rep=self.far_rep)
        greet(grp=self.far_core)
        greet(grp=self.far_row)
        below, above = self.z > 0, self.z < self.nz - 1
        pl.when(below)(lambda: greet(fs=self.z - 1))
        pl.when(above)(lambda: greet(fs=self.z + 1))
        pl.semaphore_wait(sem, 3 + below.astype(jnp.int32) + above.astype(jnp.int32))

    def at_distance(self, d):
        if d < 0 or d >= self.nz:
            return []
        if d == 0:
            return [(None, self.z, 0)]
        return [(self.z >= d, self.z - d, 1), (self.z < self.nz - d, self.z + d, -1)]

    def shard(self, other, fs, core):
        row = 1 - self.y if other else self.y
        return (row * 2 + core) * self.nz + fs

    def send(self, j, shard, first, size, sems, own=False, **where):
        rows = pl.ds(first, size)
        return pltpu.make_async_remote_copy(
            self.src.at[j, rows] if own else self.dst.at[j, shard, rows],
            self.dst.at[j, shard, rows],
            *sems,
            device_id=where,
            device_id_type=MESH,
        )

    def keep(self, j, t):
        sem = self.loc.at[lax.rem(t, self.slots)]
        return pltpu.make_async_copy(self.src.at[j], self.dst.at[j, self.own], sem)

    def sends(self, a, j, t):
        todo, nz, k, kz = [], self.nz, lax.rem(t, self.slots), lax.rem(t, 2 * self.slots)
        inner, outer, far = (self.in_first, self.stay), (self.out_first, self.away), self.far_first

        def both(left, right):
            return right if left is None else jnp.logical_and(left, right)

        for ok, fs, way in self.at_distance(a):
            shard, own = self.shard(0, fs, self.c), a == 0
            if way >= 0:
                sems = (self.zs.at[kz, 0, fs], self.zr.at[kz, fs])
                up = self.send(j, shard, *inner, sems, own, fs=self.z + 1)
                todo.append((both(ok, self.z < nz - 1), up))
            if way <= 0:
                sems = (self.zs.at[kz, 1, fs], self.zr.at[kz, fs])
                down = self.send(j, shard, *inner, sems, own, fs=self.z - 1)
                todo.append((both(ok, self.z > 0), down))
            sems = (self.ys.at[k, fs], self.yr.at[k, fs])
            todo.append((ok, self.send(j, shard, *inner, sems, own, grp=self.far_row)))
            if not own:
                sems = (self.xs.at[k, fs], self.xr.at[k, fs])
                todo.append((ok, self.send(j, shard, *outer, sems, rep=self.far_rep)))
            sems = (self.cs.at[k, fs], self.cr.at[k, fs])
            size = (0, self.rows) if own else inner
            todo.append((ok, self.send(j, shard, *size, sems, own, grp=self.far_core)))
        for ok, fs, _ in self.at_distance(a - 1):
            shard = self.shard(1, fs, self.c)
            sems = (self.xs.at[k, nz + fs], self.xr.at[k, nz + fs])
            todo.append((ok, self.send(j, shard, *outer, sems, rep=self.far_rep)))
            sems = (self.cs.at[k, nz + fs], self.cr.at[k, nz + fs])
            todo.append((ok, self.send(j, shard, *inner, sems, grp=self.far_core)))
        for other in (0, 1):
            for ok, fs, way in self.at_distance(a - 1 - other):
                if way or other:
                    i = other * nz + fs
                    sems = (self.ds.at[k, i], self.dr.at[k, i])
                    shard = self.shard(other, fs, self.c)
                    core = self.send(j, shard, far, self.away, sems, grp=self.far_core)
                    todo.append((ok, core))
        return todo

    def arrivals(self, a, j, t):
        todo, nz, k, kz = [], self.nz, lax.rem(t, self.slots), lax.rem(t, 2 * self.slots)
        inner, far = (self.in_first, self.stay), (self.far_first, self.away)

        def expect(ok, shard, first, size, sem):
            ref = self.dst.at[j, shard, pl.ds(first, size)]
            todo.append((ok, pltpu.make_async_copy(ref, ref, sem)))

        for ok, fs, way in self.at_distance(a):
            if way:
                expect(ok, self.shard(0, fs, self.c), *inner, self.zr.at[kz, fs])
        for ok, fs, _ in self.at_distance(a - 1):
            expect(ok, self.shard(1, fs, self.c), *inner, self.yr.at[k, fs])
        for other in (0, 1):
            for ok, fs, way in self.at_distance(a - 1 - other):
                i = other * nz + fs
                if way or other:
                    expect(ok, self.shard(other, fs, self.c), *far, self.xr.at[k, i])
                size = inner if way or other else (0, self.rows)
                expect(ok, self.shard(other, fs, 1 - self.c), *size, self.cr.at[k, i])
            for ok, fs, way in self.at_distance(a - 2 - other):
                if way or other:
                    i = other * nz + fs
                    expect(ok, self.shard(other, fs, 1 - self.c), *far, self.dr.at[k, i])
        return todo

    def run(self, early=None, compute=None):
        lag = self.lag

        def act(ok, fn):
            if ok is None:
                fn()
            else:
                pl.when(ok)(fn)

        def finish(a, j, t):
            for ok, copy in self.sends(a - 1, j, t):
                act(ok, copy.wait_send)
            for ok, copy in self.arrivals(a, j, t):
                act(ok, copy.wait)
            if a == 1:
                self.keep(j, t).wait()

        def begin(a, j, t):
            for ok, copy in self.sends(a, j, t):
                act(ok, copy.start)
            if a == 0:
                self.keep(j, t).start()

        def tick(t, carry):
            for a in range(self.last, 0, -1):
                j = t - lag * a
                pl.when((j >= 0) & (j < self.count))(functools.partial(finish, a, j, t - lag))
            for a in range(self.last - 1, -1, -1):
                j = t - lag * a
                pl.when((j >= 0) & (j < self.count))(functools.partial(begin, a, j, t))
            if early is not None:
                early(t)
            if compute is not None:
                j = t - lag * self.last
                pl.when(j >= 0)(functools.partial(compute, j))
            return carry

        lax.fori_loop(0, self.count + lag * self.last + (compute is not None), tick, 0)


def gather_blocks(blocks, n_fs, n_shard, name):
    count, rows, width = blocks.shape

    def kernel(src, dst, *sems):
        engine = Gather(n_fs, count, src, dst, sems)
        engine.barrier()
        engine.run()

    return pl.pallas_call(
        kernel,
        out_shape=jax.ShapeDtypeStruct((count, n_shard, rows, width), BF),
        in_specs=[pl.BlockSpec(memory_space=pl.ANY)],
        out_specs=pl.BlockSpec(memory_space=pl.ANY),
        scratch_shapes=Gather.semaphores(n_fs),
        compiler_params=pltpu.CompilerParams(collective_id=0, has_side_effects=True),
        name=name,
    )(blocks)


def make_body(sizes):
    n_rep, n_grp, n_fs = sizes
    n_shard = n_grp * n_fs

    def reduce_tables(grads, ids, count):
        per, r_lo, width = count // n_fs, RANK // n_grp, grads.shape[1]
        order = jnp.arange(count * RANK).reshape(n_fs, per, n_grp, r_lo)
        v = spread_rows(grads, order.transpose(2, 0, 1, 3).reshape(-1), ids)
        v = lax.psum_scatter(v, ("grp", "fs"), scatter_dimension=0, tiled=True)
        v = lax.psum(v, "rep")
        v = lax.all_gather(v, "grp", axis=0, tiled=True)
        v = v.reshape(n_grp, per, r_lo, width).transpose(1, 0, 2, 3)
        return v.reshape(per, RANK, width).astype(F32)

    def body(
        prompt_input_rows,
        continuation_input,
        prompt_group_adapter,
        continuation_adapter,
        first_norm_scale,
        first_norm_bias,
        second_norm_scale,
        second_norm_bias,
        frozen_query_key_value,
        frozen_output_weight,
        frozen_up_weight,
        frozen_down_weight,
        adapter_attention_input,
        adapter_attention_output,
        adapter_up_input,
        adapter_up_output,
        adapter_down_input,
        adapter_down_output,
        prompt_cotangent,
        continuation_cotangent,
    ):
        prompt_len, width = prompt_input_rows.shape[2:]
        cont_len = continuation_input.shape[3]
        rows = prompt_len + cont_len
        count = adapter_up_input.shape[0]
        hidden = frozen_up_weight.shape[1]

        inputs = jnp.concatenate(
            [
                prompt_input_rows.reshape(prompt_len, width),
                continuation_input.reshape(cont_len, width),
            ],
            0,
        ).astype(F32)
        cot_low = jnp.concatenate(
            [
                prompt_cotangent.reshape(prompt_len, width),
                continuation_cotangent.reshape(cont_len, width),
            ],
            0,
        )
        ids = [prompt_group_adapter.reshape(()), continuation_adapter.reshape(())]
        a_attn = adapter_attention_input.swapaxes(2, 3)
        b_attn = adapter_attention_output
        a_up, b_up = adapter_up_input.swapaxes(1, 2), adapter_up_output
        a_dn, b_dn = adapter_down_input.swapaxes(1, 2), adapter_down_output

        mask2 = (jnp.arange(rows) >= prompt_len)[:, None] == (jnp.arange(2 * RANK) >= RANK)[None, :]

        def low_of(product):
            return jnp.where(mask2, product, 0.0).astype(BF)

        shard_rows = frozen_query_key_value.shape[0]
        parts = hidden // n_shard // shard_rows
        wide = shard_rows * (BLOCK // shard_rows)

        def columns(w):
            return w.reshape(shard_rows, -1, BLOCK).swapaxes(0, 1)

        up_blocks = frozen_up_weight.reshape(
            shard_rows, n_shard * shard_rows // BLOCK, BLOCK // shard_rows, parts, shard_rows
        )
        up_blocks = up_blocks.transpose(3, 1, 0, 2, 4).reshape(-1, shard_rows, BLOCK)
        dn_blocks = frozen_down_weight.reshape(parts, shard_rows, -1, BLOCK).swapaxes(1, 2)
        dn_blocks = dn_blocks.reshape(-1, shard_rows, BLOCK)
        all_blocks = jnp.concatenate(
            [columns(frozen_query_key_value), columns(frozen_output_weight), dn_blocks, up_blocks], 0
        )
        got = gather_blocks(all_blocks, n_fs, n_shard, "gather_all")
        got = got.reshape(-1, n_shard * shard_rows, BLOCK)
        n_qkv, n_out = 3 * width // BLOCK, width // BLOCK
        w_qkv, w_out = got[:n_qkv], got[n_qkv : n_qkv + n_out]
        n_dn = dn_blocks.shape[0]
        w_dn = got[n_qkv + n_out : n_qkv + n_out + n_dn]
        w_up = got[n_qkv + n_out + n_dn :]

        def times(u, w):
            return jnp.einsum("rk,bkc->rbc", u, w, preferred_element_type=F32).reshape(u.shape[0], -1)

        def times_t(g, w):
            g = g.reshape(g.shape[0], w.shape[0], BLOCK)
            return jnp.einsum("rbc,bkc->rk", g, w, preferred_element_type=F32)

        def hidden_order(v):
            v = v.reshape(-1, n_shard, parts, shard_rows)
            return v.transpose(0, 2, 1, 3).reshape(-1, hidden)

        def hidden_back(v):
            v = v.reshape(-1, parts, n_shard, shard_rows)
            return v.transpose(0, 2, 1, 3).reshape(-1, hidden)

        hat_one, rstd_one = norm_stats(inputs)
        normed_one = (hat_one * first_norm_scale + first_norm_bias).astype(BF)
        a_sel = [pick_rows(a_attn[:, n], ids) for n in range(4)]
        b_sel = [pick_rows(b_attn[:, n], ids) for n in range(4)]
        lows = [low_of(mm_nt(normed_one, a_sel[n])) for n in range(3)]
        merged = times(normed_one, w_qkv)
        queries, keys_local, values_local = [
            (merged[:, n * width : (n + 1) * width] + mm(lows[n], b_sel[n])).astype(BF)
            for n in range(3)
        ]
        prompt_keys = lax.all_gather(keys_local[:prompt_len], "grp", axis=0, tiled=True)
        prompt_values = lax.all_gather(values_local[:prompt_len], "grp", axis=0, tiled=True)
        prompt_total = prompt_keys.shape[0]
        all_keys = jnp.concatenate([prompt_keys, keys_local[prompt_len:]], 0)
        all_values = jnp.concatenate([prompt_values, values_local[prompt_len:]], 0)
        query_row = jnp.arange(rows)[:, None]
        key_col = jnp.arange(all_keys.shape[0])[None, :]
        prompt_sees = key_col <= lax.axis_index("grp") * prompt_len + query_row
        cont_sees = key_col - prompt_total <= query_row - prompt_len
        allowed = jnp.where(
            query_row < prompt_len, prompt_sees & (key_col < prompt_total), cont_sees
        )
        block_width = 512
        mixtures, logsums = [], []
        for first in range(0, width, block_width):
            cut = slice(first, first + block_width)
            mixture, logsum = attend_forward(
                queries[:, cut], all_keys[:, cut], all_values[:, cut], allowed
            )
            mixtures.append(mixture)
            logsums.append(logsum)
        mixed = jnp.concatenate(mixtures, 1).astype(BF)

        lows.append(low_of(mm_nt(mixed, a_sel[3])))
        resid = inputs + (times(mixed, w_out) + mm(lows[3], b_sel[3]))
        hat_two, rstd_two = norm_stats(resid)
        normed_two = (hat_two * second_norm_scale + second_norm_bias).astype(BF)

        a_up2, b_up2 = pick_rows(a_up, ids), hidden_order(pick_rows(b_up, ids))
        a_dn2, b_dn2 = hidden_order(pick_rows(a_dn, ids)), pick_rows(b_dn, ids)
        low_up = low_of(mm_nt(normed_two, a_up2))
        dlow_dn = low_of(mm_nt(cot_low, b_dn2))
        size = n_shard * shard_rows
        out_part = back_part = low_dn = dlow_up = 0.0
        g_b_up, g_a_dn = [], []
        for n in range(parts):
            cut = slice(n * size, (n + 1) * size)
            per = width // BLOCK
            w_up_n, w_dn_n = w_up[n * size // BLOCK : (n + 1) * size // BLOCK], w_dn[n * per : (n + 1) * per]
            pre = times(normed_two, w_up_n) + mm(low_up, b_up2[:, cut])
            cdf = 0.5 * (1.0 + lax.erf(pre * math.sqrt(0.5)))
            act = (pre * cdf).astype(BF)
            slope = cdf + pre * jnp.exp(-0.5 * pre * pre) * (1.0 / math.sqrt(2.0 * math.pi))
            grad_act = times_t(cot_low, w_dn_n) + mm(dlow_dn, a_dn2[:, cut])
            grad_pre = (grad_act * slope).astype(BF)
            out_part = out_part + times(act, w_dn_n)
            back_part = back_part + times_t(grad_pre, w_up_n)
            low_dn = low_dn + mm_nt(act, a_dn2[:, cut])
            dlow_up = dlow_up + mm_nt(grad_pre, b_up2[:, cut])
            g_b_up.append(mm_tn(low_up, grad_pre))
            g_a_dn.append(mm_tn(dlow_dn, act))
        g_b_up = hidden_back(jnp.concatenate(g_b_up, 1))
        g_a_dn = hidden_back(jnp.concatenate(g_a_dn, 1))
        low_dn, dlow_up = low_of(low_dn), low_of(dlow_up)
        result = resid + (out_part + mm(low_dn, b_dn2))
        grad_two = back_part + mm(dlow_up, a_up2)
        g_a_up = mm_tn(dlow_up, normed_two)
        g_b_dn = mm_tn(low_dn, cot_low)

        cot = cot_low.astype(F32)
        grad_resid = cot + norm_back(hat_two, rstd_two, second_norm_scale, grad_two)
        grad_attn = grad_resid.astype(BF)
        dlows = [None] * 4
        dlows[3] = low_of(mm_nt(grad_attn, b_sel[3]))
        grad_mixed = (times_t(grad_attn, w_out) + mm(dlows[3], a_sel[3])).astype(BF)

        g_q, g_k, g_v = [], [], []
        for n, first in enumerate(range(0, width, block_width)):
            cut = slice(first, first + block_width)
            a, b, c = attend_backward(
                queries[:, cut],
                all_keys[:, cut],
                all_values[:, cut],
                grad_mixed[:, cut],
                logsums[n],
                allowed,
            )
            g_q.append(a)
            g_k.append(b)
            g_v.append(c)
        grad_all_keys = jnp.concatenate(g_k, 1)
        grad_all_values = jnp.concatenate(g_v, 1)

        def share(v):
            mine = lax.psum_scatter(
                v[:prompt_total].astype(BF), "grp", scatter_dimension=0, tiled=True
            )
            return jnp.concatenate([mine, v[prompt_total:].astype(BF)], 0)

        grads = [
            jnp.concatenate(g_q, 1).astype(BF),
            share(grad_all_keys),
            share(grad_all_values),
        ]
        grad_one = times_t(jnp.concatenate(grads, 1), w_qkv)
        for n in range(3):
            dlows[n] = low_of(mm_nt(grads[n], b_sel[n]))
            grad_one = grad_one + mm(dlows[n], a_sel[n])
        grad_inputs = grad_resid + norm_back(hat_one, rstd_one, first_norm_scale, grad_one)

        g_a = [mm_tn(dlows[n], normed_one) for n in range(3)] + [mm_tn(dlows[3], mixed)]
        g_b = [mm_tn(lows[n], grads[n]) for n in range(3)] + [mm_tn(lows[3], grad_attn)]

        slim = reduce_tables(jnp.concatenate([g_b_up, g_a_dn] + g_a + g_b + [g_a_up, g_b_dn], 1), ids, count)
        both = [slim[:, :, :hidden], slim[:, :, hidden : 2 * hidden]]
        slim = slim[:, :, 2 * hidden :].reshape(slim.shape[0], RANK, 10, width).transpose(0, 2, 1, 3)

        return (
            result[:prompt_len].reshape(prompt_input_rows.shape).astype(BF),
            result[prompt_len:].reshape(continuation_input.shape).astype(BF),
            grad_inputs[:prompt_len].reshape(prompt_input_rows.shape).astype(BF),
            grad_inputs[prompt_len:].reshape(continuation_input.shape).astype(BF),
            slim[:, :4].swapaxes(2, 3),
            slim[:, 4:8],
            slim[:, 8].swapaxes(1, 2),
            both[0],
            both[1].swapaxes(1, 2),
            slim[:, 9],
        )

    return body


def solution(mesh):
    sizes = (mesh.shape["rep"], mesh.shape["grp"], mesh.shape["fs"])
    rows_in = P("rep", "fs", "grp", None)
    conts_in = P("rep", "fs", "grp", None, None)
    weight = P(("grp", "fs"), None)
    return jax.shard_map(
        make_body(sizes),
        mesh=mesh,
        in_specs=(
            rows_in,
            conts_in,
            P("rep", "fs"),
            P("rep", "fs", "grp"),
            P(),
            P(),
            P(),
            P(),
            weight,
            weight,
            weight,
            weight,
            P(),
            P(),
            P(),
            P(),
            P(),
            P(),
            rows_in,
            conts_in,
        ),
        out_specs=(
            rows_in,
            conts_in,
            rows_in,
            conts_in,
            P("fs", None, None, None),
            P("fs", None, None, None),
            P("fs", None, None),
            P("fs", None, None),
            P("fs", None, None),
            P("fs", None, None),
        ),
        check_vma=False,
    )
```

time: 1170 us -> 1180 us (level)
  waiting for transfers between devices: 566 us -> 65.6 us
  Pallas kernels: 0 us -> 373 us
  local copies, waits for them, and re-layouts: 162 us -> 378 us
  matrix products: 344 us -> 281 us
  other arithmetic: 68 us -> 47.7 us
    pallas_call x0 -> x1, Pallas kernels: none -> 373 us  [gather_blocks(): pl.pallas_call(kernel, out_shape=jax.ShapeDtypeStruct((count, n_shard, ro...]
    all_gather x4 -> x1, waiting for transfers between devices: 365 us -> 0.01 us  [reduce_tables(): v = lax.all_gather(v, 'grp', axis=0, tiled=True)]
    dot_general x0 -> x10, local copies, waits for them, and re-layouts: none -> 138 us  [times(): jnp.einsum('rk,bkc->rbc', u, w, preferred_element_type=F32)]
    reduce_scatter x6 -> x1, waiting for transfers between devices: 137 us -> 24.2 us  [reduce_tables(): v = lax.psum_scatter(v, ('grp', 'fs'), scatter_dimension=0, tiled=True)]
    slice x14 -> x12, local copies, waits for them, and re-layouts: 11 us -> 84.6 us  [the longest x1 49.3 us: body(): w_dn[n * per:(n + 1) * per]]
    dot_general x96 -> x79, matrix products: 300 us -> 238 us  [the longest x10 81 us: times_t(): return jnp.einsum('rbc,bkc->rk', g, w, preferred_element_type=F32)]
    unnamed x468 -> x521, local copies, waits for them, and re-layouts: 104 us -> 58.8 us
    psum x1, waiting for transfers between devices: 61.8 us -> 23.7 us  [reduce_tables(): v = lax.psum(v, 'rep')]
  transfers between devices with their start and end apart: 15 -> 7, of which waited for: 8 -> 3; matrix products, arithmetic and copies ran while one was open for 35% -> 32% of each run, Pallas kernels for 0% -> 0%
where the time goes in v1:
time: 1180 us; the launch traced here: 1170 us
  local copies, waits for them, and re-layouts  378 us (32%)
  Pallas kernels  373 us (32%)
  matrix products  281 us (24%)
  waiting for transfers between devices  65.6 us (6%)
  other arithmetic  47.7 us (4%)
  between operations  19 us (2%)
    pallas_call x1, Pallas kernels, gather_blocks(): pl.pallas_call(kernel, out_shape=jax.ShapeDtypeStruct((count, n_shard, ro...  373 us
    dot_general x10, local copies, waits for them, and re-layouts, times(): jnp.einsum('rk,bkc->rbc', u, w, preferred_element_type=F32)  138 us
    dot_general x10, matrix products, times_t(): return jnp.einsum('rbc,bkc->rk', g, w, preferred_element_type=F32)  81 us
    dot_general x10, matrix products, times(): jnp.einsum('rk,bkc->rbc', u, w, preferred_element_type=F32)  62.5 us
    unnamed x521, local copies, waits for them, and re-layouts  58.8 us
    slice x1, local copies, waits for them, and re-layouts, body(): w_dn[n * per:(n + 1) * per]  49.3 us
    dot_general x19, matrix products, mm(): return jnp.dot(a, b, preferred_element_type=F32)  44.6 us
    reduce_scatter x1, waiting for transfers between devices, reduce_tables(): v = lax.psum_scatter(v, ('grp', 'fs'), scatter_dimension=0, tiled=True)  24.2 us
  transfers between devices with their start and end apart: 7, of which 3 were waited for; matrix products, arithmetic and copies ran while one was open for 32% of the time, Pallas kernels for 0%

profile of v1, /device:TPU:0, one launch (start us, length us, event | category | flops | bytes accessed | tf_op | source)
XLA Modules:
  0.0 1165.1 jit_solution(14794737004695382919)
XLA Ops:
  16.2 4.4 reshape.612
  25.5 3.3 reshape.610
  34.0 3.3 pad_maximum_fusion.src
  37.3 373.4 %gather_all.1 = bf16[48,16,128,512]{3,2,1,0:T(8,128)(2,1)} custom-call(bf16[48,128,512]{2,1,0:T(8,128)(2,1)} %pad_maximum_fusion.src), custom_call_target="tpu_custom_call" | custom-call | tf_op jit(solution)/shard_map/gather_all/pallas_call | solution.py:297
  410.7 20.6 %slice.262 = bf16[12,16,128,512]{3,2,1,0:T(8,128)(2,1)} slice(bf16[48,16,128,512]{3,2,1,0:T(8,128)(2,1)} %gather_all.1), slice={[0:12], [0:16], [0:128], [0:512]} | slice | bytes 50331648 | tf_op jit(solution)/shard_map/slice | solution.py:394
  431.4 33.5 %copy.223 = bf16[12,512,2048]{2,1,0:T(8,128)(2,1)} copy(bf16[12,512,2048]{1,2,0:T(8,128)(2,1)} %bitcast.467) | data formatting | bytes 50331648 | tf_op jit(solution)/shard_map/rk,bkc->rbc/dot_general | solution.py:400
  467.8 17.5 %fusion.215 = f32[384,6144]{1,0:T(8,128)} fusion(bf16[384,2048]{1,0:T(8,128)(2,1)S(1)} %fusion.14, bf16[6144,2048]{1,0:T(8,128)(2,1)} %bitcast.501), kind=kOutput, calls=%fused_computation.423 | convolution fusion | flops 9663676416 | bytes 36175872 | tf_op jit(solution)/shard_map/rk,bkc->rbc/dot_general | solution.py:400
  498.7 49.3 %fusion.203 = (bf16[4,16,128,512]{3,2,1,0:T(8,128)(2,1)}, bf16[4,16,128,512]{3,2,1,0:T(8,128)(2,1)}, bf16[4,16,128,512]{3,2,1,0:T(8,128)(2,1)}, bf16[4,16,128,51...) fusion(bf16[48,16,128,512]{3,2,1,0:T(8,128)(2,1)} %gather_all.1), kind=kLoop, calls=%fused_computation.411 | loop fusion | bytes 150994944 | tf_op jit(solution)/shard_map/slice | solution.py:462
  573.4 9.0 fusion.198
  582.5 8.5 fusion.196
  602.1 11.5 copy.236
  613.6 11.4 copy.237
  625.0 11.4 copy.240
  636.4 11.4 copy.242
  647.8 11.9 %copy.244 = bf16[4,512,2048]{2,1,0:T(8,128)(2,1)} copy(bf16[4,512,2048]{1,2,0:T(8,128)(2,1)} %bitcast.497) | data formatting | bytes 16777216 | tf_op jit(solution)/shard_map/rk,bkc->rbc/dot_general | solution.py:400
  664.1 8.5 fusion.195
  672.5 8.5 fusion.197
  681.1 3.0 fusion.120
  694.4 2.7 fusion.125
  715.2 3.5 fusion.199
  723.0 3.4 fusion.216
  729.5 3.1 fusion.26
  734.2 8.7 fusion.222
  742.9 5.1 fusion.220
  748.1 3.4 fusion.218
  769.2 5.1 fusion.83
  774.3 8.7 fusion.86
  783.1 5.2 fusion.89
  788.3 6.7 fusion.92
  795.0 3.7 fusion.201
  798.8 3.4 fusion.202
  802.8 3.4 fusion.80
  809.2 4.3 fusion.60
  813.5 6.5 multiply_reduce_fusion.3
  821.3 4.3 fusion.54
  825.6 6.7 multiply_reduce_fusion
  838.7 3.4 fusion.58
  842.1 3.7 fusion.56
  848.2 4.0 copy.290
  852.3 5.0 multiply_convert_fusion.3
  872.2 4.5 multiply_reduce_fusion.1
  876.7 3.0 multiply_convert_fusion.1
  888.7 3.9 copy.288
  915.0 17.6 %reduce-scatter.10.cloned.1.call-done = bf16[128,2048]{1,0:T(8,128)(2,1)} async-done(((bf16[512,2048]{1,0:T(8,128)(2,1)}), bf16[128,2048]{1,0:T(8,128)(2,1)}) %reduce-scatter.10.cloned.1.call-update) | async-done | bytes 524304
  948.5 6.8 convolution_convert_fusion
  955.6 11.7 %copy.239 = bf16[4,512,2048]{2,1,0:T(8,128)(2,1)} copy(bf16[4,512,2048]{1,2,0:T(8,128)(2,1)} %bitcast.482) | data formatting | bytes 16777216 | tf_op jit(solution)/shard_map/rk,bkc->rbc/dot_general | solution.py:400
  967.3 12.0 %copy.243 = bf16[4,512,2048]{2,1,0:T(8,128)(2,1)} copy(bf16[4,512,2048]{1,2,0:T(8,128)(2,1)} %bitcast.480) | data formatting | bytes 16777216 | tf_op jit(solution)/shard_map/rk,bkc->rbc/dot_general | solution.py:400
  979.3 11.7 %copy.245 = bf16[4,512,2048]{2,1,0:T(8,128)(2,1)} copy(bf16[4,512,2048]{1,2,0:T(8,128)(2,1)} %bitcast.478) | data formatting | bytes 16777216 | tf_op jit(solution)/shard_map/rk,bkc->rbc/dot_general | solution.py:400
  990.9 11.5 copy.241
  1016.8 6.1 fusion.223
  1023.0 3.4 fusion.221
  1026.5 6.2 fusion.219
  1032.7 5.1 fusion.217
  1037.8 2.9 add_convert_fusion
  1042.6 24.2 %reduce-scatter.8.cloned.1.call-done = bf16[8,36864]{1,0:T(8,128)(2,1)} async-done(((bf16[128,36864]{1,0:T(8,128)(2,1)}), bf16[8,36864]{1,0:T(8,128)(2,1)}) %reduce-scatter.8.cloned.1.call-update) | async-done | bytes 589840 | tf_op jit(solution)/shard_map/reduce_scatter | solution.py:316
  1075.2 23.7 %all-reduce.2.cloned.1.call-done = bf16[8,36864]{1,0:T(8,128)(2,1)} async-done(((bf16[8,36864]{1,0:T(8,128)(2,1)}), bf16[8,36864]{1,0:T(8,128)(2,1)}) %all-reduce.2.cloned.1.call-update) | async-done | bytes 589840 | tf_op jit(solution)/shard_map/psum | solution.py:317
  1099.0 17.4 %fusion.224 = f32[384,2048,1]{1,0,2:T(8,128)} fusion(bf16[384,12,512]{2,0,1:T(8,128)(2,1)} %constant_dynamic-update-slice_fusion, bf16[12,2048,512]{2,1,0:T(8,128)(2,1)} %bitcast.468), kind=kOutput, calls=%fused_computation.432 | convolution fusion | flops 9663676416 | bytes 33030144 | tf_op jit(solution)/shard_map/rbc,bkc->rk/dot_general | solution.py:404
  1117.7 3.5 fusion.200
  1125.0 5.1 reshape.673
  1130.0 4.9 copy.285
  1134.9 5.8 reshape.672
  1140.7 3.0 slice_bitcast_fusion
  1147.7 2.7 fusion.204
  1150.4 2.7 fusion.205
  (727 shorter events, 242.3 us)
Async XLA Ops:
  7.2 673.9 %all-gather.6.cloned.1.call-start = ((), (), s32[]{:S(2)}) async-start(), calls=%async_computation.4 | async-start | bytes 2621440 | tf_op jit(solution)/shard_map/all_gather | solution.py:424
  7.2 484.8 %copy-start.194 = (pred[32]{0:T(512)(128)(4,1)}, pred[32]{0:T(512)(128)(4,1)S(1)}, u32[]{:S(2)}) copy-start(pred[32]{0:T(512)(128)(4,1)S(1)} %iota_compare_fusion.4) | copy-start | bytes 100
  7.3 484.8 %copy-start.198 = (pred[384]{0:T(512)(128)(4,1)}, pred[384]{0:T(512)(128)(4,1)S(1)}, u32[]{:S(2)}) copy-start(pred[384]{0:T(512)(128)(4,1)S(1)} %iota_compare_fusion.3) | copy-start | bytes 1156
  10.3 456.8 %copy-start.187 = (f32[384]{0:T(512)}, f32[384]{0:T(512)S(1)}, u32[]{:S(2)}) copy-start(f32[384]{0:T(512)S(1)} %broadcast_multiply_fusion.5) | copy-start | bytes 4612
  12.2 454.9 %copy-start.192 = (f32[384]{0:T(512)}, f32[384]{0:T(512)S(1)}, u32[]{:S(2)}) copy-start(f32[384]{0:T(512)S(1)} %add_rsqrt_fusion.1) | copy-start | bytes 4612
  431.3 35.8 %copy-start.8 = (bf16[1,1,1,256,2048]{4,3,2,1,0:T(8,128)(2,1)S(1)}, bf16[1,1,1,256,2048]{4,3,2,1,0:T(8,128)(2,1)}, u32[]{:S(2)}) copy-start(bf16[1,1,1,256,2048]{4,3,2,1,0:T(8,128)(2,1)} %param.21) | copy-start | bytes 3145732
  431.3 35.8 %copy-start.19 = (bf16[1,1,128,2048]{3,2,1,0:T(8,128)(2,1)S(1)}, bf16[1,1,128,2048]{3,2,1,0:T(8,128)(2,1)}, u32[]{:S(2)}) copy-start(bf16[1,1,128,2048]{3,2,1,0:T(8,128)(2,1)} %param.20) | copy-start | bytes 1572868
  431.4 35.8 %copy-start.190 = (f32[2048]{0:T(1024)S(1)}, f32[2048]{0:T(1024)}, u32[]{:S(2)}) copy-start(f32[2048]{0:T(1024)} %param.24) | copy-start | bytes 24580
  431.4 35.8 %copy-start.204 = (f32[2048]{0:T(1024)S(1)}, f32[2048]{0:T(1024)}, u32[]{:S(2)}) copy-start(f32[2048]{0:T(1024)} %param.25) | copy-start | bytes 24580
  466.4 18.9 %copy-start.127 = (bf16[16,2048]{1,0:T(8,128)(2,1)}, bf16[16,2048]{1,0:T(8,128)(2,1)S(1)}, u32[]{:S(2)}) copy-start(bf16[16,2048]{1,0:T(8,128)(2,1)S(1)} %get-tuple-element.147) | copy-start | bytes 196612
  466.4 18.9 %copy-start.129 = (bf16[16,2048]{1,0:T(8,128)(2,1)}, bf16[16,2048]{1,0:T(8,128)(2,1)S(1)}, u32[]{:S(2)}) copy-start(bf16[16,2048]{1,0:T(8,128)(2,1)S(1)} %get-tuple-element.148) | copy-start | bytes 196612
  467.1 18.8 %copy-start.152 = (bf16[16,2048]{1,0:T(8,128)(2,1)}, bf16[16,2048]{1,0:T(8,128)(2,1)S(1)}, u32[]{:S(2)}) copy-start(bf16[16,2048]{1,0:T(8,128)(2,1)S(1)} %get-tuple-element.151) | copy-start | bytes 196612
  467.2 18.8 %copy-start.153 = (bf16[16,2048]{1,0:T(8,128)(2,1)}, bf16[16,2048]{1,0:T(8,128)(2,1)S(1)}, u32[]{:S(2)}) copy-start(bf16[16,2048]{1,0:T(8,128)(2,1)S(1)} %get-tuple-element.152) | copy-start | bytes 196612
  467.8 123.2 %copy-start.5 = (bf16[384,2048]{1,0:T(8,128)(2,1)}, bf16[384,2048]{1,0:T(8,128)(2,1)S(1)}, u32[]{:S(2)}) copy-start(bf16[384,2048]{1,0:T(8,128)(2,1)S(1)} %fusion.14) | copy-start | bytes 4718596
  488.4 109.6 %copy-start.60 = (bf16[384,2048]{1,0:T(8,128)(2,1)}, bf16[384,2048]{1,0:T(8,128)(2,1)S(1)}, u32[]{:S(2)}) copy-start(bf16[384,2048]{1,0:T(8,128)(2,1)S(1)} %fusion.45) | copy-start | bytes 4718596
  489.3 205.0 %all-gather.4.cloned.1.call-start = ((), (), s32[]{:S(2)}) async-start(), calls=%async_computation.3 | async-start | bytes 2621440 | tf_op jit(solution)/shard_map/all_gather | solution.py:425
  490.4 100.7 %copy-start.131 = (bf16[16,2048]{1,0:T(8,128)(2,1)}, bf16[16,2048]{1,0:T(8,128)(2,1)S(1)}, u32[]{:S(2)}) copy-start(bf16[16,2048]{1,0:T(8,128)(2,1)S(1)} %get-tuple-element.117) | copy-start | bytes 196612
  490.4 100.7 %copy-start.133 = (bf16[16,2048]{1,0:T(8,128)(2,1)}, bf16[16,2048]{1,0:T(8,128)(2,1)S(1)}, u32[]{:S(2)}) copy-start(bf16[16,2048]{1,0:T(8,128)(2,1)S(1)} %get-tuple-element.118) | copy-start | bytes 196612
  497.2 413.4 %reduce-scatter.12.cloned.1.call-start = ((), (), s32[]{:S(2)}) async-start(), calls=%async_computation.9 | async-start | bytes 2621440
  573.4 9.0 copy-start.113
  573.4 9.0 copy-start.136
  582.5 8.6 copy-start.195
  582.5 8.6 copy-start.199
  582.5 9.8 copy-start.156
  582.5 9.8 copy-start.158
  647.8 12.0 %copy-start.111 = (bf16[384,512]{1,0:T(8,128)(2,1)S(1)}, bf16[384,512]{1,0:T(8,128)(2,1)}, u32[]{:S(2)}) copy-start(bf16[384,512]{1,0:T(8,128)(2,1)} %get-tuple-element.95) | copy-start | bytes 1179652
  647.8 13.0 %copy-start.110 = (bf16[384,512]{1,0:T(8,128)(2,1)S(1)}, bf16[384,512]{1,0:T(8,128)(2,1)}, u32[]{:S(2)}) copy-start(bf16[384,512]{1,0:T(8,128)(2,1)} %get-tuple-element.96) | copy-start | bytes 1179652
  647.8 13.9 %copy-start.109 = (bf16[384,512]{1,0:T(8,128)(2,1)S(1)}, bf16[384,512]{1,0:T(8,128)(2,1)}, u32[]{:S(2)}) copy-start(bf16[384,512]{1,0:T(8,128)(2,1)} %get-tuple-element.97) | copy-start | bytes 1179652
  672.5 8.6 slice-start.27
  685.4 23.3 %copy-start.43 = (bf16[768,512]{0,1:T(8,128)(2,1)}, bf16[768,512]{0,1:T(8,128)(2,1)S(1)}, u32[]{:S(2)}) copy-start(bf16[768,512]{0,1:T(8,128)(2,1)S(1)} %copy.295) | copy-start | bytes 2359300
  686.0 18.4 %copy-start.44 = (bf16[768,512]{0,1:T(8,128)(2,1)}, bf16[768,512]{0,1:T(8,128)(2,1)S(1)}, u32[]{:S(2)}) copy-start(bf16[768,512]{0,1:T(8,128)(2,1)S(1)} %copy.301) | copy-start | bytes 2359300
  687.7 11.7 %copy-start.46 = (bf16[768,512]{0,1:T(8,128)(2,1)}, bf16[768,512]{0,1:T(8,128)(2,1)S(1)}, u32[]{:S(2)}) copy-start(bf16[768,512]{0,1:T(8,128)(2,1)S(1)} %copy.299) | copy-start | bytes 2359300
  697.1 9.9 copy-start.82
  697.1 14.3 %copy-start.84 = (bf16[96,4,8,128]{3,2,1,0:T(8,128)(2,1)}, bf16[96,4,8,128]{3,2,1,0:T(8,128)(2,1)S(1)}, u32[]{:S(2)}) copy-start(bf16[96,4,8,128]{3,2,1,0:T(8,128)(2,1)S(1)} %get-tuple-element.71) | copy-start | bytes 2359300
  699.4 19.4 %copy-start.211 = (bf16[4,128,384]{2,1,0:T(8,128)(2,1)}, bf16[4,128,384]{2,1,0:T(8,128)(2,1)S(1)}, u32[]{:S(2)}) copy-start(bf16[4,128,384]{2,1,0:T(8,128)(2,1)S(1)} %fusion.101) | copy-start | bytes 1179652
  704.4 14.5 %copy-start.213 = (bf16[4,128,384]{2,1,0:T(8,128)(2,1)}, bf16[4,128,384]{2,1,0:T(8,128)(2,1)S(1)}, u32[]{:S(2)}) copy-start(bf16[4,128,384]{2,1,0:T(8,128)(2,1)S(1)} %fusion.100) | copy-start | bytes 1179652
  707.0 118.6 %copy-start.168 = (f32[4,384]{1,0:T(4,128)}, f32[4,384]{1,0:T(4,128)S(1)}, u32[]{:S(2)}) copy-start(f32[4,384]{1,0:T(4,128)S(1)} %log_add_fusion) | copy-start | bytes 18436
  708.7 10.1 copy-start.215
  711.3 102.2 %copy-start.170 = (f32[4,384]{1,0:T(4,128)}, f32[4,384]{1,0:T(4,128)S(1)}, u32[]{:S(2)}) copy-start(f32[4,384]{1,0:T(4,128)S(1)} %log_add_fusion.3) | copy-start | bytes 18436
  722.9 25.2 %copy-start.31 = (bf16[384,2048]{1,0:T(8,128)(2,1)}, bf16[384,2048]{1,0:T(8,128)(2,1)S(1)}, u32[]{:S(2)}) copy-start(bf16[384,2048]{1,0:T(8,128)(2,1)S(1)} %add_convert_fusion.1) | copy-start | bytes 4718596
  732.6 10.3 slice-start.17
  734.2 8.7 slice-start.18
  734.2 13.8 %slice-start.15 = ((s8[8388608]{0:T(1024)(128)(4,1)}), s8[4194304]{0:T(1024)(128)(4,1)S(1)}, s32[]{:S(2)}) async-start(s8[8388608]{0:T(1024)(128)(4,1)} %bitcast.514), calls=%async_computation.25 | async-start | bytes 8388608
  769.2 25.8 %copy-start.162 = (bf16[384,32]{0,1:T(8,128)(2,1)}, bf16[384,32]{0,1:T(8,128)(2,1)S(1)}, u32[]{:S(2)}) copy-start(bf16[384,32]{0,1:T(8,128)(2,1)S(1)} %fusion.113) | copy-start | bytes 73732
  769.2 13.8 %slice-start.8 = ((s8[8388608]{0:T(1024)(128)(4,1)}), s8[4194304]{0:T(1024)(128)(4,1)S(1)}, s32[]{:S(2)}) async-start(s8[8388608]{0:T(1024)(128)(4,1)} %bitcast.492), calls=%async_computation.18 | async-start | bytes 8388608
  774.3 8.7 slice-start.9
  774.3 8.7 copy-start.58
  774.3 13.9 %slice-start.6 = ((s8[8388608]{0:T(1024)(128)(4,1)}), s8[4194304]{0:T(1024)(128)(4,1)S(1)}, s32[]{:S(2)}) async-start(s8[8388608]{0:T(1024)(128)(4,1)} %bitcast.488), calls=%async_computation.16 | async-start | bytes 8388608
  788.3 14.5 %slice-start.4 = ((s8[8388608]{0:T(1024)(128)(4,1)}), s8[4194304]{0:T(1024)(128)(4,1)S(1)}, s32[]{:S(2)}) async-start(s8[8388608]{0:T(1024)(128)(4,1)} %bitcast.484), calls=%async_computation.14 | async-start | bytes 8388608
  795.0 7.7 slice-start.5
  852.2 80.4 %reduce-scatter.10.cloned.1.call-start = ((), (), s32[]{:S(2)}) async-start(), calls=%async_computation.8 | async-start | bytes 2621440
  872.2 8.1 slice-start
  900.2 166.6 %reduce-scatter.8.cloned.1.call-start = ((), (), s32[]{:S(2)}) async-start(), calls=%async_computation.5 | async-start | bytes 10027008 | tf_op jit(solution)/shard_map/reduce_scatter | solution.py:316
  955.3 143.6 %all-reduce.2.cloned.1.call-start = ((), (), s32[]{:S(2)}) async-start(), calls=%async_computation.6 | async-start | bytes 1179648 | tf_op jit(solution)/shard_map/psum | solution.py:317
  1008.3 8.5 copy-start.24
  1014.6 8.3 slice-start.25
  1023.0 9.7 slice-start.23
  1040.7 26.2 %copy-start.65 = (bf16[256,2048]{0,1:T(8,128)(2,1)S(1)}, bf16[256,2048]{0,1:T(8,128)(2,1)}, u32[]{:S(2)}) copy-start(bf16[256,2048]{0,1:T(8,128)(2,1)} %maximum_convert_fusion.2) | copy-start | bytes 3145732
  1040.7 26.2 %copy-start.98 = (bf16[128,2048]{0,1:T(8,128)(2,1)S(1)}, bf16[128,2048]{0,1:T(8,128)(2,1)}, u32[]{:S(2)}) copy-start(bf16[128,2048]{0,1:T(8,128)(2,1)} %copy.291) | copy-start | bytes 1572868
  1066.8 58.1 %all-gather.8.cloned.1.call-start = ((), (), s32[]{:S(2)}) async-start(), calls=%async_computation.7 | async-start | bytes 2949120 | tf_op jit(solution)/shard_map/all_gather | solution.py:318
  1098.9 17.4 %copy-start.128 = (bf16[16,2048]{1,0:T(8,128)(2,1)S(1)}, bf16[16,2048]{1,0:T(8,128)(2,1)}, u32[]{:S(2)}) copy-start(bf16[16,2048]{1,0:T(8,128)(2,1)} %copy-done.127) | copy-start | bytes 196612
  1098.9 17.4 %copy-start.130 = (bf16[16,2048]{1,0:T(8,128)(2,1)S(1)}, bf16[16,2048]{1,0:T(8,128)(2,1)}, u32[]{:S(2)}) copy-start(bf16[16,2048]{1,0:T(8,128)(2,1)} %copy-done.129) | copy-start | bytes 196612
  1099.0 17.4 %copy-start.182 = (bf16[384,32]{0,1:T(8,128)(2,1)S(1)}, bf16[384,32]{0,1:T(8,128)(2,1)}, u32[]{:S(2)}) copy-start(bf16[384,32]{0,1:T(8,128)(2,1)} %copy-done.181) | copy-start | bytes 73732
  1099.0 18.1 %copy-start.38 = (f32[384,2048]{1,0:T(8,128)S(1)}, f32[384,2048]{1,0:T(8,128)}, u32[]{:S(2)}) copy-start(f32[384,2048]{1,0:T(8,128)} %fusion.168) | copy-start | bytes 9437188
  (194 other events, 627.4 us)
Sparse Core Ops, SparseCore 0:
  489.5 23.2 all-gather.5
  514.9 22.5 all-gather.3
  852.3 32.0 reduce-scatter.11
  900.3 32.2 reduce-scatter.9
  955.4 111.3 reduce-scatter.7
  1069.1 29.7 all-reduce.1
  1100.5 24.0 all-gather.7

commit v2 on v1

v2 whole, which is shorter than its diff:
```python
import functools
import math

import jax
import jax.numpy as jnp
from jax import lax
from jax.experimental import pallas as pl
from jax.experimental.pallas import tpu as pltpu
from jax.sharding import PartitionSpec as P

HDIM = 128
RANK = 16
BLOCK = 512
SCALE = HDIM ** (-0.5)
NEG_FILL = -1e30
BF = jnp.bfloat16
F32 = jnp.float32
MESH = pl.DeviceIdType.MESH
ANY = pl.BlockSpec(memory_space=pl.ANY)
WHOLE = pl.BlockSpec(memory_space=pltpu.VMEM)
SCALARS = pl.BlockSpec(memory_space=pltpu.SMEM)
ROOM = 62 * 2**20


def mm(a, b):
    return jnp.dot(a, b, preferred_element_type=F32)


def mm_nt(a, b):
    return lax.dot_general(a, b, (((1,), (1,)), ((), ())), preferred_element_type=F32)


def mm_tn(a, b):
    return lax.dot_general(a, b, (((0,), (0,)), ((), ())), preferred_element_type=F32)


def norm_stats(values):
    center = values - jnp.mean(values, axis=-1, keepdims=True)
    spread = jnp.mean(center * center, axis=-1, keepdims=True)
    rstd = lax.rsqrt(spread + 1e-05)
    return center * rstd, rstd


def norm_back(values, gain, grad):
    hat, rstd = norm_stats(values)
    e = grad * gain
    return (
        e - jnp.mean(e, axis=-1, keepdims=True) - hat * jnp.mean(e * hat, axis=-1, keepdims=True)
    ) * rstd


def low_of(product, prompt_len):
    row = lax.broadcasted_iota(jnp.int32, product.shape, 0)
    col = lax.broadcasted_iota(jnp.int32, product.shape, 1)
    return jnp.where((row < prompt_len) == (col < RANK), product, 0.0).astype(BF)


def spread_rows(grads, order, ids):
    owner = jnp.repeat(jnp.stack(ids), RANK)
    rank = jnp.arange(RANK * len(ids)) % RANK
    hot = (order[:, None] == (owner * RANK + rank)[None, :]).astype(BF)
    return mm(hot, grads.astype(BF)).astype(BF)


class Gather:
    def __init__(self, n_fs, count, src, dst, sems, lag=2, away=48):
        (self.zs, self.zr, self.ys, self.yr, self.xs, self.xr) = sems[:6]
        (self.cs, self.cr, self.ds, self.dr, self.loc) = sems[6:]
        self.nz, self.count, self.src, self.dst = n_fs, count, src, dst
        self.lag, self.slots, self.last = lag, 2 * lag, n_fs + 2
        self.rows = src.shape[1]
        rep, grp = lax.axis_index("rep"), lax.axis_index("grp")
        self.z = lax.axis_index("fs")
        self.y, self.c, plane = grp // 2, grp % 2, rep % 2
        self.far_rep = rep + 1 - 2 * plane
        self.far_core = self.y * 2 + 1 - self.c
        self.far_row = (1 - self.y) * 2 + self.c
        self.own = grp * n_fs + self.z
        self.away, self.stay = away, self.rows - away
        self.in_first = pl.multiple_of(away * plane, 8)
        self.out_first = pl.multiple_of(self.stay * plane, 8)
        self.far_first = pl.multiple_of(self.stay * (1 - plane), 8)

    @staticmethod
    def semaphores(n_fs, lag=2):
        slots, dma = 2 * lag, pltpu.SemaphoreType.DMA
        return (
            [dma((2 * slots, 2, n_fs)), dma((2 * slots, n_fs))]
            + [dma((slots, n_fs))] * 2
            + [dma((slots, 2 * n_fs))] * 6
            + [dma((slots,))]
        )

    def barrier(self):
        sem = pltpu.get_barrier_semaphore()

        def greet(**where):
            pl.semaphore_signal(sem, 1, device_id=where, device_id_type=MESH)

        greet(rep=self.far_rep)
        greet(grp=self.far_core)
        greet(grp=self.far_row)
        below, above = self.z > 0, self.z < self.nz - 1
        pl.when(below)(lambda: greet(fs=self.z - 1))
        pl.when(above)(lambda: greet(fs=self.z + 1))
        pl.semaphore_wait(sem, 3 + below.astype(jnp.int32) + above.astype(jnp.int32))

    def at_distance(self, d):
        if d < 0 or d >= self.nz:
            return []
        if d == 0:
            return [(None, self.z, 0)]
        return [(self.z >= d, self.z - d, 1), (self.z < self.nz - d, self.z + d, -1)]

    def shard(self, other, fs, core):
        row = 1 - self.y if other else self.y
        return (row * 2 + core) * self.nz + fs

    def send(self, j, shard, first, size, sems, own=False, **where):
        rows = pl.ds(first, size)
        return pltpu.make_async_remote_copy(
            self.src.at[j, rows] if own else self.dst.at[j, shard, rows],
            self.dst.at[j, shard, rows],
            *sems,
            device_id=where,
            device_id_type=MESH,
        )

    def keep(self, j, t):
        sem = self.loc.at[lax.rem(t, self.slots)]
        return pltpu.make_async_copy(self.src.at[j], self.dst.at[j, self.own], sem)

    def sends(self, a, j, t):
        todo, nz, k, kz = [], self.nz, lax.rem(t, self.slots), lax.rem(t, 2 * self.slots)
        inner, outer, far = (self.in_first, self.stay), (self.out_first, self.away), self.far_first

        def both(left, right):
            return right if left is None else jnp.logical_and(left, right)

        for ok, fs, way in self.at_distance(a):
            shard, own = self.shard(0, fs, self.c), a == 0
            if way >= 0:
                sems = (self.zs.at[kz, 0, fs], self.zr.at[kz, fs])
                up = self.send(j, shard, *inner, sems, own, fs=self.z + 1)
                todo.append((both(ok, self.z < nz - 1), up))
            if way <= 0:
                sems = (self.zs.at[kz, 1, fs], self.zr.at[kz, fs])
                down = self.send(j, shard, *inner, sems, own, fs=self.z - 1)
                todo.append((both(ok, self.z > 0), down))
            sems = (self.ys.at[k, fs], self.yr.at[k, fs])
            todo.append((ok, self.send(j, shard, *inner, sems, own, grp=self.far_row)))
            if not own:
                sems = (self.xs.at[k, fs], self.xr.at[k, fs])
                todo.append((ok, self.send(j, shard, *outer, sems, rep=self.far_rep)))
            sems = (self.cs.at[k, fs], self.cr.at[k, fs])
            size = (0, self.rows) if own else inner
            todo.append((ok, self.send(j, shard, *size, sems, own, grp=self.far_core)))
        for ok, fs, _ in self.at_distance(a - 1):
            shard = self.shard(1, fs, self.c)
            sems = (self.xs.at[k, nz + fs], self.xr.at[k, nz + fs])
            todo.append((ok, self.send(j, shard, *outer, sems, rep=self.far_rep)))
            sems = (self.cs.at[k, nz + fs], self.cr.at[k, nz + fs])
            todo.append((ok, self.send(j, shard, *inner, sems, grp=self.far_core)))
        for other in (0, 1):
            for ok, fs, way in self.at_distance(a - 1 - other):
                if way or other:
                    i = other * nz + fs
                    sems = (self.ds.at[k, i], self.dr.at[k, i])
                    shard = self.shard(other, fs, self.c)
                    core = self.send(j, shard, far, self.away, sems, grp=self.far_core)
                    todo.append((ok, core))
        return todo

    def arrivals(self, a, j, t):
        todo, nz, k, kz = [], self.nz, lax.rem(t, self.slots), lax.rem(t, 2 * self.slots)
        inner, far = (self.in_first, self.stay), (self.far_first, self.away)

        def expect(ok, shard, first, size, sem):
            ref = self.dst.at[j, shard, pl.ds(first, size)]
            todo.append((ok, pltpu.make_async_copy(ref, ref, sem)))

        for ok, fs, way in self.at_distance(a):
            if way:
                expect(ok, self.shard(0, fs, self.c), *inner, self.zr.at[kz, fs])
        for ok, fs, _ in self.at_distance(a - 1):
            expect(ok, self.shard(1, fs, self.c), *inner, self.yr.at[k, fs])
        for other in (0, 1):
            for ok, fs, way in self.at_distance(a - 1 - other):
                i = other * nz + fs
                if way or other:
                    expect(ok, self.shard(other, fs, self.c), *far, self.xr.at[k, i])
                size = inner if way or other else (0, self.rows)
                expect(ok, self.shard(other, fs, 1 - self.c), *size, self.cr.at[k, i])
            for ok, fs, way in self.at_distance(a - 2 - other):
                if way or other:
                    i = other * nz + fs
                    expect(ok, self.shard(other, fs, 1 - self.c), *far, self.dr.at[k, i])
        return todo

    def run(self, early=None, compute=None):
        lag = self.lag

        def act(ok, fn):
            if ok is None:
                fn()
            else:
                pl.when(ok)(fn)

        def finish(a, j, t):
            for ok, copy in self.sends(a - 1, j, t):
                act(ok, copy.wait_send)
            for ok, copy in self.arrivals(a, j, t):
                act(ok, copy.wait)
            if a == 1:
                self.keep(j, t).wait()

        def begin(a, j, t):
            for ok, copy in self.sends(a, j, t):
                act(ok, copy.start)
            if a == 0:
                self.keep(j, t).start()

        def tick(t, carry):
            for a in range(self.last, 0, -1):
                j = t - lag * a
                pl.when((j >= 0) & (j < self.count))(functools.partial(finish, a, j, t - lag))
            for a in range(self.last - 1, -1, -1):
                j = t - lag * a
                pl.when((j >= 0) & (j < self.count))(functools.partial(begin, a, j, t))
            if early is not None:
                early(t)
            if compute is not None:
                j = t - lag * self.last
                pl.when(j >= 0)(functools.partial(compute, j))
            return carry

        lax.fori_loop(0, self.count + lag * self.last + (compute is not None), tick, 0)


def head_columns(ref, rows, part, h, width):
    first = pl.multiple_of(part * width + h * HDIM, HDIM)
    return ref[rows, pl.ds(first, HDIM)]


def seen(shape, first):
    row = lax.broadcasted_iota(jnp.int32, shape, 0)
    return lax.broadcasted_iota(jnp.int32, shape, 1) <= first + row


def head_chances(qkv, kp, h, prompt_len, width, first):
    own, cont = slice(0, prompt_len), slice(prompt_len, None)
    q_p = head_columns(qkv, own, 0, h, width)
    q_c = head_columns(qkv, cont, 0, h, width)
    k_c = head_columns(qkv, cont, 1, h, width)
    v_c = head_columns(qkv, cont, 2, h, width)
    lanes = pl.ds(pl.multiple_of(h * HDIM, HDIM), HDIM)
    k_p = kp[:, :, lanes].reshape(-1, HDIM)
    lanes = pl.ds(pl.multiple_of(width + h * HDIM, HDIM), HDIM)
    v_p = kp[:, :, lanes].reshape(-1, HDIM)
    s_p = mm_nt(q_p, k_p) * SCALE
    s_p = jnp.where(seen(s_p.shape, first), s_p, NEG_FILL)
    e_p = jnp.exp(s_p - jnp.max(s_p, axis=-1, keepdims=True))
    c_p = e_p * (1.0 / jnp.sum(e_p, axis=-1, keepdims=True))
    s_1 = mm_nt(q_c, k_p) * SCALE
    s_2 = mm_nt(q_c, k_c) * SCALE
    s_2 = jnp.where(seen(s_2.shape, 0), s_2, NEG_FILL)
    peak = jnp.maximum(
        jnp.max(s_1, axis=-1, keepdims=True), jnp.max(s_2, axis=-1, keepdims=True)
    )
    e_1, e_2 = jnp.exp(s_1 - peak), jnp.exp(s_2 - peak)
    mass = jnp.sum(e_1, axis=-1, keepdims=True) + jnp.sum(e_2, axis=-1, keepdims=True)
    inv = 1.0 / mass
    return (q_p, q_c, k_p, k_c, v_p, v_c), (c_p, e_1 * inv, e_2 * inv)


def project_call(x, gain, bias, ids, a_tab, b_tab, blocks, n_fs, n_shard, prompt_len):
    count, shard_rows, _ = blocks.shape
    rows, width = x.shape
    per = width // BLOCK

    def kernel(
        x, gain, bias, ids, a_tab, b_tab, src, dst, qkv, normed, lows, a_ext, b_ext, wbuf, wsem, *sems
    ):
        engine = Gather(n_fs, count, src, dst, sems)
        engine.barrier()

        def load(j):
            return pltpu.make_async_copy(dst.at[j], wbuf.at[lax.rem(j, 2)], wsem.at[lax.rem(j, 2)])

        def early(t):
            @pl.when(t == 0)
            def _():
                for i in range(2):
                    part = slice(i * RANK, (i + 1) * RANK)
                    for n in range(3):
                        a_ext[n, part] = a_tab[ids[i], n]
                        b_ext[n, part] = b_tab[ids[i], n]
                hat, _ = norm_stats(x[...].astype(F32))
                normed[...] = (hat * gain[...] + bias[...]).astype(BF)
                for n in range(3):
                    lows[n] = low_of(mm_nt(normed[...], a_ext[n]), prompt_len)

        def compute(j):
            @pl.when(j < count)
            def _():
                load(j).start()

            @pl.when(j > 0)
            def _():
                i = j - 1
                load(i).wait()
                n = i // per
                w = wbuf[lax.rem(i, 2)].reshape(-1, BLOCK)
                inside = pl.ds(pl.multiple_of(lax.rem(i, per) * BLOCK, BLOCK), BLOCK)
                extra = mm(lows[n], b_ext[n, :, inside])
                cols = pl.ds(pl.multiple_of(i * BLOCK, BLOCK), BLOCK)
                qkv[:, cols] = (mm(normed[...], w) + extra).astype(BF)

        engine.run(early, compute)

    return pl.pallas_call(
        kernel,
        out_shape=[
            jax.ShapeDtypeStruct((count, n_shard, shard_rows, BLOCK), BF),
            jax.ShapeDtypeStruct((rows, 3 * width), BF),
            jax.ShapeDtypeStruct((rows, width), BF),
            jax.ShapeDtypeStruct((3, rows, 2 * RANK), BF),
        ],
        in_specs=[WHOLE, WHOLE, WHOLE, SCALARS, WHOLE, WHOLE, ANY],
        out_specs=[ANY, WHOLE, WHOLE, WHOLE],
        scratch_shapes=[
            pltpu.VMEM((3, 2 * RANK, width), BF),
            pltpu.VMEM((3, 2 * RANK, width), BF),
            pltpu.VMEM((2, n_shard, shard_rows, BLOCK), BF),
            pltpu.SemaphoreType.DMA((2,)),
        ]
        + Gather.semaphores(n_fs),
        compiler_params=pltpu.CompilerParams(
            collective_id=0, has_side_effects=True, vmem_limit_bytes=ROOM
        ),
        name="project",
    )(x, gain, bias, ids, a_tab, b_tab, blocks)


def middle_call(x, cot, qkv, gain, bias, ids, tables, blocks, counts, n_fs, n_shard, prompt_len):
    rows, width = x.shape
    shard_rows = blocks.shape[1]
    n_out, n_dn, n_up = counts
    count = n_out + n_dn + n_up
    hidden = n_up * BLOCK
    n_grp = n_shard // n_fs
    parts = n_dn // n_out
    heads = width // HDIM
    go, first_head = 4, 5
    first_out = first_head + heads
    a_o, b_o, a_u, b_u, a_d, b_d = range(6)

    def kernel(
        x,
        cot,
        qkv,
        gain,
        bias,
        ids,
        *refs,
    ):
        tabs, refs = refs[:6], refs[6:]
        src, refs = refs[0], refs[1:]
        (dst, kp, mixed, normed, result, resid_back, grad_attn), refs = refs[:7], refs[7:]
        (low_o, g_a_up, g_b_up, g_a_dn, g_b_dn), refs = refs[:5], refs[5:]
        ext, refs = refs[:6], refs[6:]
        (resid, out_acc, low_up, dlow_dn, low_dn, dlow_up), refs = refs[:6], refs[6:]
        (wbuf, dbuf, wsem, dsem, ksend, krecv, kloc), sems = refs[:7], refs[7:]
        engine = Gather(n_fs, count, src, dst, sems)
        engine.barrier()
        grp = lax.axis_index("grp")

        def pass_on(n, whose, to):
            return pltpu.make_async_remote_copy(
                kp.at[whose],
                kp.at[whose],
                ksend.at[n],
                krecv.at[n],
                device_id={"grp": to},
                device_id_type=MESH,
            )

        def landed(n, whose):
            return pltpu.make_async_copy(kp.at[whose], kp.at[whose], krecv.at[n])

        to_row = pass_on(0, grp, engine.far_row)
        to_core = pass_on(1, grp, engine.far_core)
        onward = pass_on(2, engine.far_row, engine.far_core)
        diagonal = (1 - engine.y) * 2 + 1 - engine.c

        def load_out(b):
            return pltpu.make_async_copy(dst.at[b], wbuf.at[lax.rem(b, 2)], wsem.at[lax.rem(b, 2)])

        def early(t):
            @pl.when(t == 0)
            def _():
                kp[grp] = qkv[:prompt_len, width:]
                to_row.start()
                to_core.start()
                for n, tab in enumerate(tabs):
                    for i in range(2):
                        ext[n][i * RANK : (i + 1) * RANK] = tab[ids[i]]
                dlow_dn[...] = low_of(mm_nt(cot[...], ext[b_d][...]), prompt_len)

            @pl.when(t == go)
            def _():
                landed(0, engine.far_row).wait()
                onward.start()

            @pl.when(t == first_head)
            def _():
                landed(1, engine.far_core).wait()
                landed(2, diagonal).wait()
                to_row.wait_send()
                to_core.wait_send()
                onward.wait_send()

            @pl.when((t >= first_head) & (t < first_out))
            def _():
                h = t - first_head
                (_, _, _, _, v_p, v_c), (c_p, c_1, c_2) = head_chances(
                    qkv, kp, h, prompt_len, width, grp * prompt_len
                )
                lanes = pl.ds(pl.multiple_of(h * HDIM, HDIM), HDIM)
                mixed[:prompt_len, lanes] = mm(c_p.astype(BF), v_p).astype(BF)
                mixed[prompt_len:, lanes] = (
                    mm(c_1.astype(BF), v_p) + mm(c_2.astype(BF), v_c)
                ).astype(BF)

            @pl.when(t == first_out - 1)
            def _():
                load_out(0).start()

            @pl.when((t >= first_out) & (t < first_out + n_out))
            def _():
                b = t - first_out

                @pl.when(b == 0)
                def _():
                    low_o[...] = low_of(mm_nt(mixed[...], ext[a_o][...]), prompt_len)

                load_out(b).wait()

                @pl.when(b + 1 < n_out)
                def _():
                    load_out(b + 1).start()

                cols = pl.ds(pl.multiple_of(b * BLOCK, BLOCK), BLOCK)
                w = wbuf[lax.rem(b, 2)].reshape(-1, BLOCK)
                branch = mm(mixed[...], w) + mm(low_o[...], ext[b_o][:, cols])
                resid[:, cols] = x[:, cols].astype(F32) + branch

            @pl.when(t == first_out + n_out)
            def _():
                hat, _ = norm_stats(resid[...])
                normed[...] = (hat * gain[...] + bias[...]).astype(BF)
                low_up[...] = low_of(mm_nt(normed[...], ext[a_u][...]), prompt_len)
                out_acc[...] = resid[...]
                resid_back[...] = jnp.zeros_like(resid_back)
                low_dn[...] = jnp.zeros_like(low_dn)
                dlow_up[...] = jnp.zeros_like(dlow_up)

        def load_up(n):
            k = lax.rem(n, 2)
            up = pltpu.make_async_copy(dst.at[n_out + n_dn + n], wbuf.at[k], wsem.at[k])
            down = pltpu.make_async_copy(dst.at[pl.ds(n_out, n_dn), n], dbuf.at[k], dsem.at[k])
            return up, down

        def compute(j):
            n = j - (n_out + n_dn)

            @pl.when((n >= 0) & (n < n_up))
            def _():
                for copy in load_up(n):
                    copy.start()

            @pl.when(n > 0)
            def _():
                i = n - 1
                for copy in load_up(i):
                    copy.wait()
                k = lax.rem(i, 2)
                cols = pl.ds(pl.multiple_of(i * BLOCK, BLOCK), BLOCK)
                w_up = wbuf[k].reshape(-1, BLOCK)
                a_dn, b_up = ext[a_d][:, cols], ext[b_u][:, cols]
                pre = mm(normed[...], w_up) + mm(low_up[...], b_up)
                cdf = 0.5 * (1.0 + lax.erf(pre * math.sqrt(0.5)))
                act = (pre * cdf).astype(BF)
                slope = cdf + pre * jnp.exp(-0.5 * pre * pre) * (1.0 / math.sqrt(2.0 * math.pi))
                grad_act = mm(dlow_dn[...], a_dn)
                for b in range(n_out):
                    w_dn = dbuf[k, b * parts : (b + 1) * parts].reshape(BLOCK, BLOCK)
                    span = slice(b * BLOCK, (b + 1) * BLOCK)
                    grad_act = grad_act + mm_nt(cot[:, span], w_dn)
                    out_acc[:, span] += mm(act, w_dn)
                grad_pre = (grad_act * slope).astype(BF)
                resid_back[...] += mm_nt(grad_pre, w_up)
                low_dn[...] += mm_nt(act, a_dn)
                dlow_up[...] += mm_nt(grad_pre, b_up)
                g_b_up[:, cols] = mm_tn(low_up[...], grad_pre).astype(BF)
                g_a_dn[:, cols] = mm_tn(dlow_dn[...], act).astype(BF)

        engine.run(early, compute)
        low = low_of(low_dn[...], prompt_len)
        result[...] = (out_acc[...] + mm(low, ext[b_d][...])).astype(BF)
        g_b_dn[...] = mm_tn(low, cot[...]).astype(BF)
        dlow = low_of(dlow_up[...], prompt_len)
        g_a_up[...] = mm_tn(dlow, normed[...]).astype(BF)
        grad = resid_back[...] + mm(dlow, ext[a_u][...])
        grad = cot[...].astype(F32) + norm_back(resid[...], gain[...], grad)
        resid_back[...] = grad
        grad_attn[...] = grad.astype(BF)

    like = jax.ShapeDtypeStruct
    two = 2 * RANK
    return pl.pallas_call(
        kernel,
        out_shape=[
            like((count, n_shard, shard_rows, BLOCK), BF),
            like((n_grp, prompt_len, 2 * width), BF),
            like((rows, width), BF),
            like((rows, width), BF),
            like((rows, width), BF),
            like((rows, width), F32),
            like((rows, width), BF),
            like((rows, two), BF),
            like((two, width), BF),
            like((two, hidden), BF),
            like((two, hidden), BF),
            like((two, width), BF),
        ],
        in_specs=[WHOLE] * 5 + [SCALARS] + [WHOLE] * 6 + [ANY],
        out_specs=[ANY] + [WHOLE] * 11,
        scratch_shapes=[
            pltpu.VMEM((two, w), BF) for w in (width, width, width, hidden, hidden, width)
        ]
        + [
            pltpu.VMEM((rows, width), F32),
            pltpu.VMEM((rows, width), F32),
            pltpu.VMEM((rows, two), BF),
            pltpu.VMEM((rows, two), BF),
            pltpu.VMEM((rows, two), F32),
            pltpu.VMEM((rows, two), F32),
            pltpu.VMEM((2, n_shard, shard_rows, BLOCK), BF),
            pltpu.VMEM((2, n_dn, shard_rows, BLOCK), BF),
            pltpu.SemaphoreType.DMA((2,)),
            pltpu.SemaphoreType.DMA((2,)),
            pltpu.SemaphoreType.DMA((3,)),
            pltpu.SemaphoreType.DMA((3,)),
            pltpu.SemaphoreType.DMA((1,)),
        ]
        + Gather.semaphores(n_fs),
        compiler_params=pltpu.CompilerParams(
            collective_id=1, has_side_effects=True, vmem_limit_bytes=ROOM
        ),
        name="middle",
    )(x, cot, qkv, gain, bias, ids, *tables, blocks)


def attention_back_call(grad_attn, mixed, low_o, qkv, kp, ids, a_tab, b_tab, w_out, n_out, prompt_len):
    rows, width = grad_attn.shape
    heads = width // HDIM
    total = kp.shape[0] * prompt_len
    n_shard, shard_rows = w_out.shape[1:3]

    def kernel(
        grad_attn, mixed, low_o, qkv, kp, ids, a_tab, b_tab, w, g_q, g_own, g_far, g_a, g_b, a_ext, b_ext, dlow, acc, gm
    ):
        step = pl.program_id(0)

        @pl.when(step == 0)
        def _():
            for i in range(2):
                part = slice(i * RANK, (i + 1) * RANK)
                a_ext[part] = a_tab[ids[i]]
                b_ext[part] = b_tab[ids[i]]
            dlow[...] = low_of(mm_nt(grad_attn[...], b_ext[...]), prompt_len)
            acc[...] = mm(dlow[...], a_ext[...])
            g_a[...] = mm_tn(dlow[...], mixed[...]).astype(BF)
            g_b[...] = mm_tn(low_o[...], grad_attn[...]).astype(BF)

        @pl.when(step < n_out)
        def _():
            cols = pl.ds(pl.multiple_of(step * BLOCK, BLOCK), BLOCK)
            acc[...] += mm_nt(grad_attn[:, cols], w[0].reshape(-1, BLOCK))

        @pl.when(step == n_out - 1)
        def _():
            gm[...] = acc[...].astype(BF)

        @pl.when(step >= n_out)
        def _():
            h = step - n_out
            first = lax.axis_index("grp") * prompt_len
            (q_p, q_c, k_p, k_c, v_p, v_c), (c_p, c_1, c_2) = head_chances(
                qkv, kp, h, prompt_len, width, first
            )
            lanes = pl.ds(pl.multiple_of(h * HDIM, HDIM), HDIM)
            far = pl.ds(pl.multiple_of(width + h * HDIM, HDIM), HDIM)
            gm_p, gm_c = gm[:prompt_len, lanes], gm[prompt_len:, lanes]
            d_p = mm_nt(gm_p, v_p)
            d_1, d_2 = mm_nt(gm_c, v_p), mm_nt(gm_c, v_c)
            s_p = (c_p * (d_p - jnp.sum(c_p * d_p, axis=-1, keepdims=True))).astype(BF)
            inner = jnp.sum(c_1 * d_1, axis=-1, keepdims=True) + jnp.sum(
                c_2 * d_2, axis=-1, keepdims=True
            )
            s_1 = (c_1 * (d_1 - inner)).astype(BF)
            s_2 = (c_2 * (d_2 - inner)).astype(BF)
            g_q[:prompt_len, lanes] = (mm(s_p, k_p) * SCALE).astype(BF)
            g_q[prompt_len:, lanes] = ((mm(s_1, k_p) + mm(s_2, k_c)) * SCALE).astype(BF)
            g_own[:, lanes] = (mm_tn(s_2, q_c) * SCALE).astype(BF)
            g_own[:, far] = mm_tn(c_2.astype(BF), gm_c).astype(BF)
            g_far[:, lanes] = ((mm_tn(s_p, q_p) + mm_tn(s_1, q_c)) * SCALE).astype(BF)
            g_far[:, far] = (mm_tn(c_p.astype(BF), gm_p) + mm_tn(c_1.astype(BF), gm_c)).astype(BF)

    like = jax.ShapeDtypeStruct
    two = 2 * RANK
    return pl.pallas_call(
        kernel,
        grid=(n_out + heads,),
        out_shape=[
            like((rows, width), BF),
            like((rows - prompt_len, 2 * width), BF),
            like((total, 2 * width), BF),
            like((two, width), BF),
            like((two, width), BF),
        ],
        in_specs=[WHOLE] * 5
        + [SCALARS, WHOLE, WHOLE]
        + [
            pl.BlockSpec(
                (1, n_shard, shard_rows, BLOCK), lambda i: (jnp.minimum(i, n_out - 1), 0, 0, 0)
            )
        ],
        out_specs=[WHOLE] * 5,
        scratch_shapes=[
            pltpu.VMEM((two, width), BF),
            pltpu.VMEM((two, width), BF),
            pltpu.VMEM((rows, two), BF),
            pltpu.VMEM((rows, width), F32),
            pltpu.VMEM((rows, width), BF),
        ],
        compiler_params=pltpu.CompilerParams(vmem_limit_bytes=ROOM),
        name="attention_back",
    )(grad_attn, mixed, low_o, qkv, kp, ids, a_tab, b_tab, w_out)


def project_back_call(grads, x, normed, lows, grad_resid, gain, ids, a_tab, b_tab, w_qkv, prompt_len):
    rows, width = x.shape
    count, n_shard, shard_rows, _ = w_qkv.shape
    per = width // BLOCK

    def kernel(
        grads, x, normed, lows, grad_resid, gain, ids, a_tab, b_tab, w, out, g_a, g_b, a_ext, b_ext, dlow, acc
    ):
        j = pl.program_id(0)
        n = j // per

        @pl.when(j == 0)
        def _():
            for i in range(2):
                part = slice(i * RANK, (i + 1) * RANK)
                for m in range(3):
                    a_ext[m, part] = a_tab[ids[i], m]
                    b_ext[m, part] = b_tab[ids[i], m]
            acc[...] = jnp.zeros_like(acc)
            dlow[...] = jnp.zeros_like(dlow)

        inside = pl.ds(pl.multiple_of(lax.rem(j, per) * BLOCK, BLOCK), BLOCK)
        part = grads[...]
        acc[...] += mm_nt(part, w[0].reshape(-1, BLOCK))
        dlow[n] += mm_nt(part, b_ext[n, :, inside])
        g_b[...] = mm_tn(lows[n], part).astype(BF)

        @pl.when(j == count - 1)
        def _():
            for m in range(3):
                low = low_of(dlow[m], prompt_len)
                acc[...] += mm(low, a_ext[m])
                g_a[m] = mm_tn(low, normed[...]).astype(BF)
            back = norm_back(x[...].astype(F32), gain[...], acc[...])
            out[...] = (grad_resid[...] + back).astype(BF)

    like = jax.ShapeDtypeStruct
    two = 2 * RANK
    return pl.pallas_call(
        kernel,
        grid=(count,),
        out_shape=[like((rows, width), BF), like((3, two, width), BF), like((two, 3 * width), BF)],
        in_specs=[pl.BlockSpec((rows, BLOCK), lambda j: (0, j))]
        + [WHOLE] * 5
        + [SCALARS, WHOLE, WHOLE]
        + [pl.BlockSpec((1, n_shard, shard_rows, BLOCK), lambda j: (j, 0, 0, 0))],
        out_specs=[WHOLE, WHOLE, pl.BlockSpec((two, BLOCK), lambda j: (0, j))],
        scratch_shapes=[
            pltpu.VMEM((3, two, width), BF),
            pltpu.VMEM((3, two, width), BF),
            pltpu.VMEM((3, rows, two), F32),
            pltpu.VMEM((rows, width), F32),
        ],
        compiler_params=pltpu.CompilerParams(vmem_limit_bytes=ROOM),
        name="project_back",
    )(grads, x, normed, lows, grad_resid, gain, ids, a_tab, b_tab, w_qkv)


def make_body(sizes):
    n_rep, n_grp, n_fs = sizes
    n_shard = n_grp * n_fs

    def reduce_tables(grads, ids, count):
        per, r_lo, width = count // n_fs, RANK // n_grp, grads.shape[1]
        order = jnp.arange(count * RANK).reshape(n_fs, per, n_grp, r_lo)
        v = spread_rows(grads, order.transpose(2, 0, 1, 3).reshape(-1), ids)
        v = lax.psum_scatter(v, ("grp", "fs"), scatter_dimension=0, tiled=True)
        v = lax.psum(v, "rep")
        v = lax.all_gather(v, "grp", axis=0, tiled=True)
        v = v.reshape(n_grp, per, r_lo, width).transpose(1, 0, 2, 3)
        return v.reshape(per, RANK, width).astype(F32)

    def body(
        prompt_input_rows,
        continuation_input,
        prompt_group_adapter,
        continuation_adapter,
        first_norm_scale,
        first_norm_bias,
        second_norm_scale,
        second_norm_bias,
        frozen_query_key_value,
        frozen_output_weight,
        frozen_up_weight,
        frozen_down_weight,
        adapter_attention_input,
        adapter_attention_output,
        adapter_up_input,
        adapter_up_output,
        adapter_down_input,
        adapter_down_output,
        prompt_cotangent,
        continuation_cotangent,
    ):
        prompt_len, width = prompt_input_rows.shape[2:]
        cont_len = continuation_input.shape[3]
        count = adapter_up_input.shape[0]
        hidden = frozen_up_weight.shape[1]
        shard_rows = frozen_query_key_value.shape[0]
        parts = frozen_down_weight.shape[0] // shard_rows
        assert hidden == n_shard * BLOCK and parts * shard_rows == BLOCK

        def tokens(prompt, cont):
            return jnp.concatenate(
                [prompt.reshape(prompt_len, width), cont.reshape(cont_len, width)], 0
            )

        def columns(w):
            return w.reshape(shard_rows, -1, BLOCK).swapaxes(0, 1)

        x = tokens(prompt_input_rows, continuation_input)
        cot = tokens(prompt_cotangent, continuation_cotangent)
        ids = jnp.concatenate(
            [prompt_group_adapter.reshape(1), continuation_adapter.reshape(1)]
        )
        a_attn = adapter_attention_input.swapaxes(2, 3)
        b_attn = adapter_attention_output
        a_up, b_up = adapter_up_input.swapaxes(1, 2), adapter_up_output
        a_dn, b_dn = adapter_down_input.swapaxes(1, 2), adapter_down_output
        gain_one, bias_one, gain_two, bias_two = [
            v[None, :]
            for v in (first_norm_scale, first_norm_bias, second_norm_scale, second_norm_bias)
        ]
        w_qkv, qkv, normed_one, lows = project_call(
            x,
            gain_one,
            bias_one,
            ids,
            a_attn,
            b_attn,
            columns(frozen_query_key_value),
            n_fs,
            n_shard,
            prompt_len,
        )
        dn_blocks = frozen_down_weight.reshape(parts, shard_rows, -1, BLOCK).transpose(2, 0, 1, 3)
        blocks = [
            columns(frozen_output_weight),
            dn_blocks.reshape(-1, shard_rows, BLOCK),
            columns(frozen_up_weight),
        ]
        counts = [b.shape[0] for b in blocks]
        tables = (a_attn[:, 3], b_attn[:, 3], a_up, b_up, a_dn, b_dn)
        (
            w_rest,
            kp,
            mixed,
            normed_two,
            result,
            grad_resid,
            grad_attn,
            low_o,
            g_a_up,
            g_b_up,
            g_a_dn,
            g_b_dn,
        ) = middle_call(
            x,
            cot,
            qkv,
            gain_two,
            bias_two,
            ids,
            tables,
            jnp.concatenate(blocks, 0),
            counts,
            n_fs,
            n_shard,
            prompt_len,
        )
        g_q, g_own, g_far, g_a_o, g_b_o = attention_back_call(
            grad_attn,
            mixed,
            low_o,
            qkv,
            kp,
            ids,
            tables[0],
            tables[1],
            w_rest,
            counts[0],
            prompt_len,
        )
        g_mine = lax.psum_scatter(g_far, "grp", scatter_dimension=0, tiled=True)
        grads = jnp.concatenate([g_q, jnp.concatenate([g_mine, g_own], 0)], 1)
        grad_inputs, g_a, g_b = project_back_call(
            grads, x, normed_one, lows, grad_resid, gain_one, ids, a_attn, b_attn, w_qkv, prompt_len
        )
        flat = [g_b_up, g_a_dn, g_a[0], g_a[1], g_a[2], g_a_o, g_b, g_b_o, g_a_up, g_b_dn]
        slim = reduce_tables(jnp.concatenate(flat, 1), [ids[0], ids[1]], count)
        both = [slim[:, :, :hidden], slim[:, :, hidden : 2 * hidden]]
        slim = slim[:, :, 2 * hidden :].reshape(slim.shape[0], RANK, 10, width).transpose(0, 2, 1, 3)

        return (
            result[:prompt_len].reshape(prompt_input_rows.shape),
            result[prompt_len:].reshape(continuation_input.shape),
            grad_inputs[:prompt_len].reshape(prompt_input_rows.shape),
            grad_inputs[prompt_len:].reshape(continuation_input.shape),
            slim[:, :4].swapaxes(2, 3),
            slim[:, 4:8],
            slim[:, 8].swapaxes(1, 2),
            both[0],
            both[1].swapaxes(1, 2),
            slim[:, 9],
        )

    return body


def solution(mesh):
    sizes = (mesh.shape["rep"], mesh.shape["grp"], mesh.shape["fs"])
    rows_in = P("rep", "fs", "grp", None)
    conts_in = P("rep", "fs", "grp", None, None)
    weight = P(("grp", "fs"), None)
    return jax.shard_map(
        make_body(sizes),
        mesh=mesh,
        in_specs=(
            rows_in,
            conts_in,
            P("rep", "fs"),
            P("rep", "fs", "grp"),
            P(),
            P(),
            P(),
            P(),
            weight,
            weight,
            weight,
            weight,
            P(),
            P(),
            P(),
            P(),
            P(),
            P(),
            rows_in,
            conts_in,
        ),
        out_specs=(
            rows_in,
            conts_in,
            rows_in,
            conts_in,
            P("fs", None, None, None),
            P("fs", None, None, None),
            P("fs", None, None),
            P("fs", None, None),
            P("fs", None, None),
            P("fs", None, None),
        ),
        check_vma=False,
    )
```

time: 1180 us -> 829 us (0.70); the launches traced: 1170 us -> 828 us
  local copies, waits for them, and re-layouts: 378 us -> 64.9 us
  matrix products: 281 us -> 6.77 us
  Pallas kernels: 373 us -> 522 us
  waiting for transfers between devices: 65.6 us -> 210 us
  other arithmetic: 47.7 us -> 9.31 us
    dot_general x80 -> x0, matrix products: 236 us -> none  [the longest x10 81 us: times_t(): return jnp.einsum('rbc,bkc->rk', g, w, preferred_element_type=F32)]
    pallas_call x1 -> x4, Pallas kernels: 373 us -> 522 us  [the longest x1 340 us: middle_call(): pl.pallas_call(kernel, out_shape=[like((count, n_shard, shard_rows, BLOCK...]
    dot_general x10 -> x0, local copies, waits for them, and re-layouts: 138 us -> none  [times(): jnp.einsum('rk,bkc->rbc', u, w, preferred_element_type=F32)]
    reduce_scatter x1, waiting for transfers between devices: 24.2 us -> 111 us  [reduce_tables(): v = lax.psum_scatter(v, ('grp', 'fs'), scatter_dimension=0, tiled=True)]
    slice x13 -> x0, local copies, waits for them, and re-layouts: 80.3 us -> none  [the longest x1 49.3 us: body(): w_dn[n * per:(n + 1) * per]]
    reduce_scatter x0 -> x1, waiting for transfers between devices: none -> 44.7 us  [body(): g_mine = lax.psum_scatter(g_far, 'grp', scatter_dimension=0, tiled=True)]
    dot_general x19 -> x1, matrix products: 44.6 us -> 6.77 us  [mm(): return jnp.dot(a, b, preferred_element_type=F32)]
    unnamed x521 -> x50, local copies, waits for them, and re-layouts: 58.8 us -> 21.8 us
  transfers between devices with their start and end apart: 7 -> 4, of which waited for: 3 -> 4; matrix products, arithmetic and copies ran while one was open for 32% -> 1% of each run, Pallas kernels for 0% -> 0%
where the time goes in v2:
time: 829 us; the launch traced here: 828 us
  Pallas kernels  522 us (63%)
  waiting for transfers between devices  210 us (25%)
  local copies, waits for them, and re-layouts  64.9 us (8%)
  between operations  15.3 us (2%)
  other arithmetic  9.31 us (1%)
    pallas_call x1, Pallas kernels, middle_call(): pl.pallas_call(kernel, out_shape=[like((count, n_shard, shard_rows, BLOCK...  340 us
    pallas_call x1, Pallas kernels, project_call(): pl.pallas_call(kernel, out_shape=[jax.ShapeDtypeStruct((count, n_shard, s...  118 us
    reduce_scatter x1, waiting for transfers between devices, reduce_tables(): v = lax.psum_scatter(v, ('grp', 'fs'), scatter_dimension=0, tiled=True)  111 us
    reduce_scatter x1, waiting for transfers between devices, body(): g_mine = lax.psum_scatter(g_far, 'grp', scatter_dimension=0, tiled=True)  44.7 us
    pallas_call x1, Pallas kernels, attention_back_call(): pl.pallas_call(kernel, grid=(n_out + heads,), out_shape=[like((rows, widt...  36.2 us
    psum x1, waiting for transfers between devices, reduce_tables(): v = lax.psum(v, 'rep')  32 us
    pallas_call x1, Pallas kernels, project_back_call(): pl.pallas_call(kernel, grid=(count,), out_shape=[like((rows, width), BF),...  27.5 us
    all_gather x1, waiting for transfers between devices, reduce_tables(): v = lax.all_gather(v, 'grp', axis=0, tiled=True)  21.8 us
  transfers between devices with their start and end apart: 4, of which 4 were waited for; matrix products, arithmetic and copies ran while one was open for 1% of the time, Pallas kernels for 0%

profile of v2, /device:TPU:0, one launch (start us, length us, event | category | flops | bytes accessed | tf_op | source)
XLA Modules:
  0.0 828.0 jit_solution(11804452395095107123)
XLA Ops:
  7.2 0.0 reduce-scatter.3.cloned.1.call-start
  8.5 1.9 copy.35
  10.4 1.6 copy.36
  12.0 3.3 reshape.160
  15.3 1.8 copy.40
  17.1 3.2 copy.41
  20.3 0.0 copy-start.10
  20.3 2.6 copy.42
  22.9 0.3 copy.38
  23.2 0.2 copy.39
  23.5 0.6 broadcast_multiply_fusion
  24.0 2.4 slice_bitcast_fusion.4
  26.5 0.0 copy-start.7
  26.5 2.6 pad_maximum_fusion.refs_6_
  29.1 0.2 copy-done.8
  29.3 0.6 copy-done.9
  29.9 1.8 pad_maximum_fusion.1
  31.7 118.1 %project.1 = (bf16[12,16,128,512]{3,2,1,0:T(8,128)(2,1)}, bf16[384,6144]{1,0:T(8,128)(2,1)}, bf16[384,2048]{1,0:T(8,128)(2,1)}, bf16[3,384,32]{2,1,0:T(8,128)(2,1)}) custom-call(bf16[384,2048]{1,0:T(8,128)(2,1)} %get-tuple-element.84.x, f32[1,2048]{1,0:T(1,128)} %bitcast.80, f32[1,2048]{1,0:T(1,128)} %bitcast.84, s32[2]{0:T(128)} %get-tuple-element.77.ids, ...), custom_call_target="tpu_custom_call" | custom-call | tf_op jit(solution)/shard_map/project/pallas_call | solution.py:321
  149.8 339.7 %middle.1 = (bf16[36,16,128,512]{3,2,1,0:T(8,128)(2,1)}, bf16[4,128,4096]{2,1,0:T(8,128)(2,1)}, bf16[384,2048]{1,0:T(8,128)(2,1)}, bf16[384,2048]{1,0:T(8,128)(2...) custom-call(bf16[384,2048]{1,0:T(8,128)(2,1)} %get-tuple-element.84., ...), custom_call_target="tpu_custom_call" | custom-call | tf_op jit(solution)/shard_map/middle/pallas_call | solution.py:521
  489.5 36.2 %attention_back.1 = (bf16[384,2048]{1,0:T(8,128)(2,1)}, bf16[256,4096]{1,0:T(8,128)(2,1)}, bf16[512,4096]{1,0:T(8,128)(2,1)}, bf16[32,2048]{1,0:T(8,128)(2,1)}, bf16[32,2048]{1,0:T(8,128)(2,1)}) custom-call(bf16[384,2048]{1,0:T(8,128)(2,1)} %get-tuple-element.35.grad_attn, bf16[384,2048]{1,0:T(8,128)(2,1)} %get-tuple-element.36.mixed, ...), custom_call_target="tpu_custom_call" | custom-call | tf_op jit(solution)/shard_map/attention_back/pallas_call | solution.py:623
  525.8 0.0 reduce-scatter.3.cloned.1.call-update
  525.8 0.0 reduce-scatter.5.cloned.1.call-start
  525.8 0.1 broadcast_in_dim.20
  525.9 0.1 mul.18
  526.0 0.1 reshape.176
  526.1 0.7 copy-done.12
  526.8 0.9 constant_dynamic-update-slice_fusion.6
  527.6 0.8 constant_dynamic-update-slice_fusion.5
  528.5 44.7 %reduce-scatter.3.cloned.1.call-done = bf16[128,4096]{1,0:T(8,128)(2,1)} async-done(((bf16[512,4096]{1,0:T(8,128)(2,1)}), bf16[128,4096]{1,0:T(8,128)(2,1)}) %reduce-scatter.3.cloned.1.call-update) | async-done | bytes 1048592 | tf_op jit(solution)/shard_map/reduce_scatter | solution.py:836
  573.2 4.3 maximum_maximum_fusion.grads
  577.5 27.5 %project_back.1 = (bf16[384,2048]{1,0:T(8,128)(2,1)}, bf16[3,32,2048]{2,1,0:T(8,128)(2,1)}, bf16[32,6144]{1,0:T(8,128)(2,1)}) custom-call(bf16[384,6144]{1,0:T(8,128)(2,1)} %maximum_maximum_fusion.grads, bf16[384,2048]{1,0:T(8,128)(2,1)} %get-tuple-element.84.x, bf16[384,2048]{1,0:T(8,128)(2,1)} %get-tuple-element.43.normed, ...), custom_call_target="tpu_custom_call" | custom-call | tf_op jit(solution)/shard_map/project_back/pallas_call | solution.py:691
  605.0 1.6 bitcast_dynamic-update-slice_fusion.2
  606.6 1.6 bitcast_dynamic-update-slice_fusion.1
  608.2 1.6 bitcast_dynamic-update-slice_fusion
  609.8 0.7 constant_dynamic-update-slice_fusion.4
  610.4 1.8 constant_dynamic-update-slice_fusion.3
  612.2 0.7 constant_dynamic-update-slice_fusion.2
  612.9 0.7 constant_dynamic-update-slice_fusion.1
  613.5 0.7 constant_dynamic-update-slice_fusion
  614.2 6.8 convolution_convert_fusion
  621.0 0.0 reduce-scatter.5.cloned.1.call-update
  621.0 0.0 all-reduce.2.cloned.1.call-start
  621.1 111.4 %reduce-scatter.5.cloned.1.call-done = bf16[8,36864]{1,0:T(8,128)(2,1)} async-done(((bf16[128,36864]{1,0:T(8,128)(2,1)}), bf16[8,36864]{1,0:T(8,128)(2,1)}) %reduce-scatter.5.cloned.1.call-update) | async-done | bytes 589840 | tf_op jit(solution)/shard_map/reduce_scatter | solution.py:719
  732.5 0.0 all-reduce.2.cloned.1.call-update
  732.5 0.0 all-gather.2.cloned.1.call-start
  732.6 32.0 %all-reduce.2.cloned.1.call-done = bf16[8,36864]{1,0:T(8,128)(2,1)} async-done(((bf16[8,36864]{1,0:T(8,128)(2,1)}), bf16[8,36864]{1,0:T(8,128)(2,1)}) %all-reduce.2.cloned.1.call-update) | async-done | bytes 589840 | tf_op jit(solution)/shard_map/psum | solution.py:720
  764.6 0.0 all-gather.2.cloned.1.call-update
  764.7 0.8 slice_bitcast_fusion.6
  765.5 1.0 slice_bitcast_fusion.3
  766.5 0.8 slice_bitcast_fusion.5
  767.4 1.0 slice_bitcast_fusion.2
  768.4 21.8 %all-gather.2.cloned.1.call-done = bf16[32,36864]{1,0:T(8,128)(2,1)} async-done(((bf16[8,36864]{1,0:T(8,128)(2,1)}), bf16[32,36864]{1,0:T(8,128)(2,1)}) %all-gather.2.cloned.1.call-update) | async-done | bytes 2359312 | tf_op jit(solution)/shard_map/all_gather | solution.py:721
  790.2 4.9 reshape.179
  795.2 4.8 copy.43
  800.0 5.7 reshape.178
  805.7 1.7 slice-done
  807.4 2.3 reshape.177
  809.7 2.8 fusion.5
  812.6 2.7 fusion.4
  815.3 1.5 slice_bitcast_fusion
  816.7 1.6 copy.44
  818.3 1.6 copy.45
  819.9 0.8 copy.51
  820.7 0.8 copy.52
  (32 shorter events, 0.1 us)
Async XLA Ops:
  7.2 566.0 %reduce-scatter.3.cloned.1.call-start = ((), (), s32[]{:S(2)}) async-start(), calls=%async_computation.2 | async-start | bytes 5242880 | tf_op jit(solution)/shard_map/reduce_scatter | solution.py:836
  20.3 2.6 copy-start.10
  22.9 3.5 copy-start.1
  23.4 3.0 copy-start.2
  26.5 2.6 copy-start.6
  26.5 2.6 copy-start.7
  26.5 2.8 copy-start.8
  26.5 3.4 copy-start.9
  525.7 1.0 copy-start.12
  525.7 1.9 copy-start.11
  525.7 47.4 %copy-start.3 = (bf16[256,4096]{1,0:T(8,128)(2,1)S(1)}, bf16[256,4096]{1,0:T(8,128)(2,1)}, u32[]{:S(2)}) copy-start(bf16[256,4096]{1,0:T(8,128)(2,1)} %get-tuple-element.42) | copy-start | bytes 6291460
  525.8 206.7 %reduce-scatter.5.cloned.1.call-start = ((), (), s32[]{:S(2)}) async-start(), calls=%async_computation.3 | async-start | bytes 10027008 | tf_op jit(solution)/shard_map/reduce_scatter | solution.py:719
  577.5 32.3 %copy-start.16 = (bf16[32,2048]{1,0:T(8,128)(2,1)S(1)}, bf16[32,2048]{1,0:T(8,128)(2,1)}, u32[]{:S(2)}) copy-start(bf16[32,2048]{1,0:T(8,128)(2,1)} %get-tuple-element.51) | copy-start | bytes 393220
  577.5 34.7 %copy-start.15 = (bf16[32,2048]{1,0:T(8,128)(2,1)S(1)}, bf16[32,2048]{1,0:T(8,128)(2,1)}, u32[]{:S(2)}) copy-start(bf16[32,2048]{1,0:T(8,128)(2,1)} %get-tuple-element.53) | copy-start | bytes 393220
  577.5 35.4 %copy-start.14 = (bf16[32,2048]{1,0:T(8,128)(2,1)S(1)}, bf16[32,2048]{1,0:T(8,128)(2,1)}, u32[]{:S(2)}) copy-start(bf16[32,2048]{1,0:T(8,128)(2,1)} %get-tuple-element.54) | copy-start | bytes 393220
  605.0 8.5 %copy-start.13 = (bf16[32,2048]{1,0:T(8,128)(2,1)S(1)}, bf16[32,2048]{1,0:T(8,128)(2,1)}, u32[]{:S(2)}) copy-start(bf16[32,2048]{1,0:T(8,128)(2,1)} %get-tuple-element.55) | copy-start | bytes 393220
  621.0 143.7 %copy-start.4 = (bf16[384,2048]{1,0:T(8,128)(2,1)S(1)}, bf16[384,2048]{1,0:T(8,128)(2,1)}, u32[]{:S(2)}) copy-start(bf16[384,2048]{1,0:T(8,128)(2,1)} %get-tuple-element.34) | copy-start | bytes 4718596
  621.0 145.5 %copy-start.5 = (bf16[384,2048]{1,0:T(8,128)(2,1)S(1)}, bf16[384,2048]{1,0:T(8,128)(2,1)}, u32[]{:S(2)}) copy-start(bf16[384,2048]{1,0:T(8,128)(2,1)} %get-tuple-element.47) | copy-start | bytes 4718596
  621.0 143.6 %all-reduce.2.cloned.1.call-start = ((), (), s32[]{:S(2)}) async-start(), calls=%async_computation.4 | async-start | bytes 1179648 | tf_op jit(solution)/shard_map/psum | solution.py:720
  732.5 57.7 %all-gather.2.cloned.1.call-start = ((), (), s32[]{:S(2)}) async-start(), calls=%async_computation.5 | async-start | bytes 2949120 | tf_op jit(solution)/shard_map/all_gather | solution.py:721
  805.7 1.7 slice-start
  809.7 5.5 copy-start
Sparse Core Ops, SparseCore 0:
  525.9 47.2 reduce-scatter.2
  621.1 111.3 reduce-scatter.4
  734.8 29.7 all-reduce.1
  766.1 24.0 all-gather.1

commit v3 on v2

--- a/solution.py
+++ b/solution.py
@@ -55,20 +55,13 @@
     return jnp.where((row < prompt_len) == (col < RANK), product, 0.0).astype(BF)
 
 
-def spread_rows(grads, order, ids):
-    owner = jnp.repeat(jnp.stack(ids), RANK)
-    rank = jnp.arange(RANK * len(ids)) % RANK
-    hot = (order[:, None] == (owner * RANK + rank)[None, :]).astype(BF)
-    return mm(hot, grads.astype(BF)).astype(BF)
-
-
 class Gather:
-    def __init__(self, n_fs, count, src, dst, sems, lag=2, away=48):
+    def __init__(self, n_fs, sources, dst, sems, lag=2, away=48):
         (self.zs, self.zr, self.ys, self.yr, self.xs, self.xr) = sems[:6]
         (self.cs, self.cr, self.ds, self.dr, self.loc) = sems[6:]
-        self.nz, self.count, self.src, self.dst = n_fs, count, src, dst
+        self.nz, self.sources, self.dst = n_fs, sources, dst
+        self.count, self.rows = dst.shape[0], dst.shape[2]
         self.lag, self.slots, self.last = lag, 2 * lag, n_fs + 2
-        self.rows = src.shape[1]
         rep, grp = lax.axis_index("rep"), lax.axis_index("grp")
         self.z = lax.axis_index("fs")
         self.y, self.c, plane = grp // 2, grp % 2, rep % 2
@@ -116,19 +109,27 @@
         row = 1 - self.y if other else self.y
         return (row * 2 + core) * self.nz + fs
 
-    def send(self, j, shard, first, size, sems, own=False, **where):
+    def send(self, j, shard, first, size, sems, src=None, **where):
         rows = pl.ds(first, size)
         return pltpu.make_async_remote_copy(
-            self.src.at[j, rows] if own else self.dst.at[j, shard, rows],
+            self.dst.at[j, shard, rows] if src is None else src(first, size),
             self.dst.at[j, shard, rows],
             *sems,
             device_id=where,
             device_id_type=MESH,
         )
 
-    def keep(self, j, t):
+    def own_blocks(self, j):
+        start = 0
+        for count, ref in self.sources:
+            ok = (j >= start) & (j < start + count) if len(self.sources) > 1 else None
+            yield ok, functools.partial(ref, j - start)
+            start += count
+
+    def keeps(self, j, t):
         sem = self.loc.at[lax.rem(t, self.slots)]
-        return pltpu.make_async_copy(self.src.at[j], self.dst.at[j, self.own], sem)
+        for ok, src in self.own_blocks(j):
+            yield ok, pltpu.make_async_copy(src(0, self.rows), self.dst.at[j, self.own], sem)
 
     def sends(self, a, j, t):
         todo, nz, k, kz = [], self.nz, lax.rem(t, self.slots), lax.rem(t, 2 * self.slots)
@@ -137,24 +138,31 @@
         def both(left, right):
             return right if left is None else jnp.logical_and(left, right)
 
-        for ok, fs, way in self.at_distance(a):
-            shard, own = self.shard(0, fs, self.c), a == 0
+        def column(ok, fs, way, src):
+            shard = self.shard(0, fs, self.c)
             if way >= 0:
                 sems = (self.zs.at[kz, 0, fs], self.zr.at[kz, fs])
-                up = self.send(j, shard, *inner, sems, own, fs=self.z + 1)
+                up = self.send(j, shard, *inner, sems, src, fs=self.z + 1)
                 todo.append((both(ok, self.z < nz - 1), up))
             if way <= 0:
                 sems = (self.zs.at[kz, 1, fs], self.zr.at[kz, fs])
-                down = self.send(j, shard, *inner, sems, own, fs=self.z - 1)
+                down = self.send(j, shard, *inner, sems, src, fs=self.z - 1)
                 todo.append((both(ok, self.z > 0), down))
             sems = (self.ys.at[k, fs], self.yr.at[k, fs])
-            todo.append((ok, self.send(j, shard, *inner, sems, own, grp=self.far_row)))
-            if not own:
+            todo.append((ok, self.send(j, shard, *inner, sems, src, grp=self.far_row)))
+            if way:
                 sems = (self.xs.at[k, fs], self.xr.at[k, fs])
                 todo.append((ok, self.send(j, shard, *outer, sems, rep=self.far_rep)))
             sems = (self.cs.at[k, fs], self.cr.at[k, fs])
-            size = (0, self.rows) if own else inner
-            todo.append((ok, self.send(j, shard, *size, sems, own, grp=self.far_core)))
+            size = inner if way else (0, self.rows)
+            todo.append((ok, self.send(j, shard, *size, sems, src, grp=self.far_core)))
+
+        if a == 0:
+            for ok, src in self.own_blocks(j):
+                column(ok, self.z, 0, src)
+        else:
+            for ok, fs, way in self.at_distance(a):
+                column(ok, fs, way, None)
         for ok, fs, _ in self.at_distance(a - 1):
             shard = self.shard(1, fs, self.c)
             sems = (self.xs.at[k, nz + fs], self.xr.at[k, nz + fs])
@@ -212,13 +220,15 @@
             for ok, copy in self.arrivals(a, j, t):
                 act(ok, copy.wait)
             if a == 1:
-                self.keep(j, t).wait()
+                for ok, copy in self.keeps(j, t):
+                    act(ok, copy.wait)
 
         def begin(a, j, t):
             for ok, copy in self.sends(a, j, t):
                 act(ok, copy.start)
             if a == 0:
-                self.keep(j, t).start()
+                for ok, copy in self.keeps(j, t):
+                    act(ok, copy.start)
 
         def tick(t, carry):
             for a in range(self.last, 0, -1):
@@ -273,15 +283,57 @@
     return (q_p, q_c, k_p, k_c, v_p, v_c), (c_p, e_1 * inv, e_2 * inv)
 
 
-def project_call(x, gain, bias, ids, a_tab, b_tab, blocks, n_fs, n_shard, prompt_len):
-    count, shard_rows, _ = blocks.shape
-    rows, width = x.shape
+def columns_of(ref):
+    return lambda j, first, size: ref.at[
+        pl.ds(first, size), pl.ds(pl.multiple_of(j * BLOCK, BLOCK), BLOCK)
+    ]
+
+
+def tiles_of(ref, shard_rows, parts):
+    def tile(j, first, size):
+        row = pl.multiple_of(lax.rem(j, parts) * shard_rows + first, 8)
+        return ref.at[pl.ds(row, size), pl.ds(pl.multiple_of(j // parts * BLOCK, BLOCK), BLOCK)]
+
+    return tile
+
+
+def select_call(ids, tables):
+    def kernel(ids, *refs):
+        for src, dst in zip(refs[: len(tables)], refs[len(tables) :]):
+            dst[...] = src[0]
+
+    def spec_in(t):
+        return pl.BlockSpec((1,) + t.shape[1:], lambda i, ids: (ids[i],) + (0,) * (t.ndim - 1))
+
+    def spec_out(t):
+        lead = t.ndim - 3
+        return pl.BlockSpec(t.shape[1:], lambda i, ids: (0,) * lead + (i, 0))
+
+    return pl.pallas_call(
+        kernel,
+        grid_spec=pltpu.PrefetchScalarGridSpec(
+            num_scalar_prefetch=1,
+            grid=(2,),
+            in_specs=[spec_in(t) for t in tables],
+            out_specs=[spec_out(t) for t in tables],
+        ),
+        out_shape=[
+            jax.ShapeDtypeStruct(t.shape[1:-2] + (2 * RANK, t.shape[-1]), BF) for t in tables
+        ],
+        name="select",
+    )(ids, *tables)
+
+
+def project_call(x_p, x_c, gain, bias, a_ext, b_ext, weight, n_fs, n_shard):
+    prompt_len, width = x_p.shape
+    rows = prompt_len + x_c.shape[0]
+    shard_rows, count = weight.shape[0], weight.shape[1] // BLOCK
     per = width // BLOCK
 
     def kernel(
-        x, gain, bias, ids, a_tab, b_tab, src, dst, qkv, normed, lows, a_ext, b_ext, wbuf, wsem, *sems
+        x_p, x_c, gain, bias, a_ext, b_ext, src, dst, qkv, normed, lows, wbuf, wsem, *sems
     ):
-        engine = Gather(n_fs, count, src, dst, sems)
+        engine = Gather(n_fs, [(count, columns_of(src))], dst, sems)
         engine.barrier()
 
         def load(j):
@@ -290,13 +342,9 @@
         def early(t):
             @pl.when(t == 0)
             def _():
-                for i in range(2):
-                    part = slice(i * RANK, (i + 1) * RANK)
-                    for n in range(3):
-                        a_ext[n, part] = a_tab[ids[i], n]
-                        b_ext[n, part] = b_tab[ids[i], n]
-                hat, _ = norm_stats(x[...].astype(F32))
-                normed[...] = (hat * gain[...] + bias[...]).astype(BF)
+                for x, part in ((x_p, slice(0, prompt_len)), (x_c, slice(prompt_len, None))):
+                    hat, _ = norm_stats(x[...].astype(F32))
+                    normed[part] = (hat * gain[...] + bias[...]).astype(BF)
                 for n in range(3):
                     lows[n] = low_of(mm_nt(normed[...], a_ext[n]), prompt_len)
 
@@ -326,11 +374,9 @@
             jax.ShapeDtypeStruct((rows, width), BF),
             jax.ShapeDtypeStruct((3, rows, 2 * RANK), BF),
         ],
-        in_specs=[WHOLE, WHOLE, WHOLE, SCALARS, WHOLE, WHOLE, ANY],
+        in_specs=[WHOLE] * 6 + [ANY],
         out_specs=[ANY, WHOLE, WHOLE, WHOLE],
         scratch_shapes=[
-            pltpu.VMEM((3, 2 * RANK, width), BF),
-            pltpu.VMEM((3, 2 * RANK, width), BF),
             pltpu.VMEM((2, n_shard, shard_rows, BLOCK), BF),
             pltpu.SemaphoreType.DMA((2,)),
         ]
@@ -339,39 +385,36 @@
             collective_id=0, has_side_effects=True, vmem_limit_bytes=ROOM
         ),
         name="project",
-    )(x, gain, bias, ids, a_tab, b_tab, blocks)
-
-
-def middle_call(x, cot, qkv, gain, bias, ids, tables, blocks, counts, n_fs, n_shard, prompt_len):
-    rows, width = x.shape
-    shard_rows = blocks.shape[1]
-    n_out, n_dn, n_up = counts
+    )(x_p, x_c, gain, bias, a_ext, b_ext, weight)
+
+
+def middle_call(x_p, x_c, cot_p, cot_c, qkv, gain, bias, tables, weights, n_fs, n_shard):
+    prompt_len, width = x_p.shape
+    rows = prompt_len + x_c.shape[0]
+    shard_rows, hidden = weights[2].shape
+    parts = weights[1].shape[0] // shard_rows
+    n_out, n_up = width // BLOCK, hidden // BLOCK
+    n_dn = n_out * parts
     count = n_out + n_dn + n_up
-    hidden = n_up * BLOCK
     n_grp = n_shard // n_fs
-    parts = n_dn // n_out
     heads = width // HDIM
     go, first_head = 4, 5
     first_out = first_head + heads
     a_o, b_o, a_u, b_u, a_d, b_d = range(6)
 
-    def kernel(
-        x,
-        cot,
-        qkv,
-        gain,
-        bias,
-        ids,
-        *refs,
-    ):
-        tabs, refs = refs[:6], refs[6:]
-        src, refs = refs[0], refs[1:]
-        (dst, kp, mixed, normed, result, resid_back, grad_attn), refs = refs[:7], refs[7:]
+    def kernel(x_p, x_c, cot_p, cot_c, qkv, gain, bias, *refs):
+        ext, src, refs = refs[:6], refs[6:9], refs[9:]
+        (dst, kp, mixed, normed, res_p, res_c, resid_back, grad_attn), refs = refs[:8], refs[8:]
         (low_o, g_a_up, g_b_up, g_a_dn, g_b_dn), refs = refs[:5], refs[5:]
-        ext, refs = refs[:6], refs[6:]
-        (resid, out_acc, low_up, dlow_dn, low_dn, dlow_up), refs = refs[:6], refs[6:]
-        (wbuf, dbuf, wsem, dsem, ksend, krecv, kloc), sems = refs[:7], refs[7:]
-        engine = Gather(n_fs, count, src, dst, sems)
+        (cot, resid, out_acc, low_up, dlow_dn, low_dn, dlow_up), refs = refs[:7], refs[7:]
+        (wbuf, dbuf, wsem, dsem, ksend, krecv), sems = refs[:6], refs[6:]
+        own, rest = slice(0, prompt_len), slice(prompt_len, None)
+        sources = [
+            (n_out, columns_of(src[0])),
+            (n_dn, tiles_of(src[1], shard_rows, parts)),
+            (n_up, columns_of(src[2])),
+        ]
+        engine = Gather(n_fs, sources, dst, sems)
         engine.barrier()
         grp = lax.axis_index("grp")
 
@@ -402,9 +445,8 @@
                 kp[grp] = qkv[:prompt_len, width:]
                 to_row.start()
                 to_core.start()
-                for n, tab in enumerate(tabs):
-                    for i in range(2):
-                        ext[n][i * RANK : (i + 1) * RANK] = tab[ids[i]]
+                cot[own] = cot_p[...]
+                cot[rest] = cot_c[...]
                 dlow_dn[...] = low_of(mm_nt(cot[...], ext[b_d][...]), prompt_len)
 
             @pl.when(t == go)
@@ -453,7 +495,8 @@
                 cols = pl.ds(pl.multiple_of(b * BLOCK, BLOCK), BLOCK)
                 w = wbuf[lax.rem(b, 2)].reshape(-1, BLOCK)
                 branch = mm(mixed[...], w) + mm(low_o[...], ext[b_o][:, cols])
-                resid[:, cols] = x[:, cols].astype(F32) + branch
+                resid[own, cols] = x_p[:, cols].astype(F32) + branch[own]
+                resid[rest, cols] = x_c[:, cols].astype(F32) + branch[rest]
 
             @pl.when(t == first_out + n_out)
             def _():
@@ -507,7 +550,9 @@
 
         engine.run(early, compute)
         low = low_of(low_dn[...], prompt_len)
-        result[...] = (out_acc[...] + mm(low, ext[b_d][...])).astype(BF)
+        result = (out_acc[...] + mm(low, ext[b_d][...])).astype(BF)
+        res_p[...] = result[own]
+        res_c[...] = result[rest]
         g_b_dn[...] = mm_tn(low, cot[...]).astype(BF)
         dlow = low_of(dlow_up[...], prompt_len)
         g_a_up[...] = mm_tn(dlow, normed[...]).astype(BF)
@@ -525,7 +570,8 @@
             like((n_grp, prompt_len, 2 * width), BF),
             like((rows, width), BF),
             like((rows, width), BF),
-            like((rows, width), BF),
+            like(x_p.shape, BF),
+            like(x_c.shape, BF),
             like((rows, width), F32),
             like((rows, width), BF),
             like((rows, two), BF),
@@ -534,12 +580,10 @@
             like((two, hidden), BF),
             like((two, width), BF),
         ],
-        in_specs=[WHOLE] * 5 + [SCALARS] + [WHOLE] * 6 + [ANY],
-        out_specs=[ANY] + [WHOLE] * 11,
+        in_specs=[WHOLE] * 13 + [ANY] * 3,
+        out_specs=[ANY] + [WHOLE] * 12,
         scratch_shapes=[
-            pltpu.VMEM((two, w), BF) for w in (width, width, width, hidden, hidden, width)
-        ]
-        + [
+            pltpu.VMEM((rows, width), BF),
             pltpu.VMEM((rows, width), F32),
             pltpu.VMEM((rows, width), F32),
             pltpu.VMEM((rows, two), BF),
@@ -552,57 +596,259 @@
             pltpu.SemaphoreType.DMA((2,)),
             pltpu.SemaphoreType.DMA((3,)),
             pltpu.SemaphoreType.DMA((3,)),
-            pltpu.SemaphoreType.DMA((1,)),
         ]
         + Gather.semaphores(n_fs),
         compiler_params=pltpu.CompilerParams(
             collective_id=1, has_side_effects=True, vmem_limit_bytes=ROOM
         ),
         name="middle",
-    )(x, cot, qkv, gain, bias, ids, *tables, blocks)
-
-
-def attention_back_call(grad_attn, mixed, low_o, qkv, kp, ids, a_tab, b_tab, w_out, n_out, prompt_len):
+    )(x_p, x_c, cot_p, cot_c, qkv, gain, bias, *tables, *weights)
+
+
+PIECES = 8
+
+
+class TableSum:
+    def __init__(self, n_fs, hots, units, bufs, sems):
+        self.n_fs, self.hots, self.units = n_fs, hots, units
+        self.out, self.got, self.dense, self.parts, self.sums = bufs
+        (self.s1, self.r1, self.s2, self.r2, self.s3, self.r3) = sems
+        rep, self.grp = lax.axis_index("rep"), lax.axis_index("grp")
+        self.z = lax.axis_index("fs")
+        plane = rep % 2
+        y, c = self.grp // 2, self.grp % 2
+        self.me = plane * 4 + self.grp
+        self.peers = []
+        for q in range(1, PIECES):
+            x_to = 1 - plane if q // 4 else plane
+            y_to = 1 - y if q // 2 % 2 else y
+            c_to = 1 - c if q % 2 else c
+            where = {"grp": y_to * 2 + c_to}
+            if q // 4:
+                where["rep"] = rep + 1 - 2 * plane
+            self.peers.append((q, x_to * 4 + y_to * 2 + c_to, where))
+        self.piece = self.out.shape[2] // units
+
+    @staticmethod
+    def scratch(n_fs, units, piece, count):
+        two, wide = 2 * RANK, units * piece
+        rows = count * RANK // n_fs
+        bufs = [
+            pltpu.VMEM((PIECES, two, wide), BF),
+            pltpu.VMEM((PIECES, two, wide), BF),
+            pltpu.VMEM((n_fs, rows, wide), BF),
+            pltpu.VMEM((n_fs, rows, wide), BF),
+            pltpu.VMEM((PIECES, rows, wide), BF),
+        ]
+        dma = pltpu.SemaphoreType.DMA
+        return bufs, [dma((PIECES,))] * 2 + [dma((n_fs,))] * 2 + [dma((PIECES,))] * 2
+
+    def pack(self, unit, value, first=0):
+        value = value.astype(BF)
+        cols = slice(unit * self.piece, (unit + 1) * self.piece)
+        for n in range(value.shape[1] // self.piece):
+            self.out[first + n, :, cols] = value[:, n * self.piece : (n + 1) * self.piece]
+
+    def exchange(self):
+        return [
+            pltpu.make_async_remote_copy(
+                self.out.at[to],
+                self.got.at[self.me],
+                self.s1.at[q],
+                self.r1.at[q],
+                device_id=where,
+                device_id_type=MESH,
+            )
+            for q, to, where in self.peers
+        ]
+
+    def along_fs(self):
+        copies = []
+        for d in range(1, self.n_fs):
+            to = lax.rem(self.z + d, self.n_fs)
+            copies.append(
+                pltpu.make_async_remote_copy(
+                    self.dense.at[to],
+                    self.parts.at[self.z],
+                    self.s2.at[d],
+                    self.r2.at[d],
+                    device_id={"fs": to},
+                    device_id_type=MESH,
+                )
+            )
+        return copies
+
+    def hand_out(self):
+        return [
+            pltpu.make_async_remote_copy(
+                self.sums.at[self.me],
+                self.sums.at[self.me],
+                self.s3.at[q],
+                self.r3.at[q],
+                device_id=where,
+                device_id_type=MESH,
+            )
+            for q, _, where in self.peers
+        ]
+
+    def first(self):
+        for copy in self.exchange():
+            copy.start()
+        self.got[self.me] = self.out[self.me]
+
+    def second(self):
+        for q, whose, _ in self.peers:
+            ref = self.got.at[whose]
+            pltpu.make_async_copy(ref, ref, self.r1.at[q]).wait()
+        for copy in self.exchange():
+            copy.wait_send()
+        wide = self.out.shape[2]
+        hots = self.hots[...].reshape(PIECES * 2 * RANK, -1)
+        dense = mm_tn(hots, self.got[...].reshape(PIECES * 2 * RANK, wide))
+        self.dense[...] = dense.astype(BF).reshape(self.dense.shape)
+        for copy in self.along_fs():
+            copy.start()
+        self.parts[self.z] = self.dense[self.z]
+
+    def third(self):
+        for d in range(1, self.n_fs):
+            ref = self.parts.at[lax.rem(self.z + self.n_fs - d, self.n_fs)]
+            pltpu.make_async_copy(ref, ref, self.r2.at[d]).wait()
+        for copy in self.along_fs():
+            copy.wait_send()
+        total = self.parts[0].astype(F32)
+        for n in range(1, self.n_fs):
+            total = total + self.parts[n].astype(F32)
+        self.sums[self.me] = total.astype(BF)
+        for copy in self.hand_out():
+            copy.start()
+
+    def last(self, places):
+        for q, whose, _ in self.peers:
+            ref = self.sums.at[whose]
+            pltpu.make_async_copy(ref, ref, self.r3.at[q]).wait()
+        for copy in self.hand_out():
+            copy.wait_send()
+        for unit, place in enumerate(places):
+            for k in range(PIECES):
+                cols = slice(unit * self.piece, (unit + 1) * self.piece)
+                for a in range(self.sums.shape[1] // RANK):
+                    value = self.sums[k, a * RANK : (a + 1) * RANK, cols]
+                    place(a, k * self.piece, value)
+
+
+def back_call(
+    grad_attn, mixed, low_o, lows, gain, a_ext, b_ext, hot, mid, qkv, kp, x_p, x_c, normed, grad_resid, w_rest, w_qkv, n_fs, count
+):
     rows, width = grad_attn.shape
+    prompt_len, cont_len = x_p.shape[0], x_c.shape[0]
     heads = width // HDIM
-    total = kp.shape[0] * prompt_len
-    n_shard, shard_rows = w_out.shape[1:3]
-
-    def kernel(
-        grad_attn, mixed, low_o, qkv, kp, ids, a_tab, b_tab, w, g_q, g_own, g_far, g_a, g_b, a_ext, b_ext, dlow, acc, gm
-    ):
-        step = pl.program_id(0)
-
-        @pl.when(step == 0)
-        def _():
-            for i in range(2):
-                part = slice(i * RANK, (i + 1) * RANK)
-                a_ext[part] = a_tab[ids[i]]
-                b_ext[part] = b_tab[ids[i]]
-            dlow[...] = low_of(mm_nt(grad_attn[...], b_ext[...]), prompt_len)
-            acc[...] = mm(dlow[...], a_ext[...])
-            g_a[...] = mm_tn(dlow[...], mixed[...]).astype(BF)
-            g_b[...] = mm_tn(low_o[...], grad_attn[...]).astype(BF)
-
-        @pl.when(step < n_out)
-        def _():
-            cols = pl.ds(pl.multiple_of(step * BLOCK, BLOCK), BLOCK)
-            acc[...] += mm_nt(grad_attn[:, cols], w[0].reshape(-1, BLOCK))
-
-        @pl.when(step == n_out - 1)
-        def _():
-            gm[...] = acc[...].astype(BF)
-
-        @pl.when(step >= n_out)
-        def _():
-            h = step - n_out
-            first = lax.axis_index("grp") * prompt_len
+    n_grp = kp.shape[0]
+    n_shard, shard_rows = w_qkv.shape[1:3]
+    per = width // BLOCK
+    n_qkv = w_qkv.shape[0]
+    hidden = mid[1].shape[1]
+    adapters = count // n_fs
+    half_heads = heads // 2
+    half = half_heads * HDIM
+    two = 2 * RANK
+    wide_units = hidden // width
+    first_units = 2 * wide_units + 4
+    last_units = 6
+    piece = width // PIECES
+
+    def kernel(*refs):
+        (grad_attn, mixed, low_o, lows, gain, a_ext, b_ext, hot), refs = refs[:8], refs[8:]
+        (g_a_up, g_b_up, g_a_dn, g_b_dn), refs = refs[:4], refs[4:]
+        (qkv, kp, x_p, x_c, normed, grad_resid, w_rest, w_qkv), refs = refs[:8], refs[8:]
+        (out_p, out_c, t_a, t_b, t_a_up, t_b_up, t_a_dn, t_b_dn), refs = refs[:8], refs[8:]
+        (grads, keep, late, x, normed_here, wbuf, gm, acc, dlow, dlow_o), refs = refs[:10], refs[10:]
+        (far, far_core, far_row, hots), refs = refs[:4], refs[4:]
+        bufs_one, bufs_two, refs = refs[:5], refs[5:10], refs[10:]
+        sems_one, sems_two, refs = refs[:6], refs[6:12], refs[12:]
+        lsem, wsem, csend, crecv, rsend, rrecv, hsend, hrecv = refs
+        grp = lax.axis_index("grp")
+        y, c = grp // 2, grp % 2
+        own, rest = slice(0, prompt_len), slice(prompt_len, None)
+        one = TableSum(n_fs, hots, first_units, bufs_one, sems_one)
+        two_ = TableSum(n_fs, hots, last_units, bufs_two, sems_two)
+        barrier = pltpu.get_barrier_semaphore()
+        for _, _, where in one.peers:
+            pl.semaphore_signal(barrier, 1, device_id=where, device_id_type=MESH)
+        for d in range(1, n_fs):
+            to = lax.rem(one.z + d, n_fs)
+            pl.semaphore_signal(barrier, 1, device_id={"fs": to}, device_id_type=MESH)
+
+        loads = [
+            pltpu.make_async_copy(src, dst, lsem.at[n])
+            for n, (src, dst) in enumerate(
+                [
+                    (qkv, grads),
+                    (kp, keep),
+                    (grad_resid, late),
+                    (normed, normed_here),
+                    (x_p, x.at[pl.ds(0, prompt_len)]),
+                    (x_c, x.at[pl.ds(prompt_len, cont_len)]),
+                ]
+            )
+        ]
+        for copy in loads:
+            copy.start()
+
+        def load_w(ref, i, k):
+            return pltpu.make_async_copy(ref.at[i], wbuf.at[k], wsem.at[k])
+
+        load_w(w_rest, 0, 0).start()
+        pl.semaphore_wait(barrier, len(one.peers) + n_fs - 1)
+
+        hots[one.me] = hot[...]
+        hot_sends = [
+            pltpu.make_async_remote_copy(
+                hots.at[one.me],
+                hots.at[one.me],
+                hsend.at[q],
+                hrecv.at[q],
+                device_id=where,
+                device_id_type=MESH,
+            )
+            for q, _, where in one.peers
+        ]
+        for copy in hot_sends:
+            copy.start()
+        for n in range(wide_units):
+            one.pack(n, g_b_up[:, n * width : (n + 1) * width])
+            one.pack(wide_units + n, g_a_dn[:, n * width : (n + 1) * width])
+        one.pack(2 * wide_units, g_a_up[...])
+        one.pack(2 * wide_units + 1, g_b_dn[...])
+        dlow_o[...] = low_of(mm_nt(grad_attn[...], b_ext[3]), prompt_len)
+        one.pack(2 * wide_units + 2, mm_tn(dlow_o[...], mixed[...]))
+        one.pack(2 * wide_units + 3, mm_tn(low_o[...], grad_attn[...]))
+        one.first()
+
+        acc[...] = mm(dlow_o[...], a_ext[3])
+        for n in range(per):
+            load_w(w_rest, n, n % 2).wait()
+            if n + 1 < per:
+                load_w(w_rest, n + 1, (n + 1) % 2).start()
+            w = wbuf[n % 2].reshape(-1, BLOCK)
+            acc[...] += mm_nt(grad_attn[:, n * BLOCK : (n + 1) * BLOCK], w)
+        gm[...] = acc[...].astype(BF)
+        load_w(w_qkv, 0, 0).start()
+        load_w(w_qkv, 1, 1).start()
+
+        loads[0].wait()
+        loads[1].wait()
+
+        def head(part, n, carry):
+            h = part * half_heads + n
+            first = grp * prompt_len
             (q_p, q_c, k_p, k_c, v_p, v_c), (c_p, c_1, c_2) = head_chances(
-                qkv, kp, h, prompt_len, width, first
+                grads, keep, h, prompt_len, width, first
             )
-            lanes = pl.ds(pl.multiple_of(h * HDIM, HDIM), HDIM)
-            far = pl.ds(pl.multiple_of(width + h * HDIM, HDIM), HDIM)
-            gm_p, gm_c = gm[:prompt_len, lanes], gm[prompt_len:, lanes]
+            lanes = [
+                pl.ds(pl.multiple_of(i * width + h * HDIM, HDIM), HDIM) for i in range(3)
+            ]
+            gm_p, gm_c = gm[own, lanes[0]], gm[rest, lanes[0]]
             d_p = mm_nt(gm_p, v_p)
             d_1, d_2 = mm_nt(gm_c, v_p), mm_nt(gm_c, v_c)
             s_p = (c_p * (d_p - jnp.sum(c_p * d_p, axis=-1, keepdims=True))).astype(BF)
@@ -611,116 +857,191 @@
             )
             s_1 = (c_1 * (d_1 - inner)).astype(BF)
             s_2 = (c_2 * (d_2 - inner)).astype(BF)
-            g_q[:prompt_len, lanes] = (mm(s_p, k_p) * SCALE).astype(BF)
-            g_q[prompt_len:, lanes] = ((mm(s_1, k_p) + mm(s_2, k_c)) * SCALE).astype(BF)
-            g_own[:, lanes] = (mm_tn(s_2, q_c) * SCALE).astype(BF)
-            g_own[:, far] = mm_tn(c_2.astype(BF), gm_c).astype(BF)
-            g_far[:, lanes] = ((mm_tn(s_p, q_p) + mm_tn(s_1, q_c)) * SCALE).astype(BF)
-            g_far[:, far] = (mm_tn(c_p.astype(BF), gm_p) + mm_tn(c_1.astype(BF), gm_c)).astype(BF)
+            grads[own, lanes[0]] = (mm(s_p, k_p) * SCALE).astype(BF)
+            grads[rest, lanes[0]] = ((mm(s_1, k_p) + mm(s_2, k_c)) * SCALE).astype(BF)
+            grads[rest, lanes[1]] = (mm_tn(s_2, q_c) * SCALE).astype(BF)
+            grads[rest, lanes[2]] = mm_tn(c_2.astype(BF), gm_c).astype(BF)
+            g_k = ((mm_tn(s_p, q_p) + mm_tn(s_1, q_c)) * SCALE).astype(BF)
+            g_v = (mm_tn(c_p.astype(BF), gm_p) + mm_tn(c_1.astype(BF), gm_c)).astype(BF)
+            into = [pl.ds(pl.multiple_of(i * half + n * HDIM, HDIM), HDIM) for i in range(2)]
+            far[part, :, :, into[0]] = g_k.reshape(n_grp, prompt_len, HDIM)
+            far[part, :, :, into[1]] = g_v.reshape(n_grp, prompt_len, HDIM)
+            return carry
+
+        def to_core(part):
+            return [
+                pltpu.make_async_remote_copy(
+                    far.at[part, row * 2 + 1 - c],
+                    far_core.at[part, row],
+                    csend.at[part, row],
+                    crecv.at[part, row],
+                    device_id={"grp": y * 2 + 1 - c},
+                    device_id_type=MESH,
+                )
+                for row in range(2)
+            ]
+
+        def to_row(part):
+            return pltpu.make_async_remote_copy(
+                far.at[part, (1 - y) * 2 + c],
+                far_row.at[part],
+                rsend.at[part],
+                rrecv.at[part],
+                device_id={"grp": (1 - y) * 2 + c},
+                device_id_type=MESH,
+            )
+
+        def add_core(part):
+            for copy in to_core(part):
+                copy.wait()
+            for row in range(2):
+                total = far[part, row * 2 + c].astype(F32) + far_core[part, row].astype(F32)
+                far[part, row * 2 + c] = total.astype(BF)
+            to_row(part).start()
+
+        def add_row(part):
+            to_row(part).wait()
+            total = far[part, grp].astype(F32) + far_row[part].astype(F32)
+            total = total.astype(BF)
+            for i in range(2):
+                cols = slice((i + 1) * width + part * half, (i + 1) * width + (part + 1) * half)
+                grads[own, cols] = total[:, i * half : (i + 1) * half]
+
+        lax.fori_loop(0, half_heads, functools.partial(head, 0), 0)
+        for copy in to_core(0):
+            copy.start()
+        for copy in hot_sends:
+            copy.wait_send()
+        for q, whose, _ in one.peers:
+            pltpu.make_async_copy(hots.at[whose], hots.at[whose], hrecv.at[q]).wait()
+        one.second()
+        lax.fori_loop(0, half_heads // 2, functools.partial(head, 1), 0)
+        add_core(0)
+        lax.fori_loop(half_heads // 2, half_heads, functools.partial(head, 1), 0)
+        for copy in to_core(1):
+            copy.start()
+        one.third()
+
+        acc[...] = jnp.zeros_like(acc)
+        dlow[...] = jnp.zeros_like(dlow)
+
+        def project(i, m, carry):
+            n = i * per + m
+            k = lax.rem(n, 2)
+            load_w(w_qkv, n, k).wait()
+            part = grads[:, pl.ds(pl.multiple_of(n * BLOCK, BLOCK), BLOCK)]
+            acc[...] += mm_nt(part, wbuf[k].reshape(-1, BLOCK))
+            dlow[i] += mm_nt(part, b_ext[i, :, pl.ds(pl.multiple_of(m * BLOCK, BLOCK), BLOCK)])
+            two_.pack(3 + i, mm_tn(lows[i], part), m * (BLOCK // piece))
+
+            @pl.when(n + 2 < n_qkv)
+            def _():
+                load_w(w_qkv, n + 2, k).start()
+
+            return carry
+
+        lax.fori_loop(0, 1, functools.partial(project, 0), 0)
+        add_core(1)
+        lax.fori_loop(1, per, functools.partial(project, 0), 0)
+        add_row(0)
+        add_row(1)
+        for i in (1, 2):
+            lax.fori_loop(0, per, functools.partial(project, i), 0)
+
+        for copy in loads[2:]:
+            copy.wait()
+        for i in range(3):
+            low = low_of(dlow[i], prompt_len)
+            acc[...] += mm(low, a_ext[i])
+            two_.pack(i, mm_tn(low, normed_here[...]))
+        two_.first()
+        back = late[...] + norm_back(x[...].astype(F32), gain[...], acc[...])
+        back = back.astype(BF)
+        out_p[...] = back[own]
+        out_c[...] = back[rest]
+
+        def whole(ref, first):
+            def place(a, col, value):
+                ref[a, :, first + col : first + col + piece] = value
+
+            return place
+
+        def one_map(ref, n):
+            def place(a, col, value):
+                ref[a, n, :, col : col + piece] = value
+
+            return place
+
+        one.last(
+            [whole(t_b_up, n * width) for n in range(wide_units)]
+            + [whole(t_a_dn, n * width) for n in range(wide_units)]
+            + [whole(t_a_up, 0), whole(t_b_dn, 0), one_map(t_a, 3), one_map(t_b, 3)]
+        )
+        two_.second()
+        two_.third()
+        two_.last([one_map(t_a, n) for n in range(3)] + [one_map(t_b, n) for n in range(3)])
 
     like = jax.ShapeDtypeStruct
-    two = 2 * RANK
+    bufs_one, sems_one = TableSum.scratch(n_fs, first_units, piece, count)
+    bufs_two, sems_two = TableSum.scratch(n_fs, last_units, piece, count)
+    dma = pltpu.SemaphoreType.DMA
     return pl.pallas_call(
         kernel,
-        grid=(n_out + heads,),
         out_shape=[
-            like((rows, width), BF),
-            like((rows - prompt_len, 2 * width), BF),
-            like((total, 2 * width), BF),
-            like((two, width), BF),
-            like((two, width), BF),
+            like(x_p.shape, BF),
+            like(x_c.shape, BF),
+            like((adapters, 4, RANK, width), BF),
+            like((adapters, 4, RANK, width), BF),
+            like((adapters, RANK, width), BF),
+            like((adapters, RANK, hidden), BF),
+            like((adapters, RANK, hidden), BF),
+            like((adapters, RANK, width), BF),
         ],
-        in_specs=[WHOLE] * 5
-        + [SCALARS, WHOLE, WHOLE]
-        + [
-            pl.BlockSpec(
-                (1, n_shard, shard_rows, BLOCK), lambda i: (jnp.minimum(i, n_out - 1), 0, 0, 0)
-            )
-        ],
-        out_specs=[WHOLE] * 5,
+        in_specs=[WHOLE] * 12 + [ANY] * 8,
+        out_specs=[WHOLE] * 8,
         scratch_shapes=[
-            pltpu.VMEM((two, width), BF),
-            pltpu.VMEM((two, width), BF),
-            pltpu.VMEM((rows, two), BF),
+            pltpu.VMEM((rows, 3 * width), BF),
+            pltpu.VMEM(kp.shape, BF),
             pltpu.VMEM((rows, width), F32),
             pltpu.VMEM((rows, width), BF),
-        ],
-        compiler_params=pltpu.CompilerParams(vmem_limit_bytes=ROOM),
-        name="attention_back",
-    )(grad_attn, mixed, low_o, qkv, kp, ids, a_tab, b_tab, w_out)
-
-
-def project_back_call(grads, x, normed, lows, grad_resid, gain, ids, a_tab, b_tab, w_qkv, prompt_len):
-    rows, width = x.shape
-    count, n_shard, shard_rows, _ = w_qkv.shape
-    per = width // BLOCK
-
-    def kernel(
-        grads, x, normed, lows, grad_resid, gain, ids, a_tab, b_tab, w, out, g_a, g_b, a_ext, b_ext, dlow, acc
-    ):
-        j = pl.program_id(0)
-        n = j // per
-
-        @pl.when(j == 0)
-        def _():
-            for i in range(2):
-                part = slice(i * RANK, (i + 1) * RANK)
-                for m in range(3):
-                    a_ext[m, part] = a_tab[ids[i], m]
-                    b_ext[m, part] = b_tab[ids[i], m]
-            acc[...] = jnp.zeros_like(acc)
-            dlow[...] = jnp.zeros_like(dlow)
-
-        inside = pl.ds(pl.multiple_of(lax.rem(j, per) * BLOCK, BLOCK), BLOCK)
-        part = grads[...]
-        acc[...] += mm_nt(part, w[0].reshape(-1, BLOCK))
-        dlow[n] += mm_nt(part, b_ext[n, :, inside])
-        g_b[...] = mm_tn(lows[n], part).astype(BF)
-
-        @pl.when(j == count - 1)
-        def _():
-            for m in range(3):
-                low = low_of(dlow[m], prompt_len)
-                acc[...] += mm(low, a_ext[m])
-                g_a[m] = mm_tn(low, normed[...]).astype(BF)
-            back = norm_back(x[...].astype(F32), gain[...], acc[...])
-            out[...] = (grad_resid[...] + back).astype(BF)
-
-    like = jax.ShapeDtypeStruct
-    two = 2 * RANK
-    return pl.pallas_call(
-        kernel,
-        grid=(count,),
-        out_shape=[like((rows, width), BF), like((3, two, width), BF), like((two, 3 * width), BF)],
-        in_specs=[pl.BlockSpec((rows, BLOCK), lambda j: (0, j))]
-        + [WHOLE] * 5
-        + [SCALARS, WHOLE, WHOLE]
-        + [pl.BlockSpec((1, n_shard, shard_rows, BLOCK), lambda j: (j, 0, 0, 0))],
-        out_specs=[WHOLE, WHOLE, pl.BlockSpec((two, BLOCK), lambda j: (0, j))],
-        scratch_shapes=[
-            pltpu.VMEM((3, two, width), BF),
-            pltpu.VMEM((3, two, width), BF),
+            pltpu.VMEM((rows, width), BF),
+            pltpu.VMEM((2, n_shard, shard_rows, BLOCK), BF),
+            pltpu.VMEM((rows, width), BF),
+            pltpu.VMEM((rows, width), F32),
             pltpu.VMEM((3, rows, two), F32),
-            pltpu.VMEM((rows, width), F32),
-        ],
-        compiler_params=pltpu.CompilerParams(vmem_limit_bytes=ROOM),
-        name="project_back",
-    )(grads, x, normed, lows, grad_resid, gain, ids, a_tab, b_tab, w_qkv)
+            pltpu.VMEM((rows, two), BF),
+            pltpu.VMEM((2, n_grp, prompt_len, 2 * half), BF),
+            pltpu.VMEM((2, 2, prompt_len, 2 * half), BF),
+            pltpu.VMEM((2, prompt_len, 2 * half), BF),
+            pltpu.VMEM((PIECES,) + hot.shape, BF),
+        ]
+        + bufs_one
+        + bufs_two
+        + sems_one
+        + sems_two
+        + [dma((6,)), dma((2,)), dma((2, 2)), dma((2, 2)), dma((2,)), dma((2,))]
+        + [dma((PIECES,)), dma((PIECES,))],
+        compiler_params=pltpu.CompilerParams(
+            collective_id=2, has_side_effects=True, vmem_limit_bytes=ROOM
+        ),
+        name="back",
+    )(
+        grad_attn, mixed, low_o, lows, gain, a_ext, b_ext, hot, *mid,
+        qkv, kp, x_p, x_c, normed, grad_resid, w_rest, w_qkv,
+    )
 
 
 def make_body(sizes):
     n_rep, n_grp, n_fs = sizes
     n_shard = n_grp * n_fs
 
-    def reduce_tables(grads, ids, count):
-        per, r_lo, width = count // n_fs, RANK // n_grp, grads.shape[1]
-        order = jnp.arange(count * RANK).reshape(n_fs, per, n_grp, r_lo)
-        v = spread_rows(grads, order.transpose(2, 0, 1, 3).reshape(-1), ids)
-        v = lax.psum_scatter(v, ("grp", "fs"), scatter_dimension=0, tiled=True)
-        v = lax.psum(v, "rep")
-        v = lax.all_gather(v, "grp", axis=0, tiled=True)
-        v = v.reshape(n_grp, per, r_lo, width).transpose(1, 0, 2, 3)
-        return v.reshape(per, RANK, width).astype(F32)
+    def other_pairs(v):
+        step = 2
+        while step < n_rep:
+            far = lax.ppermute(v, "rep", [(i, i ^ step) for i in range(n_rep)])
+            v = (v.astype(F32) + far.astype(F32)).astype(BF)
+            step *= 2
+        return v.astype(F32)
 
     def body(
         prompt_input_rows,
@@ -745,115 +1066,94 @@
         continuation_cotangent,
     ):
         prompt_len, width = prompt_input_rows.shape[2:]
-        cont_len = continuation_input.shape[3]
         count = adapter_up_input.shape[0]
         hidden = frozen_up_weight.shape[1]
         shard_rows = frozen_query_key_value.shape[0]
-        parts = frozen_down_weight.shape[0] // shard_rows
-        assert hidden == n_shard * BLOCK and parts * shard_rows == BLOCK
-
-        def tokens(prompt, cont):
-            return jnp.concatenate(
-                [prompt.reshape(prompt_len, width), cont.reshape(cont_len, width)], 0
-            )
-
-        def columns(w):
-            return w.reshape(shard_rows, -1, BLOCK).swapaxes(0, 1)
-
-        x = tokens(prompt_input_rows, continuation_input)
-        cot = tokens(prompt_cotangent, continuation_cotangent)
-        ids = jnp.concatenate(
-            [prompt_group_adapter.reshape(1), continuation_adapter.reshape(1)]
+        assert n_grp == 4 and hidden == n_shard * BLOCK
+        assert frozen_down_weight.shape[0] == BLOCK and BLOCK % shard_rows == 0
+
+        def flat(v):
+            return v.reshape(v.shape[-2:])
+
+        x_p, x_c = flat(prompt_input_rows), flat(continuation_input)
+        cot_p, cot_c = flat(prompt_cotangent), flat(continuation_cotangent)
+        ids = jnp.concatenate([prompt_group_adapter.reshape(1), continuation_adapter.reshape(1)])
+        a_ext, b_ext, a_up, b_up, a_dn, b_dn = select_call(
+            ids,
+            [
+                adapter_attention_input.swapaxes(2, 3),
+                adapter_attention_output,
+                adapter_up_input.swapaxes(1, 2),
+                adapter_up_output,
+                adapter_down_input.swapaxes(1, 2),
+                adapter_down_output,
+            ],
         )
-        a_attn = adapter_attention_input.swapaxes(2, 3)
-        b_attn = adapter_attention_output
-        a_up, b_up = adapter_up_input.swapaxes(1, 2), adapter_up_output
-        a_dn, b_dn = adapter_down_input.swapaxes(1, 2), adapter_down_output
+        place = jnp.repeat(ids, RANK) * RANK + jnp.arange(2 * RANK) % RANK
+        hot = (place[:, None] == jnp.arange(count * RANK)[None, :]).astype(BF)
         gain_one, bias_one, gain_two, bias_two = [
             v[None, :]
             for v in (first_norm_scale, first_norm_bias, second_norm_scale, second_norm_bias)
         ]
         w_qkv, qkv, normed_one, lows = project_call(
-            x,
-            gain_one,
-            bias_one,
-            ids,
-            a_attn,
-            b_attn,
-            columns(frozen_query_key_value),
-            n_fs,
-            n_shard,
-            prompt_len,
+            x_p, x_c, gain_one, bias_one, a_ext, b_ext, frozen_query_key_value, n_fs, n_shard
         )
-        dn_blocks = frozen_down_weight.reshape(parts, shard_rows, -1, BLOCK).transpose(2, 0, 1, 3)
-        blocks = [
-            columns(frozen_output_weight),
-            dn_blocks.reshape(-1, shard_rows, BLOCK),
-            columns(frozen_up_weight),
-        ]
-        counts = [b.shape[0] for b in blocks]
-        tables = (a_attn[:, 3], b_attn[:, 3], a_up, b_up, a_dn, b_dn)
         (
             w_rest,
             kp,
             mixed,
             normed_two,
-            result,
+            res_p,
+            res_c,
             grad_resid,
             grad_attn,
             low_o,
-            g_a_up,
-            g_b_up,
-            g_a_dn,
-            g_b_dn,
+            *mid,
         ) = middle_call(
-            x,
-            cot,
+            x_p,
+            x_c,
+            cot_p,
+            cot_c,
             qkv,
             gain_two,
             bias_two,
-            ids,
-            tables,
-            jnp.concatenate(blocks, 0),
-            counts,
+            (a_ext[3], b_ext[3], a_up, b_up, a_dn, b_dn),
+            (frozen_output_weight, frozen_down_weight, frozen_up_weight),
             n_fs,
             n_shard,
-            prompt_len,
         )
-        g_q, g_own, g_far, g_a_o, g_b_o = attention_back_call(
+        grad_p, grad_c, t_a, t_b, t_a_up, t_b_up, t_a_dn, t_b_dn = back_call(
             grad_attn,
             mixed,
             low_o,
+            lows,
+            gain_one,
+            a_ext,
+            b_ext,
+            hot,
+            mid,
             qkv,
             kp,
-            ids,
-            tables[0],
-            tables[1],
+            x_p,
+            x_c,
+            normed_one,
+            grad_resid,
             w_rest,
-            counts[0],
-            prompt_len,
+            w_qkv,
+            n_fs,
+            count,
         )
-        g_mine = lax.psum_scatter(g_far, "grp", scatter_dimension=0, tiled=True)
-        grads = jnp.concatenate([g_q, jnp.concatenate([g_mine, g_own], 0)], 1)
-        grad_inputs, g_a, g_b = project_back_call(
-            grads, x, normed_one, lows, grad_resid, gain_one, ids, a_attn, b_attn, w_qkv, prompt_len
-        )
-        flat = [g_b_up, g_a_dn, g_a[0], g_a[1], g_a[2], g_a_o, g_b, g_b_o, g_a_up, g_b_dn]
-        slim = reduce_tables(jnp.concatenate(flat, 1), [ids[0], ids[1]], count)
-        both = [slim[:, :, :hidden], slim[:, :, hidden : 2 * hidden]]
-        slim = slim[:, :, 2 * hidden :].reshape(slim.shape[0], RANK, 10, width).transpose(0, 2, 1, 3)
-
         return (
-            result[:prompt_len].reshape(prompt_input_rows.shape),
-            result[prompt_len:].reshape(continuation_input.shape),
-            grad_inputs[:prompt_len].reshape(prompt_input_rows.shape),
-            grad_inputs[prompt_len:].reshape(continuation_input.shape),
-            slim[:, :4].swapaxes(2, 3),
-            slim[:, 4:8],
-            slim[:, 8].swapaxes(1, 2),
-            both[0],
-            both[1].swapaxes(1, 2),
-            slim[:, 9],
+            res_p.reshape(prompt_input_rows.shape),
+            res_c.reshape(continuation_input.shape),
+            grad_p.reshape(prompt_input_rows.shape),
+            grad_c.reshape(continuation_input.shape),
+            other_pairs(t_a).swapaxes(2, 3),
+            other_pairs(t_b),
+            other_pairs(t_a_up).swapaxes(1, 2),
+            other_pairs(t_b_up),
+            other_pairs(t_a_dn).swapaxes(1, 2),
+            other_pairs(t_b_dn),
         )
 
     return body

time: 829 us -> 598 us (0.72)
  waiting for transfers between devices: 210 us -> 0 us
  local copies, waits for them, and re-layouts: 64.9 us -> 5.4 us
  Pallas kernels: 522 us -> 581 us
  between operations: 15.3 us -> 1.99 us
    reduce_scatter x2 -> x0, waiting for transfers between devices: 156 us -> none  [the longest x1 111 us: reduce_tables(): v = lax.psum_scatter(v, ('grp', 'fs'), scatter_dimension=0, tiled=True)]
    pallas_call x2, Pallas kernels: 63.8 us -> 125 us  [the longest x1 122 us: back_call(): pl.pallas_call(kernel, out_shape=[like(x_p.shape, BF), like(x_c.shape, BF...]
    psum x1 -> x0, waiting for transfers between devices: 32 us -> none  [reduce_tables(): v = lax.psum(v, 'rep')]
    all_gather x1 -> x0, waiting for transfers between devices: 21.8 us -> none  [reduce_tables(): v = lax.all_gather(v, 'grp', axis=0, tiled=True)]
    unnamed x50 -> x20, local copies, waits for them, and re-layouts: 21.8 us -> 3.56 us
    reshape x11 -> x0, local copies, waits for them, and re-layouts: 15.6 us -> none  [the longest x2 5.08 us: body(): frozen_down_weight.reshape(parts, shard_rows, -1, BLOCK)]
    convert_element_type x3 -> x0, local copies, waits for them, and re-layouts: 15.4 us -> none  [reduce_tables(): return v.reshape(per, RANK, width).astype(F32)]
    concatenate x3 -> x0, other arithmetic: 8.71 us -> none  [the longest x1 4.29 us: body(): grads = jnp.concatenate([g_q, jnp.concatenate([g_mine, g_own], 0)], 1)]
  transfers between devices with their start and end apart: 4 -> 0, of which waited for: 4 -> 0; matrix products, arithmetic and copies ran while one was open for 1% -> 0% of each run, Pallas kernels for 0% -> 0%
where the time goes in v3:
time: 598 us; the launch traced here: 597 us
  Pallas kernels  581 us (97%)
  other arithmetic  9.15 us (2%)
    pallas_call x1, Pallas kernels, middle_call(): pl.pallas_call(kernel, out_shape=[like((count, n_shard, shard_rows, BLOCK...  339 us
    pallas_call x1, Pallas kernels, back_call(): pl.pallas_call(kernel, out_shape=[like(x_p.shape, BF), like(x_c.shape, BF...  122 us
    pallas_call x1, Pallas kernels, project_call(): pl.pallas_call(kernel, out_shape=[jax.ShapeDtypeStruct((count, n_shard, s...  117 us

profile of v3, /device:TPU:0, one launch (start us, length us, event | category | flops | bytes accessed | tf_op | source)
XLA Modules:
  0.0 597.3 jit_solution(9211100127959292234)
XLA Ops:
  1.9 0.6 broadcast_multiply_fusion
  2.5 3.4 select.3
  5.9 117.0 %project.1 = (bf16[12,16,128,512]{3,2,1,0:T(8,128)(2,1)}, bf16[384,6144]{1,0:T(8,128)(2,1)}, bf16[384,2048]{1,0:T(8,128)(2,1)}, bf16[3,384,32]{2,1,0:T(8,128)(2,1)}) custom-call(bf16[128,2048]{1,0:T(8,128)(2,1)} %bitcast.32, bf16[256,2048]{1,0:T(8,128)(2,1)} %bitcast.29, f32[1,2048]{1,0:T(1,128)} %bitcast.44, f32[1,2048]{1,0:T(1,128)} %bitcast.46, ...), custom_call_target="tpu_custom_call" | custom-call | tf_op jit(solution)/shard_map/project/pallas_call | solution.py:369
  122.9 1.7 slice_bitcast_fusion
  124.6 338.6 %middle.1 = (bf16[36,16,128,512]{3,2,1,0:T(8,128)(2,1)}, bf16[4,128,4096]{2,1,0:T(8,128)(2,1)}, bf16[384,2048]{1,0:T(8,128)(2,1)}, bf16[384,2048]{1,0:T(8,128)(2...) custom-call(bf16[128,2048]{1,0:T(8,128)(2,1)} %bitcast.33, ...), custom_call_target="tpu_custom_call" | custom-call | tf_op jit(solution)/shard_map/middle/pallas_call | solution.py:566
  463.2 0.1 broadcast_in_dim.21
  463.3 0.1 mul.18
  463.4 0.7 fusion.refs_7_
  464.1 121.7 %back.1 = (bf16[128,2048]{1,0:T(8,128)(2,1)}, bf16[256,2048]{1,0:T(8,128)(2,1)}, bf16[2,4,16,2048]{3,2,1,0:T(8,128)(2,1)}, bf16[2,4,16,2048]{3,2,1,0:T(8,128)(2,...) custom-call(bf16[384,2048]{1,0:T(8,128)(2,1)} %get-tuple-element.49., ...), custom_call_target="tpu_custom_call" | custom-call | tf_op jit(solution)/shard_map/back/pallas_call | solution.py:988
  585.8 0.0 copy-start.7
  585.8 0.0 copy-start.3
  585.8 2.2 convert_bitcast_fusion.1
  588.0 0.0 copy-start.2
  588.0 2.2 convert_element_type.16
  590.2 0.0 copy-start.6
  590.2 0.0 copy-start.4
  590.2 0.0 copy-done.7
  590.2 0.7 convert_bitcast_fusion.2
  590.9 0.0 copy-done.3
  590.9 0.0 copy-start
  590.9 1.0 convert_element_type.17
  592.0 0.0 copy-done.2
  592.0 1.0 convert_bitcast_fusion
  593.0 0.0 copy-start.5
  593.0 0.0 copy-done.6
  593.0 0.7 convert_element_type.18
  593.7 0.0 copy-done.4
  593.7 0.0 copy-start.1
  593.7 0.8 copy.36
  594.5 0.0 copy-done
  594.5 1.0 copy.37
  595.5 0.0 copy-done.5
  595.5 0.8 copy.38
  596.3 0.0 copy-done.1
  596.3 1.0 copy.39
  (1 shorter events, 0.0 us)
Async XLA Ops:
  585.8 4.4 copy-start.7
  585.8 5.1 copy-start.3
  588.0 4.0 copy-start.2
  590.2 2.8 copy-start.6
  590.2 3.5 copy-start.4
  590.9 3.6 copy-start
  593.0 2.5 copy-start.5
  593.7 2.6 copy-start.1

commit v4 on v3

--- a/solution.py
+++ b/solution.py
@@ -11,6 +11,7 @@
 HDIM = 128
 RANK = 16
 BLOCK = 512
+PART = 256
 SCALE = HDIM ** (-0.5)
 NEG_FILL = -1e30
 BF = jnp.bfloat16
@@ -18,7 +19,6 @@
 MESH = pl.DeviceIdType.MESH
 ANY = pl.BlockSpec(memory_space=pl.ANY)
 WHOLE = pl.BlockSpec(memory_space=pltpu.VMEM)
-SCALARS = pl.BlockSpec(memory_space=pltpu.SMEM)
 ROOM = 62 * 2**20
 
 
@@ -283,20 +283,6 @@
     return (q_p, q_c, k_p, k_c, v_p, v_c), (c_p, e_1 * inv, e_2 * inv)
 
 
-def columns_of(ref):
-    return lambda j, first, size: ref.at[
-        pl.ds(first, size), pl.ds(pl.multiple_of(j * BLOCK, BLOCK), BLOCK)
-    ]
-
-
-def tiles_of(ref, shard_rows, parts):
-    def tile(j, first, size):
-        row = pl.multiple_of(lax.rem(j, parts) * shard_rows + first, 8)
-        return ref.at[pl.ds(row, size), pl.ds(pl.multiple_of(j // parts * BLOCK, BLOCK), BLOCK)]
-
-    return tile
-
-
 def select_call(ids, tables):
     def kernel(ids, *refs):
         for src, dst in zip(refs[: len(tables)], refs[len(tables) :]):
@@ -324,99 +310,77 @@
     )(ids, *tables)
 
 
-def project_call(x_p, x_c, gain, bias, a_ext, b_ext, weight, n_fs, n_shard):
+def columns_of(ref):
+    return lambda j, first, size: ref.at[
+        pl.ds(first, size), pl.ds(pl.multiple_of(j * PART, PART), PART)
+    ]
+
+
+def tiles_of(ref, shard_rows, parts):
+    def tile(j, first, size):
+        row = pl.multiple_of(lax.rem(j, parts) * shard_rows + first, 8)
+        return ref.at[pl.ds(row, size), pl.ds(pl.multiple_of(j // parts * PART, PART), PART)]
+
+    return tile
+
+
+def pair_loads(blocks, first, wbuf, wsem, k):
+    return [
+        pltpu.make_async_copy(
+            blocks.at[first + i], wbuf.at[k, :, :, pl.ds(i * PART, PART)], wsem.at[k, i]
+        )
+        for i in range(2)
+    ]
+
+
+def forward_call(x_p, x_c, cot_p, cot_c, norms, tables, weights, n_fs, n_shard):
     prompt_len, width = x_p.shape
     rows = prompt_len + x_c.shape[0]
-    shard_rows, count = weight.shape[0], weight.shape[1] // BLOCK
-    per = width // BLOCK
-
-    def kernel(
-        x_p, x_c, gain, bias, a_ext, b_ext, src, dst, qkv, normed, lows, wbuf, wsem, *sems
-    ):
-        engine = Gather(n_fs, [(count, columns_of(src))], dst, sems)
-        engine.barrier()
-
-        def load(j):
-            return pltpu.make_async_copy(dst.at[j], wbuf.at[lax.rem(j, 2)], wsem.at[lax.rem(j, 2)])
-
-        def early(t):
-            @pl.when(t == 0)
-            def _():
-                for x, part in ((x_p, slice(0, prompt_len)), (x_c, slice(prompt_len, None))):
-                    hat, _ = norm_stats(x[...].astype(F32))
-                    normed[part] = (hat * gain[...] + bias[...]).astype(BF)
-                for n in range(3):
-                    lows[n] = low_of(mm_nt(normed[...], a_ext[n]), prompt_len)
-
-        def compute(j):
-            @pl.when(j < count)
-            def _():
-                load(j).start()
-
-            @pl.when(j > 0)
-            def _():
-                i = j - 1
-                load(i).wait()
-                n = i // per
-                w = wbuf[lax.rem(i, 2)].reshape(-1, BLOCK)
-                inside = pl.ds(pl.multiple_of(lax.rem(i, per) * BLOCK, BLOCK), BLOCK)
-                extra = mm(lows[n], b_ext[n, :, inside])
-                cols = pl.ds(pl.multiple_of(i * BLOCK, BLOCK), BLOCK)
-                qkv[:, cols] = (mm(normed[...], w) + extra).astype(BF)
-
-        engine.run(early, compute)
-
-    return pl.pallas_call(
-        kernel,
-        out_shape=[
-            jax.ShapeDtypeStruct((count, n_shard, shard_rows, BLOCK), BF),
-            jax.ShapeDtypeStruct((rows, 3 * width), BF),
-            jax.ShapeDtypeStruct((rows, width), BF),
-            jax.ShapeDtypeStruct((3, rows, 2 * RANK), BF),
-        ],
-        in_specs=[WHOLE] * 6 + [ANY],
-        out_specs=[ANY, WHOLE, WHOLE, WHOLE],
-        scratch_shapes=[
-            pltpu.VMEM((2, n_shard, shard_rows, BLOCK), BF),
-            pltpu.SemaphoreType.DMA((2,)),
-        ]
-        + Gather.semaphores(n_fs),
-        compiler_params=pltpu.CompilerParams(
-            collective_id=0, has_side_effects=True, vmem_limit_bytes=ROOM
-        ),
-        name="project",
-    )(x_p, x_c, gain, bias, a_ext, b_ext, weight)
-
-
-def middle_call(x_p, x_c, cot_p, cot_c, qkv, gain, bias, tables, weights, n_fs, n_shard):
-    prompt_len, width = x_p.shape
-    rows = prompt_len + x_c.shape[0]
-    shard_rows, hidden = weights[2].shape
-    parts = weights[1].shape[0] // shard_rows
-    n_out, n_up = width // BLOCK, hidden // BLOCK
+    shard_rows, hidden = weights[3].shape
+    parts = weights[2].shape[0] // shard_rows
+    n_qkv, n_out, n_up = 3 * width // PART, width // PART, hidden // PART
     n_dn = n_out * parts
-    count = n_out + n_dn + n_up
+    before_up = n_qkv + n_out + n_dn
+    count = before_up + n_up
     n_grp = n_shard // n_fs
     heads = width // HDIM
-    go, first_head = 4, 5
-    first_out = first_head + heads
-    a_o, b_o, a_u, b_u, a_d, b_d = range(6)
-
-    def kernel(x_p, x_c, cot_p, cot_c, qkv, gain, bias, *refs):
-        ext, src, refs = refs[:6], refs[6:9], refs[9:]
-        (dst, kp, mixed, normed, res_p, res_c, resid_back, grad_attn), refs = refs[:8], refs[8:]
-        (low_o, g_a_up, g_b_up, g_a_dn, g_b_dn), refs = refs[:5], refs[5:]
-        (cot, resid, out_acc, low_up, dlow_dn, low_dn, dlow_up), refs = refs[:7], refs[7:]
-        (wbuf, dbuf, wsem, dsem, ksend, krecv), sems = refs[:6], refs[6:]
+    per = width // BLOCK
+    lag = 2
+    t_share = n_qkv + lag * (n_fs + 2) + 1
+    t_onward = t_share + 10
+    t_head = t_onward + 1
+    t_out = t_head + heads
+    t_norm = t_out + per
+
+    def kernel(x_p, x_c, gain_one, bias_one, gain_two, bias_two, *refs):
+        (a_ext, b_ext, a_up, b_up, a_dn, b_dn), refs = refs[:6], refs[6:]
+        (cot_p, cot_c), src, refs = refs[:2], refs[2:6], refs[6:]
+        (dst, qkv_out, kp_out, normed_out, mixed_out), refs = refs[:5], refs[5:]
+        (lows, res_p, res_c, resid_back, grad_attn, low_o), refs = refs[:6], refs[6:]
+        (g_a_up, g_b_up, g_a_dn, g_b_dn), refs = refs[:4], refs[4:]
+        (qkv, kp, normed_one, normed, mixed, cot, resid, out_acc), refs = refs[:8], refs[8:]
+        (low_up, dlow_dn, low_dn, dlow_up, wbuf, dbuf), refs = refs[:6], refs[6:]
+        (wsem, dsem, ksend, krecv, lsem), sems = refs[:5], refs[5:]
         own, rest = slice(0, prompt_len), slice(prompt_len, None)
         sources = [
-            (n_out, columns_of(src[0])),
-            (n_dn, tiles_of(src[1], shard_rows, parts)),
-            (n_up, columns_of(src[2])),
+            (n_qkv, columns_of(src[0])),
+            (n_out, columns_of(src[1])),
+            (n_dn, tiles_of(src[2], shard_rows, parts)),
+            (n_up, columns_of(src[3])),
         ]
-        engine = Gather(n_fs, sources, dst, sems)
+        engine = Gather(n_fs, sources, dst, sems, lag)
         engine.barrier()
         grp = lax.axis_index("grp")
+        loads = [
+            pltpu.make_async_copy(cot_p, cot.at[pl.ds(0, prompt_len)], lsem.at[0]),
+            pltpu.make_async_copy(cot_c, cot.at[pl.ds(prompt_len, rows - prompt_len)], lsem.at[1]),
+        ]
+        stores = [
+            pltpu.make_async_copy(qkv, qkv_out, lsem.at[2]),
+            pltpu.make_async_copy(kp, kp_out, lsem.at[3]),
+            pltpu.make_async_copy(normed_one, normed_out, lsem.at[4]),
+            pltpu.make_async_copy(mixed, mixed_out, lsem.at[5]),
+        ]
 
         def pass_on(n, whose, to):
             return pltpu.make_async_remote_copy(
@@ -436,140 +400,185 @@
         onward = pass_on(2, engine.far_row, engine.far_core)
         diagonal = (1 - engine.y) * 2 + 1 - engine.c
 
-        def load_out(b):
-            return pltpu.make_async_copy(dst.at[b], wbuf.at[lax.rem(b, 2)], wsem.at[lax.rem(b, 2)])
-
         def early(t):
             @pl.when(t == 0)
+            def _():
+                for copy in loads:
+                    copy.start()
+                for x, part in ((x_p, own), (x_c, rest)):
+                    hat, _ = norm_stats(x[...].astype(F32))
+                    normed_one[part] = (hat * gain_one[...] + bias_one[...]).astype(BF)
+                for n in range(3):
+                    lows[n] = low_of(mm_nt(normed_one[...], a_ext[n]), prompt_len)
+                for copy in loads:
+                    copy.wait()
+                dlow_dn[...] = low_of(mm_nt(cot[...], b_dn[...]), prompt_len)
+
+            @pl.when(t == t_share)
             def _():
                 kp[grp] = qkv[:prompt_len, width:]
                 to_row.start()
                 to_core.start()
-                cot[own] = cot_p[...]
-                cot[rest] = cot_c[...]
-                dlow_dn[...] = low_of(mm_nt(cot[...], ext[b_d][...]), prompt_len)
-
-            @pl.when(t == go)
+                stores[0].start()
+                stores[2].start()
+
+            @pl.when(t == t_onward)
             def _():
                 landed(0, engine.far_row).wait()
                 onward.start()
 
-            @pl.when(t == first_head)
+            @pl.when(t == t_head)
             def _():
                 landed(1, engine.far_core).wait()
                 landed(2, diagonal).wait()
                 to_row.wait_send()
                 to_core.wait_send()
                 onward.wait_send()
-
-            @pl.when((t >= first_head) & (t < first_out))
-            def _():
-                h = t - first_head
+                stores[1].start()
+
+            @pl.when((t >= t_head) & (t < t_out))
+            def _():
+                h = t - t_head
                 (_, _, _, _, v_p, v_c), (c_p, c_1, c_2) = head_chances(
                     qkv, kp, h, prompt_len, width, grp * prompt_len
                 )
                 lanes = pl.ds(pl.multiple_of(h * HDIM, HDIM), HDIM)
-                mixed[:prompt_len, lanes] = mm(c_p.astype(BF), v_p).astype(BF)
-                mixed[prompt_len:, lanes] = (
-                    mm(c_1.astype(BF), v_p) + mm(c_2.astype(BF), v_c)
-                ).astype(BF)
-
-            @pl.when(t == first_out - 1)
-            def _():
-                load_out(0).start()
-
-            @pl.when((t >= first_out) & (t < first_out + n_out))
-            def _():
-                b = t - first_out
+                mixed[own, lanes] = mm(c_p.astype(BF), v_p).astype(BF)
+                mixed[rest, lanes] = (mm(c_1.astype(BF), v_p) + mm(c_2.astype(BF), v_c)).astype(BF)
+
+            def load_out(b):
+                return pair_loads(dst, n_qkv + 2 * b, wbuf, wsem, lax.rem(b, 2))
+
+            @pl.when(t == t_out - 1)
+            def _():
+                for copy in load_out(0):
+                    copy.start()
+
+            @pl.when((t >= t_out) & (t < t_norm))
+            def _():
+                b = t - t_out
 
                 @pl.when(b == 0)
                 def _():
-                    low_o[...] = low_of(mm_nt(mixed[...], ext[a_o][...]), prompt_len)
-
-                load_out(b).wait()
-
-                @pl.when(b + 1 < n_out)
+                    stores[3].start()
+                    low_o[...] = low_of(mm_nt(mixed[...], a_ext[3]), prompt_len)
+
+                for copy in load_out(b):
+                    copy.wait()
+
+                @pl.when(b + 1 < per)
                 def _():
-                    load_out(b + 1).start()
+                    for copy in load_out(b + 1):
+                        copy.start()
 
                 cols = pl.ds(pl.multiple_of(b * BLOCK, BLOCK), BLOCK)
                 w = wbuf[lax.rem(b, 2)].reshape(-1, BLOCK)
-                branch = mm(mixed[...], w) + mm(low_o[...], ext[b_o][:, cols])
+                branch = mm(mixed[...], w) + mm(low_o[...], b_ext[3, :, cols])
                 resid[own, cols] = x_p[:, cols].astype(F32) + branch[own]
                 resid[rest, cols] = x_c[:, cols].astype(F32) + branch[rest]
 
-            @pl.when(t == first_out + n_out)
+            @pl.when(t == t_norm)
             def _():
                 hat, _ = norm_stats(resid[...])
-                normed[...] = (hat * gain[...] + bias[...]).astype(BF)
-                low_up[...] = low_of(mm_nt(normed[...], ext[a_u][...]), prompt_len)
+                normed[...] = (hat * gain_two[...] + bias_two[...]).astype(BF)
+                low_up[...] = low_of(mm_nt(normed[...], a_up[...]), prompt_len)
                 out_acc[...] = resid[...]
                 resid_back[...] = jnp.zeros_like(resid_back)
                 low_dn[...] = jnp.zeros_like(low_dn)
                 dlow_up[...] = jnp.zeros_like(dlow_up)
 
-        def load_up(n):
+        def load(j):
+            k, i = lax.rem(j // 2, 2), lax.rem(j, 2)
+            into = wbuf.at[k, :, :, pl.ds(pl.multiple_of(i * PART, PART), PART)]
+            return pltpu.make_async_copy(dst.at[j], into, wsem.at[k, i])
+
+        def load_down(n):
             k = lax.rem(n, 2)
-            up = pltpu.make_async_copy(dst.at[n_out + n_dn + n], wbuf.at[k], wsem.at[k])
-            down = pltpu.make_async_copy(dst.at[pl.ds(n_out, n_dn), n], dbuf.at[k], dsem.at[k])
-            return up, down
+            return [
+                pltpu.make_async_copy(
+                    dst.at[pl.ds(n_qkv + n_out + b * parts, parts), n],
+                    dbuf.at[k, :, :, pl.ds(b * PART, PART)],
+                    dsem.at[k, b],
+                )
+                for b in range(n_out)
+            ]
 
         def compute(j):
-            n = j - (n_out + n_dn)
-
-            @pl.when((n >= 0) & (n < n_up))
-            def _():
-                for copy in load_up(n):
+            n = j - before_up
+
+            @pl.when((j < n_qkv) | ((n >= 0) & (n < n_up)))
+            def _():
+                load(j).start()
+
+            @pl.when((n >= 0) & (n < n_up) & (lax.rem(j, 2) == 0))
+            def _():
+                for copy in load_down(n // 2):
                     copy.start()
 
-            @pl.when(n > 0)
-            def _():
-                i = n - 1
-                for copy in load_up(i):
+            @pl.when((j > 0) & (j <= n_qkv) & (lax.rem(j, 2) == 0))
+            def _():
+                i = j // 2 - 1
+                for first in (j - 2, j - 1):
+                    load(first).wait()
+                w = wbuf[lax.rem(i, 2)].reshape(-1, BLOCK)
+                m = i // per
+                inside = pl.ds(pl.multiple_of(lax.rem(i, per) * BLOCK, BLOCK), BLOCK)
+                cols = pl.ds(pl.multiple_of(i * BLOCK, BLOCK), BLOCK)
+                extra = mm(lows[m], b_ext[m, :, inside])
+                qkv[:, cols] = (mm(normed_one[...], w) + extra).astype(BF)
+
+            @pl.when((n > 0) & (lax.rem(j, 2) == 0))
+            def _():
+                i = n // 2 - 1
+                for first in (j - 2, j - 1):
+                    load(first).wait()
+                for copy in load_down(i):
                     copy.wait()
-                k = lax.rem(i, 2)
                 cols = pl.ds(pl.multiple_of(i * BLOCK, BLOCK), BLOCK)
-                w_up = wbuf[k].reshape(-1, BLOCK)
-                a_dn, b_up = ext[a_d][:, cols], ext[b_u][:, cols]
-                pre = mm(normed[...], w_up) + mm(low_up[...], b_up)
+                w_up = wbuf[lax.rem(j // 2 - 1, 2)].reshape(-1, BLOCK)
+                w_dn = dbuf[lax.rem(i, 2)].reshape(BLOCK, width)
+                a_d, b_u = a_dn[:, cols], b_up[:, cols]
+                pre = mm(normed[...], w_up) + mm(low_up[...], b_u)
                 cdf = 0.5 * (1.0 + lax.erf(pre * math.sqrt(0.5)))
                 act = (pre * cdf).astype(BF)
                 slope = cdf + pre * jnp.exp(-0.5 * pre * pre) * (1.0 / math.sqrt(2.0 * math.pi))
-                grad_act = mm(dlow_dn[...], a_dn)
-                for b in range(n_out):
-                    w_dn = dbuf[k, b * parts : (b + 1) * parts].reshape(BLOCK, BLOCK)
-                    span = slice(b * BLOCK, (b + 1) * BLOCK)
-                    grad_act = grad_act + mm_nt(cot[:, span], w_dn)
-                    out_acc[:, span] += mm(act, w_dn)
+                grad_act = mm_nt(cot[...], w_dn) + mm(dlow_dn[...], a_d)
                 grad_pre = (grad_act * slope).astype(BF)
+                out_acc[...] += mm(act, w_dn)
                 resid_back[...] += mm_nt(grad_pre, w_up)
-                low_dn[...] += mm_nt(act, a_dn)
-                dlow_up[...] += mm_nt(grad_pre, b_up)
+                low_dn[...] += mm_nt(act, a_d)
+                dlow_up[...] += mm_nt(grad_pre, b_u)
                 g_b_up[:, cols] = mm_tn(low_up[...], grad_pre).astype(BF)
                 g_a_dn[:, cols] = mm_tn(dlow_dn[...], act).astype(BF)
 
         engine.run(early, compute)
+        dlow = low_of(dlow_up[...], prompt_len)
+        g_a_up[...] = mm_tn(dlow, normed[...]).astype(BF)
+        grad = resid_back[...] + mm(dlow, a_up[...])
+        grad = cot[...].astype(F32) + norm_back(resid[...], gain_two[...], grad)
+        resid_back[...] = grad
+        grad_attn[...] = grad.astype(BF)
         low = low_of(low_dn[...], prompt_len)
-        result = (out_acc[...] + mm(low, ext[b_d][...])).astype(BF)
+        result = (out_acc[...] + mm(low, b_dn[...])).astype(BF)
         res_p[...] = result[own]
         res_c[...] = result[rest]
         g_b_dn[...] = mm_tn(low, cot[...]).astype(BF)
-        dlow = low_of(dlow_up[...], prompt_len)
-        g_a_up[...] = mm_tn(dlow, normed[...]).astype(BF)
-        grad = resid_back[...] + mm(dlow, ext[a_u][...])
-        grad = cot[...].astype(F32) + norm_back(resid[...], gain[...], grad)
-        resid_back[...] = grad
-        grad_attn[...] = grad.astype(BF)
+        for copy in stores:
+            copy.wait()
 
     like = jax.ShapeDtypeStruct
     two = 2 * RANK
+    dma = pltpu.SemaphoreType.DMA
+    share = (n_grp, prompt_len, 2 * width)
     return pl.pallas_call(
         kernel,
         out_shape=[
-            like((count, n_shard, shard_rows, BLOCK), BF),
-            like((n_grp, prompt_len, 2 * width), BF),
+            like((count, n_shard, shard_rows, PART), BF),
+            like((rows, 3 * width), BF),
+            like(share, BF),
             like((rows, width), BF),
             like((rows, width), BF),
+            like((3, rows, two), BF),
             like(x_p.shape, BF),
             like(x_c.shape, BF),
             like((rows, width), F32),
@@ -580,9 +589,14 @@
             like((two, hidden), BF),
             like((two, width), BF),
         ],
-        in_specs=[WHOLE] * 13 + [ANY] * 3,
-        out_specs=[ANY] + [WHOLE] * 12,
+        in_specs=[WHOLE] * 12 + [ANY] * 6,
+        out_specs=[ANY] * 5 + [WHOLE] * 10,
         scratch_shapes=[
+            pltpu.VMEM((rows, 3 * width), BF),
+            pltpu.VMEM(share, BF),
+            pltpu.VMEM((rows, width), BF),
+            pltpu.VMEM((rows, width), BF),
+            pltpu.VMEM((rows, width), BF),
             pltpu.VMEM((rows, width), BF),
             pltpu.VMEM((rows, width), F32),
             pltpu.VMEM((rows, width), F32),
@@ -591,26 +605,27 @@
             pltpu.VMEM((rows, two), F32),
             pltpu.VMEM((rows, two), F32),
             pltpu.VMEM((2, n_shard, shard_rows, BLOCK), BF),
-            pltpu.VMEM((2, n_dn, shard_rows, BLOCK), BF),
-            pltpu.SemaphoreType.DMA((2,)),
-            pltpu.SemaphoreType.DMA((2,)),
-            pltpu.SemaphoreType.DMA((3,)),
-            pltpu.SemaphoreType.DMA((3,)),
+            pltpu.VMEM((2, parts, shard_rows, width), BF),
+            dma((2, 2)),
+            dma((2, n_out)),
+            dma((3,)),
+            dma((3,)),
+            dma((6,)),
         ]
-        + Gather.semaphores(n_fs),
+        + Gather.semaphores(n_fs, lag),
         compiler_params=pltpu.CompilerParams(
-            collective_id=1, has_side_effects=True, vmem_limit_bytes=ROOM
+            collective_id=0, has_side_effects=True, vmem_limit_bytes=ROOM
         ),
-        name="middle",
-    )(x_p, x_c, cot_p, cot_c, qkv, gain, bias, *tables, *weights)
+        name="forward",
+    )(x_p, x_c, *norms, *tables, cot_p, cot_c, *weights)
 
 
 PIECES = 8
 
 
 class TableSum:
-    def __init__(self, n_fs, hots, units, bufs, sems):
-        self.n_fs, self.hots, self.units = n_fs, hots, units
+    def __init__(self, n_fs, hots, units, bufs, sems, stepwise):
+        self.n_fs, self.hots, self.units, self.stepwise = n_fs, hots, units, stepwise
         self.out, self.got, self.dense, self.parts, self.sums = bufs
         (self.s1, self.r1, self.s2, self.r2, self.s3, self.r3) = sems
         rep, self.grp = lax.axis_index("rep"), lax.axis_index("grp")
@@ -678,18 +693,31 @@
             )
         return copies
 
+    def hand(self, n, whose, q):
+        return pltpu.make_async_remote_copy(
+            self.sums.at[whose],
+            self.sums.at[whose],
+            self.s3.at[n],
+            self.r3.at[n],
+            device_id=self.peers[q - 1][2],
+            device_id_type=MESH,
+        )
+
     def hand_out(self):
-        return [
-            pltpu.make_async_remote_copy(
-                self.sums.at[self.me],
-                self.sums.at[self.me],
-                self.s3.at[q],
-                self.r3.at[q],
-                device_id=where,
-                device_id_type=MESH,
-            )
-            for q, _, where in self.peers
+        return [self.hand(q, self.me, q) for q, _, _ in self.peers]
+
+    def relay(self, stage):
+        far_row, far_rep, both = (self.peers[q - 1][1] for q in (2, 4, 6))
+        steps = [
+            [(4, self.me, 4), (2, self.me, 2), (1, self.me, 1)],
+            [(6, far_rep, 2), (5, far_rep, 1), (3, far_row, 1)],
+            [(7, both, 1)],
         ]
+        return [self.hand(*step) for step in steps[stage]]
+
+    def arrived(self, q):
+        ref = self.sums.at[self.peers[q - 1][1]]
+        pltpu.make_async_copy(ref, ref, self.r3.at[q]).wait()
 
     def first(self):
         for copy in self.exchange():
@@ -720,14 +748,34 @@
         for n in range(1, self.n_fs):
             total = total + self.parts[n].astype(F32)
         self.sums[self.me] = total.astype(BF)
-        for copy in self.hand_out():
+        if not self.stepwise:
+            for copy in self.hand_out():
+                copy.start()
+            return
+        for copy in self.relay(0):
             copy.start()
 
+    def fourth(self):
+        self.arrived(4)
+        self.arrived(2)
+        for copy in self.relay(1):
+            copy.start()
+
+    def fifth(self):
+        self.arrived(6)
+        for copy in self.relay(2):
+            copy.start()
+
     def last(self, places):
-        for q, whose, _ in self.peers:
-            ref = self.sums.at[whose]
-            pltpu.make_async_copy(ref, ref, self.r3.at[q]).wait()
-        for copy in self.hand_out():
+        if self.stepwise:
+            for q in (1, 3, 5, 7):
+                self.arrived(q)
+            sent = self.relay(0) + self.relay(1) + self.relay(2)
+        else:
+            for q, _, _ in self.peers:
+                self.arrived(q)
+            sent = self.hand_out()
+        for copy in sent:
             copy.wait_send()
         for unit, place in enumerate(places):
             for k in range(PIECES):
@@ -738,19 +786,20 @@
 
 
 def back_call(
-    grad_attn, mixed, low_o, lows, gain, a_ext, b_ext, hot, mid, qkv, kp, x_p, x_c, normed, grad_resid, w_rest, w_qkv, n_fs, count
+    grad_attn, mixed, low_o, lows, gain, a_ext, b_ext, hot, mid, qkv, kp, x_p, x_c, normed, grad_resid, w_all, n_fs, count
 ):
     rows, width = grad_attn.shape
     prompt_len, cont_len = x_p.shape[0], x_c.shape[0]
     heads = width // HDIM
     n_grp = kp.shape[0]
-    n_shard, shard_rows = w_qkv.shape[1:3]
+    n_shard, shard_rows = w_all.shape[1:3]
     per = width // BLOCK
-    n_qkv = w_qkv.shape[0]
+    n_qkv = 3 * per
     hidden = mid[1].shape[1]
     adapters = count // n_fs
-    half_heads = heads // 2
-    half = half_heads * HDIM
+    groups = 4
+    group_heads = heads // groups
+    half = group_heads * HDIM
     two = 2 * RANK
     wide_units = hidden // width
     first_units = 2 * wide_units + 4
@@ -760,7 +809,7 @@
     def kernel(*refs):
         (grad_attn, mixed, low_o, lows, gain, a_ext, b_ext, hot), refs = refs[:8], refs[8:]
         (g_a_up, g_b_up, g_a_dn, g_b_dn), refs = refs[:4], refs[4:]
-        (qkv, kp, x_p, x_c, normed, grad_resid, w_rest, w_qkv), refs = refs[:8], refs[8:]
+        (qkv, kp, x_p, x_c, normed, grad_resid, w_all), refs = refs[:7], refs[7:]
         (out_p, out_c, t_a, t_b, t_a_up, t_b_up, t_a_dn, t_b_dn), refs = refs[:8], refs[8:]
         (grads, keep, late, x, normed_here, wbuf, gm, acc, dlow, dlow_o), refs = refs[:10], refs[10:]
         (far, far_core, far_row, hots), refs = refs[:4], refs[4:]
@@ -770,8 +819,8 @@
         grp = lax.axis_index("grp")
         y, c = grp // 2, grp % 2
         own, rest = slice(0, prompt_len), slice(prompt_len, None)
-        one = TableSum(n_fs, hots, first_units, bufs_one, sems_one)
-        two_ = TableSum(n_fs, hots, last_units, bufs_two, sems_two)
+        one = TableSum(n_fs, hots, first_units, bufs_one, sems_one, True)
+        two_ = TableSum(n_fs, hots, last_units, bufs_two, sems_two, False)
         barrier = pltpu.get_barrier_semaphore()
         for _, _, where in one.peers:
             pl.semaphore_signal(barrier, 1, device_id=where, device_id_type=MESH)
@@ -795,10 +844,15 @@
         for copy in loads:
             copy.start()
 
-        def load_w(ref, i, k):
-            return pltpu.make_async_copy(ref.at[i], wbuf.at[k], wsem.at[k])
-
-        load_w(w_rest, 0, 0).start()
+        def load_w(i, k):
+            for copy in pair_loads(w_all, 2 * i, wbuf, wsem, k):
+                copy.start()
+
+        def wait_w(i, k):
+            for copy in pair_loads(w_all, 2 * i, wbuf, wsem, k):
+                copy.wait()
+
+        load_w(n_qkv, 0)
         pl.semaphore_wait(barrier, len(one.peers) + n_fs - 1)
 
         hots[one.me] = hot[...]
@@ -827,20 +881,20 @@
 
         acc[...] = mm(dlow_o[...], a_ext[3])
         for n in range(per):
-            load_w(w_rest, n, n % 2).wait()
+            wait_w(n_qkv + n, n % 2)
             if n + 1 < per:
-                load_w(w_rest, n + 1, (n + 1) % 2).start()
+                load_w(n_qkv + n + 1, (n + 1) % 2)
             w = wbuf[n % 2].reshape(-1, BLOCK)
             acc[...] += mm_nt(grad_attn[:, n * BLOCK : (n + 1) * BLOCK], w)
         gm[...] = acc[...].astype(BF)
-        load_w(w_qkv, 0, 0).start()
-        load_w(w_qkv, 1, 1).start()
+        load_w(0, 0)
+        load_w(1, 1)
 
         loads[0].wait()
         loads[1].wait()
 
         def head(part, n, carry):
-            h = part * half_heads + n
+            h = part * group_heads + n
             first = grp * prompt_len
             (q_p, q_c, k_p, k_c, v_p, v_c), (c_p, c_1, c_2) = head_chances(
                 grads, keep, h, prompt_len, width, first
@@ -907,54 +961,74 @@
                 cols = slice((i + 1) * width + part * half, (i + 1) * width + (part + 1) * half)
                 grads[own, cols] = total[:, i * half : (i + 1) * half]
 
-        lax.fori_loop(0, half_heads, functools.partial(head, 0), 0)
-        for copy in to_core(0):
-            copy.start()
-        for copy in hot_sends:
-            copy.wait_send()
-        for q, whose, _ in one.peers:
-            pltpu.make_async_copy(hots.at[whose], hots.at[whose], hrecv.at[q]).wait()
-        one.second()
-        lax.fori_loop(0, half_heads // 2, functools.partial(head, 1), 0)
-        add_core(0)
-        lax.fori_loop(half_heads // 2, half_heads, functools.partial(head, 1), 0)
-        for copy in to_core(1):
-            copy.start()
-        one.third()
-
-        acc[...] = jnp.zeros_like(acc)
-        dlow[...] = jnp.zeros_like(dlow)
-
-        def project(i, m, carry):
-            n = i * per + m
+        def half_group(i, carry):
+            part = i // 2
+
+            @pl.when((lax.rem(i, 2) == 1) & (part > 0))
+            def _():
+                add_core(part - 1)
+
+            first = lax.rem(i, 2) * (group_heads // 2)
+            lax.fori_loop(first, first + group_heads // 2, functools.partial(head, part), 0)
+
+            @pl.when(lax.rem(i, 2) == 1)
+            def _():
+                for copy in to_core(part):
+                    copy.start()
+
+            @pl.when(i == groups + 1)
+            def _():
+                for copy in hot_sends:
+                    copy.wait_send()
+                for q, whose, _ in one.peers:
+                    pltpu.make_async_copy(hots.at[whose], hots.at[whose], hrecv.at[q]).wait()
+                one.second()
+
+            return carry
+
+        lax.fori_loop(0, 2 * groups, half_group, 0)
+
+        def tables(i):
+            part = grads[:, i * width : (i + 1) * width]
+            low = low_of(mm_nt(part, b_ext[i]), prompt_len)
+            two_.pack(i, mm_tn(low, normed_here[...]))
+            two_.pack(3 + i, mm_tn(lows[i], part))
+            dlow[i] = low
+
+        def project(n, carry):
             k = lax.rem(n, 2)
-            load_w(w_qkv, n, k).wait()
+            wait_w(n, k)
             part = grads[:, pl.ds(pl.multiple_of(n * BLOCK, BLOCK), BLOCK)]
             acc[...] += mm_nt(part, wbuf[k].reshape(-1, BLOCK))
-            dlow[i] += mm_nt(part, b_ext[i, :, pl.ds(pl.multiple_of(m * BLOCK, BLOCK), BLOCK)])
-            two_.pack(3 + i, mm_tn(lows[i], part), m * (BLOCK // piece))
 
             @pl.when(n + 2 < n_qkv)
             def _():
-                load_w(w_qkv, n + 2, k).start()
+                load_w(n + 2, k)
 
             return carry
 
-        lax.fori_loop(0, 1, functools.partial(project, 0), 0)
-        add_core(1)
-        lax.fori_loop(1, per, functools.partial(project, 0), 0)
-        add_row(0)
-        add_row(1)
-        for i in (1, 2):
-            lax.fori_loop(0, per, functools.partial(project, i), 0)
-
-        for copy in loads[2:]:
+        loads[3].wait()
+        tables(0)
+        add_core(groups - 1)
+        acc[...] = mm(dlow[0], a_ext[0])
+        lax.fori_loop(0, per, project, 0)
+        for part in range(groups):
+            add_row(part)
+        tables(1)
+        tables(2)
+        two_.first()
+        one.third()
+        acc[...] += mm(dlow[1], a_ext[1]) + mm(dlow[2], a_ext[2])
+
+        def project_more(n, carry):
+            pl.when(n == 2 * per)(one.fourth)
+            return project(n, carry)
+
+        lax.fori_loop(per, n_qkv, project_more, 0)
+        two_.second()
+        one.fifth()
+        for copy in (loads[2], loads[4], loads[5]):
             copy.wait()
-        for i in range(3):
-            low = low_of(dlow[i], prompt_len)
-            acc[...] += mm(low, a_ext[i])
-            two_.pack(i, mm_tn(low, normed_here[...]))
-        two_.first()
         back = late[...] + norm_back(x[...].astype(F32), gain[...], acc[...])
         back = back.astype(BF)
         out_p[...] = back[own]
@@ -977,7 +1051,6 @@
             + [whole(t_a_dn, n * width) for n in range(wide_units)]
             + [whole(t_a_up, 0), whole(t_b_dn, 0), one_map(t_a, 3), one_map(t_b, 3)]
         )
-        two_.second()
         two_.third()
         two_.last([one_map(t_a, n) for n in range(3)] + [one_map(t_b, n) for n in range(3)])
 
@@ -997,7 +1070,7 @@
             like((adapters, RANK, hidden), BF),
             like((adapters, RANK, width), BF),
         ],
-        in_specs=[WHOLE] * 12 + [ANY] * 8,
+        in_specs=[WHOLE] * 12 + [ANY] * 7,
         out_specs=[WHOLE] * 8,
         scratch_shapes=[
             pltpu.VMEM((rows, 3 * width), BF),
@@ -1008,18 +1081,18 @@
             pltpu.VMEM((2, n_shard, shard_rows, BLOCK), BF),
             pltpu.VMEM((rows, width), BF),
             pltpu.VMEM((rows, width), F32),
-            pltpu.VMEM((3, rows, two), F32),
+            pltpu.VMEM((3, rows, two), BF),
             pltpu.VMEM((rows, two), BF),
-            pltpu.VMEM((2, n_grp, prompt_len, 2 * half), BF),
-            pltpu.VMEM((2, 2, prompt_len, 2 * half), BF),
-            pltpu.VMEM((2, prompt_len, 2 * half), BF),
+            pltpu.VMEM((groups, n_grp, prompt_len, 2 * half), BF),
+            pltpu.VMEM((groups, 2, prompt_len, 2 * half), BF),
+            pltpu.VMEM((groups, prompt_len, 2 * half), BF),
             pltpu.VMEM((PIECES,) + hot.shape, BF),
         ]
         + bufs_one
         + bufs_two
         + sems_one
         + sems_two
-        + [dma((6,)), dma((2,)), dma((2, 2)), dma((2, 2)), dma((2,)), dma((2,))]
+        + [dma((6,)), dma((2, 2)), dma((groups, 2)), dma((groups, 2)), dma((groups,)), dma((groups,))]
         + [dma((PIECES,)), dma((PIECES,))],
         compiler_params=pltpu.CompilerParams(
             collective_id=2, has_side_effects=True, vmem_limit_bytes=ROOM
@@ -1027,7 +1100,7 @@
         name="back",
     )(
         grad_attn, mixed, low_o, lows, gain, a_ext, b_ext, hot, *mid,
-        qkv, kp, x_p, x_c, normed, grad_resid, w_rest, w_qkv,
+        qkv, kp, x_p, x_c, normed, grad_resid, w_all,
     )
 
 
@@ -1091,34 +1164,31 @@
         )
         place = jnp.repeat(ids, RANK) * RANK + jnp.arange(2 * RANK) % RANK
         hot = (place[:, None] == jnp.arange(count * RANK)[None, :]).astype(BF)
-        gain_one, bias_one, gain_two, bias_two = [
+        norms = [
             v[None, :]
             for v in (first_norm_scale, first_norm_bias, second_norm_scale, second_norm_bias)
         ]
-        w_qkv, qkv, normed_one, lows = project_call(
-            x_p, x_c, gain_one, bias_one, a_ext, b_ext, frozen_query_key_value, n_fs, n_shard
-        )
         (
-            w_rest,
+            w_all,
+            qkv,
             kp,
+            normed_one,
             mixed,
-            normed_two,
+            lows,
             res_p,
             res_c,
             grad_resid,
             grad_attn,
             low_o,
             *mid,
-        ) = middle_call(
+        ) = forward_call(
             x_p,
             x_c,
             cot_p,
             cot_c,
-            qkv,
-            gain_two,
-            bias_two,
-            (a_ext[3], b_ext[3], a_up, b_up, a_dn, b_dn),
-            (frozen_output_weight, frozen_down_weight, frozen_up_weight),
+            norms,
+            (a_ext, b_ext, a_up, b_up, a_dn, b_dn),
+            (frozen_query_key_value, frozen_output_weight, frozen_down_weight, frozen_up_weight),
             n_fs,
             n_shard,
         )
@@ -1127,7 +1197,7 @@
             mixed,
             low_o,
             lows,
-            gain_one,
+            norms[0],
             a_ext,
             b_ext,
             hot,
@@ -1138,8 +1208,7 @@
             x_c,
             normed_one,
             grad_resid,
-            w_rest,
-            w_qkv,
+            w_all,
             n_fs,
             count,
         )

time: 598 us -> 534 us (0.89)
  Pallas kernels: 581 us -> 517 us
    pallas_call x2 -> x1, Pallas kernels: 456 us -> 422 us  [forward_call(): pl.pallas_call(kernel, out_shape=[like((count, n_shard, shard_rows, PART)...]
    pallas_call x1, Pallas kernels: 122 us -> 92.1 us  [back_call(): pl.pallas_call(kernel, out_shape=[like(x_p.shape, BF), like(x_c.shape, BF...]
where the time goes in v4:
time: 534 us; the launch traced here: 533 us
  Pallas kernels  517 us (97%)
  other arithmetic  9.92 us (2%)
    pallas_call x1, Pallas kernels, forward_call(): pl.pallas_call(kernel, out_shape=[like((count, n_shard, shard_rows, PART)...  422 us
    pallas_call x1, Pallas kernels, back_call(): pl.pallas_call(kernel, out_shape=[like(x_p.shape, BF), like(x_c.shape, BF...  92.1 us

profile of v4, /device:TPU:0, one launch (start us, length us, event | category | flops | bytes accessed | tf_op | source)
XLA Modules:
  0.0 533.1 jit_solution(12842691896169251114)
XLA Ops:
  1.9 0.6 broadcast_multiply_fusion
  2.5 0.1 broadcast_in_dim.21
  2.6 0.1 mul.18
  2.7 0.7 fusion.refs_7_
  3.4 3.4 select.3
  6.7 422.1 %forward.1 = (bf16[96,16,128,256]{3,2,1,0:T(8,128)(2,1)}, bf16[384,6144]{1,0:T(8,128)(2,1)}, bf16[4,128,4096]{2,1,0:T(8,128)(2,1)}, bf16[384,2048]{1,0:T(8,128)(...) custom-call(bf16[128,2048]{1,0:T(8,128)(2,1)} %bitcast.27, ...), custom_call_target="tpu_custom_call" | custom-call | tf_op jit(solution)/shard_map/forward/pallas_call | solution.py:573
  428.8 92.1 %back.1 = (bf16[128,2048]{1,0:T(8,128)(2,1)}, bf16[256,2048]{1,0:T(8,128)(2,1)}, bf16[2,4,16,2048]{3,2,1,0:T(8,128)(2,1)}, bf16[2,4,16,2048]{3,2,1,0:T(8,128)(2,...) custom-call(bf16[384,2048]{1,0:T(8,128)(2,1)} %get-tuple-element.47., ...), custom_call_target="tpu_custom_call" | custom-call | tf_op jit(solution)/shard_map/back/pallas_call | solution.py:1061
  520.9 0.0 copy-start.4
  520.9 0.0 copy-start.3
  520.9 1.7 convert_bitcast_fusion.2
  522.6 1.6 convert_element_type.18
  524.2 0.0 copy-start.2
  524.2 2.2 convert_bitcast_fusion.1
  526.4 0.0 copy-done.4
  526.4 0.0 copy-start.5
  526.4 1.1 convert_element_type.16
  527.5 0.0 copy-done.3
  527.5 0.0 copy-start
  527.5 1.0 convert_element_type.17
  528.5 0.0 copy-done.2
  528.5 0.0 copy-start.6
  528.5 1.0 convert_bitcast_fusion
  529.6 0.0 copy-done.5
  529.6 0.0 copy-start.1
  529.6 0.8 copy.36
  530.4 0.0 copy-done
  530.4 1.0 copy.37
  531.3 0.0 copy-done.6
  531.3 0.8 copy.38
  532.1 0.0 copy-done.1
  532.1 1.0 copy.39
  (1 shorter events, 0.0 us)
Async XLA Ops:
  520.9 5.5 %copy-start.4 = (bf16[2,4,16,2048]{3,2,1,0:T(8,128)(2,1)S(1)}, bf16[2,4,16,2048]{3,2,1,0:T(8,128)(2,1)}, u32[]{:S(2)}) copy-start(bf16[2,4,16,2048]{3,2,1,0:T(8,128)(2,1)} %get-tuple-element.63) | copy-start | bytes 1572868
  520.9 6.6 %copy-start.3 = (bf16[2,16,8192]{2,1,0:T(8,128)(2,1)S(1)}, bf16[2,16,8192]{2,1,0:T(8,128)(2,1)}, u32[]{:S(2)}) copy-start(bf16[2,16,8192]{2,1,0:T(8,128)(2,1)} %get-tuple-element.65) | copy-start | bytes 1572868
  524.2 4.3 copy-start.2
  526.4 3.2 copy-start.5
  527.5 2.9 copy-start
  528.5 2.8 copy-start.6
  529.6 2.6 copy-start.1

commit v5 on v4

--- a/solution.py
+++ b/solution.py
@@ -12,6 +12,8 @@
 RANK = 16
 BLOCK = 512
 PART = 256
+AWAY = (40, 48)
+ALONG = 40
 SCALE = HDIM ** (-0.5)
 NEG_FILL = -1e30
 BF = jnp.bfloat16
@@ -56,9 +58,9 @@
 
 
 class Gather:
-    def __init__(self, n_fs, sources, dst, sems, lag=2, away=48):
-        (self.zs, self.zr, self.ys, self.yr, self.xs, self.xr) = sems[:6]
-        (self.cs, self.cr, self.ds, self.dr, self.loc) = sems[6:]
+    def __init__(self, n_fs, sources, dst, sems, lag=2):
+        (self.zs, self.zr, self.ws, self.wr, self.ys, self.yr, self.xs, self.xr) = sems[:8]
+        (self.cs, self.cr, self.ds, self.dr, self.loc) = sems[8:]
         self.nz, self.sources, self.dst = n_fs, sources, dst
         self.count, self.rows = dst.shape[0], dst.shape[2]
         self.lag, self.slots, self.last = lag, 2 * lag, n_fs + 2
@@ -69,16 +71,22 @@
         self.far_core = self.y * 2 + 1 - self.c
         self.far_row = (1 - self.y) * 2 + self.c
         self.own = grp * n_fs + self.z
-        self.away, self.stay = away, self.rows - away
-        self.in_first = pl.multiple_of(away * plane, 8)
-        self.out_first = pl.multiple_of(self.stay * plane, 8)
-        self.far_first = pl.multiple_of(self.stay * (1 - plane), 8)
+        self.inner, self.outer, self.far = [], [], []
+        for away in AWAY:
+            stay = self.rows - away
+            self.inner.append((pl.multiple_of(away * plane, 8), stay))
+            self.outer.append((pl.multiple_of(stay * plane, 8), away))
+            self.far.append((pl.multiple_of(stay * (1 - plane), 8), away))
+        first, stay = self.inner[1]
+        self.near = (first, stay - ALONG)
+        self.along = (pl.multiple_of(first + stay - ALONG, 8), ALONG)
 
     @staticmethod
     def semaphores(n_fs, lag=2):
         slots, dma = 2 * lag, pltpu.SemaphoreType.DMA
         return (
-            [dma((2 * slots, 2, n_fs)), dma((2 * slots, n_fs))]
+            [dma((3 * slots, 2, n_fs)), dma((3 * slots, n_fs))]
+            + [dma((3 * slots, n_fs))] * 2
             + [dma((slots, n_fs))] * 2
             + [dma((slots, 2 * n_fs))] * 6
             + [dma((slots,))]
@@ -105,14 +113,27 @@
             return [(None, self.z, 0)]
         return [(self.z >= d, self.z - d, 1), (self.z < self.nz - d, self.z + d, -1)]
 
+    def crossing(self, d, ok, fs, way):
+        if d < self.nz // 2:
+            return [(ok, self.inner[1])]
+        if d == self.nz - 1:
+            return [(ok, self.near)]
+        end = fs == (0 if way > 0 else self.nz - 1)
+        inside = jnp.logical_not(end)
+        return [(self.both(ok, inside), self.inner[1]), (self.both(ok, end), self.near)]
+
+    @staticmethod
+    def both(left, right):
+        return right if left is None else jnp.logical_and(left, right)
+
     def shard(self, other, fs, core):
         row = 1 - self.y if other else self.y
         return (row * 2 + core) * self.nz + fs
 
-    def send(self, j, shard, first, size, sems, src=None, **where):
-        rows = pl.ds(first, size)
+    def send(self, j, shard, span, sems, src=None, **where):
+        rows = pl.ds(*span)
         return pltpu.make_async_remote_copy(
-            self.dst.at[j, shard, rows] if src is None else src(first, size),
+            self.dst.at[j, shard, rows] if src is None else src(*span),
             self.dst.at[j, shard, rows],
             *sems,
             device_id=where,
@@ -132,30 +153,28 @@
             yield ok, pltpu.make_async_copy(src(0, self.rows), self.dst.at[j, self.own], sem)
 
     def sends(self, a, j, t):
-        todo, nz, k, kz = [], self.nz, lax.rem(t, self.slots), lax.rem(t, 2 * self.slots)
-        inner, outer, far = (self.in_first, self.stay), (self.out_first, self.away), self.far_first
-
-        def both(left, right):
-            return right if left is None else jnp.logical_and(left, right)
+        todo, nz = [], self.nz
+        k, kz = lax.rem(t, self.slots), lax.rem(t, 3 * self.slots)
 
         def column(ok, fs, way, src):
             shard = self.shard(0, fs, self.c)
             if way >= 0:
                 sems = (self.zs.at[kz, 0, fs], self.zr.at[kz, fs])
-                up = self.send(j, shard, *inner, sems, src, fs=self.z + 1)
-                todo.append((both(ok, self.z < nz - 1), up))
+                up = self.send(j, shard, self.inner[0], sems, src, fs=self.z + 1)
+                todo.append((self.both(ok, self.z < nz - 1), up))
             if way <= 0:
                 sems = (self.zs.at[kz, 1, fs], self.zr.at[kz, fs])
-                down = self.send(j, shard, *inner, sems, src, fs=self.z - 1)
-                todo.append((both(ok, self.z > 0), down))
+                down = self.send(j, shard, self.inner[0], sems, src, fs=self.z - 1)
+                todo.append((self.both(ok, self.z > 0), down))
             sems = (self.ys.at[k, fs], self.yr.at[k, fs])
-            todo.append((ok, self.send(j, shard, *inner, sems, src, grp=self.far_row)))
+            for ok_row, span in self.crossing(a, ok, fs, way):
+                todo.append((ok_row, self.send(j, shard, span, sems, src, grp=self.far_row)))
             if way:
                 sems = (self.xs.at[k, fs], self.xr.at[k, fs])
-                todo.append((ok, self.send(j, shard, *outer, sems, rep=self.far_rep)))
+                todo.append((ok, self.send(j, shard, self.outer[0], sems, rep=self.far_rep)))
             sems = (self.cs.at[k, fs], self.cr.at[k, fs])
-            size = inner if way else (0, self.rows)
-            todo.append((ok, self.send(j, shard, *size, sems, src, grp=self.far_core)))
+            span = self.inner[0] if way else (0, self.rows)
+            todo.append((ok, self.send(j, shard, span, sems, src, grp=self.far_core)))
 
         if a == 0:
             for ok, src in self.own_blocks(j):
@@ -163,46 +182,57 @@
         else:
             for ok, fs, way in self.at_distance(a):
                 column(ok, fs, way, None)
-        for ok, fs, _ in self.at_distance(a - 1):
+        for ok, fs, way in self.at_distance(a - 1):
             shard = self.shard(1, fs, self.c)
             sems = (self.xs.at[k, nz + fs], self.xr.at[k, nz + fs])
-            todo.append((ok, self.send(j, shard, *outer, sems, rep=self.far_rep)))
+            todo.append((ok, self.send(j, shard, self.outer[1], sems, rep=self.far_rep)))
             sems = (self.cs.at[k, nz + fs], self.cr.at[k, nz + fs])
-            todo.append((ok, self.send(j, shard, *inner, sems, grp=self.far_core)))
+            todo.append((ok, self.send(j, shard, self.inner[1], sems, grp=self.far_core)))
+            if nz // 2 <= a < nz:
+                to = self.z + way
+                ok = (fs == (0 if way > 0 else nz - 1)) & (to >= 0) & (to < nz)
+                sems = (self.ws.at[kz, fs], self.wr.at[kz, fs])
+                todo.append((ok, self.send(j, shard, self.along, sems, fs=to)))
         for other in (0, 1):
             for ok, fs, way in self.at_distance(a - 1 - other):
                 if way or other:
                     i = other * nz + fs
                     sems = (self.ds.at[k, i], self.dr.at[k, i])
                     shard = self.shard(other, fs, self.c)
-                    core = self.send(j, shard, far, self.away, sems, grp=self.far_core)
+                    core = self.send(j, shard, self.far[other], sems, grp=self.far_core)
                     todo.append((ok, core))
         return todo
 
     def arrivals(self, a, j, t):
-        todo, nz, k, kz = [], self.nz, lax.rem(t, self.slots), lax.rem(t, 2 * self.slots)
-        inner, far = (self.in_first, self.stay), (self.far_first, self.away)
-
-        def expect(ok, shard, first, size, sem):
-            ref = self.dst.at[j, shard, pl.ds(first, size)]
+        todo, nz = [], self.nz
+        k, kz = lax.rem(t, self.slots), lax.rem(t, 3 * self.slots)
+
+        def expect(ok, shard, span, sem):
+            ref = self.dst.at[j, shard, pl.ds(*span)]
             todo.append((ok, pltpu.make_async_copy(ref, ref, sem)))
 
         for ok, fs, way in self.at_distance(a):
             if way:
-                expect(ok, self.shard(0, fs, self.c), *inner, self.zr.at[kz, fs])
-        for ok, fs, _ in self.at_distance(a - 1):
-            expect(ok, self.shard(1, fs, self.c), *inner, self.yr.at[k, fs])
+                expect(ok, self.shard(0, fs, self.c), self.inner[0], self.zr.at[kz, fs])
+        for ok, fs, way in self.at_distance(a - 1):
+            shard = self.shard(1, fs, self.c)
+            for ok_row, span in self.crossing(a - 1, ok, fs, way):
+                expect(ok_row, shard, span, self.yr.at[k, fs])
+            if a - 1 >= nz // 2:
+                end = self.both(ok, fs == (0 if way > 0 else nz - 1))
+                expect(end, shard, self.along, self.wr.at[kz, fs])
         for other in (0, 1):
+            inner, far = self.inner[other], self.far[other]
             for ok, fs, way in self.at_distance(a - 1 - other):
                 i = other * nz + fs
                 if way or other:
-                    expect(ok, self.shard(other, fs, self.c), *far, self.xr.at[k, i])
-                size = inner if way or other else (0, self.rows)
-                expect(ok, self.shard(other, fs, 1 - self.c), *size, self.cr.at[k, i])
+                    expect(ok, self.shard(other, fs, self.c), far, self.xr.at[k, i])
+                span = inner if way or other else (0, self.rows)
+                expect(ok, self.shard(other, fs, 1 - self.c), span, self.cr.at[k, i])
             for ok, fs, way in self.at_distance(a - 2 - other):
                 if way or other:
                     i = other * nz + fs
-                    expect(ok, self.shard(other, fs, 1 - self.c), *far, self.dr.at[k, i])
+                    expect(ok, self.shard(other, fs, 1 - self.c), far, self.dr.at[k, i])
         return todo
 
     def run(self, early=None, compute=None):
@@ -333,6 +363,15 @@
     ]
 
 
+PIECES = 8
+
+
+def pack(out, unit, piece, value):
+    value = value.astype(BF)
+    for n in range(PIECES):
+        out[n, :, unit * piece : (unit + 1) * piece] = value[:, n * piece : (n + 1) * piece]
+
+
 def forward_call(x_p, x_c, cot_p, cot_c, norms, tables, weights, n_fs, n_shard):
     prompt_len, width = x_p.shape
     rows = prompt_len + x_c.shape[0]
@@ -345,6 +384,7 @@
     n_grp = n_shard // n_fs
     heads = width // HDIM
     per = width // BLOCK
+    piece = width // PIECES
     lag = 2
     t_share = n_qkv + lag * (n_fs + 2) + 1
     t_onward = t_share + 10
@@ -357,7 +397,7 @@
         (cot_p, cot_c), src, refs = refs[:2], refs[2:6], refs[6:]
         (dst, qkv_out, kp_out, normed_out, mixed_out), refs = refs[:5], refs[5:]
         (lows, res_p, res_c, resid_back, grad_attn, low_o), refs = refs[:6], refs[6:]
-        (g_a_up, g_b_up, g_a_dn, g_b_dn), refs = refs[:4], refs[4:]
+        packed, refs = refs[0], refs[1:]
         (qkv, kp, normed_one, normed, mixed, cot, resid, out_acc), refs = refs[:8], refs[8:]
         (low_up, dlow_dn, low_dn, dlow_up, wbuf, dbuf), refs = refs[:6], refs[6:]
         (wsem, dsem, ksend, krecv, lsem), sems = refs[:5], refs[5:]
@@ -548,12 +588,19 @@
                 resid_back[...] += mm_nt(grad_pre, w_up)
                 low_dn[...] += mm_nt(act, a_d)
                 dlow_up[...] += mm_nt(grad_pre, b_u)
-                g_b_up[:, cols] = mm_tn(low_up[...], grad_pre).astype(BF)
-                g_a_dn[:, cols] = mm_tn(dlow_dn[...], act).astype(BF)
+                wide = hidden // width
+                for base, grad in (
+                    (0, mm_tn(low_up[...], grad_pre).astype(BF)),
+                    (wide, mm_tn(dlow_dn[...], act).astype(BF)),
+                ):
+                    unit = pl.ds(pl.multiple_of((base + i // per) * piece, piece), piece)
+                    for m in range(BLOCK // piece):
+                        where = lax.rem(i, per) * (BLOCK // piece) + m
+                        packed[where, :, unit] = grad[:, m * piece : (m + 1) * piece]
 
         engine.run(early, compute)
         dlow = low_of(dlow_up[...], prompt_len)
-        g_a_up[...] = mm_tn(dlow, normed[...]).astype(BF)
+        pack(packed, 2 * (hidden // width), piece, mm_tn(dlow, normed[...]))
         grad = resid_back[...] + mm(dlow, a_up[...])
         grad = cot[...].astype(F32) + norm_back(resid[...], gain_two[...], grad)
         resid_back[...] = grad
@@ -562,7 +609,7 @@
         result = (out_acc[...] + mm(low, b_dn[...])).astype(BF)
         res_p[...] = result[own]
         res_c[...] = result[rest]
-        g_b_dn[...] = mm_tn(low, cot[...]).astype(BF)
+        pack(packed, 2 * (hidden // width) + 1, piece, mm_tn(low, cot[...]))
         for copy in stores:
             copy.wait()
 
@@ -584,13 +631,10 @@
             like((rows, width), F32),
             like((rows, width), BF),
             like((rows, two), BF),
-            like((two, width), BF),
-            like((two, hidden), BF),
-            like((two, hidden), BF),
-            like((two, width), BF),
+            like((PIECES, two, (2 * (hidden // width) + 2) * piece), BF),
         ],
         in_specs=[WHOLE] * 12 + [ANY] * 6,
-        out_specs=[ANY] * 5 + [WHOLE] * 10,
+        out_specs=[ANY] * 5 + [WHOLE] * 7,
         scratch_shapes=[
             pltpu.VMEM((rows, 3 * width), BF),
             pltpu.VMEM(share, BF),
@@ -620,9 +664,6 @@
     )(x_p, x_c, *norms, *tables, cot_p, cot_c, *weights)
 
 
-PIECES = 8
-
-
 class TableSum:
     def __init__(self, n_fs, hots, units, bufs, sems, stepwise):
         self.n_fs, self.hots, self.units, self.stepwise = n_fs, hots, units, stepwise
@@ -658,11 +699,8 @@
         dma = pltpu.SemaphoreType.DMA
         return bufs, [dma((PIECES,))] * 2 + [dma((n_fs,))] * 2 + [dma((PIECES,))] * 2
 
-    def pack(self, unit, value, first=0):
-        value = value.astype(BF)
-        cols = slice(unit * self.piece, (unit + 1) * self.piece)
-        for n in range(value.shape[1] // self.piece):
-            self.out[first + n, :, cols] = value[:, n * self.piece : (n + 1) * self.piece]
+    def pack(self, unit, value):
+        pack(self.out, unit, self.piece, value)
 
     def exchange(self):
         return [
@@ -786,7 +824,7 @@
 
 
 def back_call(
-    grad_attn, mixed, low_o, lows, gain, a_ext, b_ext, hot, mid, qkv, kp, x_p, x_c, normed, grad_resid, w_all, n_fs, count
+    grad_attn, mixed, low_o, lows, gain, a_ext, b_ext, hot, packed, qkv, kp, x_p, x_c, normed, grad_resid, w_all, n_fs, count
 ):
     rows, width = grad_attn.shape
     prompt_len, cont_len = x_p.shape[0], x_c.shape[0]
@@ -795,31 +833,32 @@
     n_shard, shard_rows = w_all.shape[1:3]
     per = width // BLOCK
     n_qkv = 3 * per
-    hidden = mid[1].shape[1]
+    piece = width // PIECES
     adapters = count // n_fs
     groups = 4
     group_heads = heads // groups
     half = group_heads * HDIM
     two = 2 * RANK
-    wide_units = hidden // width
-    first_units = 2 * wide_units + 4
-    last_units = 6
-    piece = width // PIECES
+    first_units = packed.shape[2] // piece
+    wide_units = first_units // 2 - 1
+    hidden = wide_units * width
+    last_units = 4
 
     def kernel(*refs):
         (grad_attn, mixed, low_o, lows, gain, a_ext, b_ext, hot), refs = refs[:8], refs[8:]
-        (g_a_up, g_b_up, g_a_dn, g_b_dn), refs = refs[:4], refs[4:]
+        packed, refs = refs[0], refs[1:]
         (qkv, kp, x_p, x_c, normed, grad_resid, w_all), refs = refs[:7], refs[7:]
         (out_p, out_c, t_a, t_b, t_a_up, t_b_up, t_a_dn, t_b_dn), refs = refs[:8], refs[8:]
         (grads, keep, late, x, normed_here, wbuf, gm, acc, dlow, dlow_o), refs = refs[:10], refs[10:]
         (far, far_core, far_row, hots), refs = refs[:4], refs[4:]
-        bufs_one, bufs_two, refs = refs[:5], refs[5:10], refs[10:]
-        sems_one, sems_two, refs = refs[:6], refs[6:12], refs[12:]
+        bufs_one, bufs_mid, bufs_two, refs = (packed, *refs[:4]), refs[4:9], refs[9:14], refs[14:]
+        sems_one, sems_mid, sems_two, refs = refs[:6], refs[6:12], refs[12:18], refs[18:]
         lsem, wsem, csend, crecv, rsend, rrecv, hsend, hrecv = refs
         grp = lax.axis_index("grp")
         y, c = grp // 2, grp % 2
         own, rest = slice(0, prompt_len), slice(prompt_len, None)
         one = TableSum(n_fs, hots, first_units, bufs_one, sems_one, True)
+        mid = TableSum(n_fs, hots, last_units, bufs_mid, sems_mid, True)
         two_ = TableSum(n_fs, hots, last_units, bufs_two, sems_two, False)
         barrier = pltpu.get_barrier_semaphore()
         for _, _, where in one.peers:
@@ -869,15 +908,10 @@
         ]
         for copy in hot_sends:
             copy.start()
-        for n in range(wide_units):
-            one.pack(n, g_b_up[:, n * width : (n + 1) * width])
-            one.pack(wide_units + n, g_a_dn[:, n * width : (n + 1) * width])
-        one.pack(2 * wide_units, g_a_up[...])
-        one.pack(2 * wide_units + 1, g_b_dn[...])
+        one.first()
         dlow_o[...] = low_of(mm_nt(grad_attn[...], b_ext[3]), prompt_len)
-        one.pack(2 * wide_units + 2, mm_tn(dlow_o[...], mixed[...]))
-        one.pack(2 * wide_units + 3, mm_tn(low_o[...], grad_attn[...]))
-        one.first()
+        mid.pack(0, mm_tn(dlow_o[...], mixed[...]))
+        mid.pack(1, mm_tn(low_o[...], grad_attn[...]))
 
         acc[...] = mm(dlow_o[...], a_ext[3])
         for n in range(per):
@@ -976,7 +1010,7 @@
                 for copy in to_core(part):
                     copy.start()
 
-            @pl.when(i == groups + 1)
+            @pl.when(i == 1)
             def _():
                 for copy in hot_sends:
                     copy.wait_send()
@@ -988,11 +1022,11 @@
 
         lax.fori_loop(0, 2 * groups, half_group, 0)
 
-        def tables(i):
+        def tables(i, into, first):
             part = grads[:, i * width : (i + 1) * width]
             low = low_of(mm_nt(part, b_ext[i]), prompt_len)
-            two_.pack(i, mm_tn(low, normed_here[...]))
-            two_.pack(3 + i, mm_tn(lows[i], part))
+            into.pack(first, mm_tn(low, normed_here[...]))
+            into.pack(first + 1, mm_tn(lows[i], part))
             dlow[i] = low
 
         def project(n, carry):
@@ -1008,25 +1042,27 @@
             return carry
 
         loads[3].wait()
-        tables(0)
         add_core(groups - 1)
+        tables(0, mid, 2)
+        mid.first()
         acc[...] = mm(dlow[0], a_ext[0])
         lax.fori_loop(0, per, project, 0)
         for part in range(groups):
             add_row(part)
-        tables(1)
-        tables(2)
+        tables(1, two_, 0)
+        tables(2, two_, 2)
         two_.first()
+        mid.second()
         one.third()
         acc[...] += mm(dlow[1], a_ext[1]) + mm(dlow[2], a_ext[2])
 
         def project_more(n, carry):
-            pl.when(n == 2 * per)(one.fourth)
+            pl.when(n == 2 * per + 1)(two_.second)
             return project(n, carry)
 
         lax.fori_loop(per, n_qkv, project_more, 0)
-        two_.second()
-        one.fifth()
+        mid.third()
+        one.fourth()
         for copy in (loads[2], loads[4], loads[5]):
             copy.wait()
         back = late[...] + norm_back(x[...].astype(F32), gain[...], acc[...])
@@ -1046,16 +1082,21 @@
 
             return place
 
+        two_.third()
+        one.fifth()
+        mid.fourth()
+        mid.fifth()
         one.last(
             [whole(t_b_up, n * width) for n in range(wide_units)]
             + [whole(t_a_dn, n * width) for n in range(wide_units)]
-            + [whole(t_a_up, 0), whole(t_b_dn, 0), one_map(t_a, 3), one_map(t_b, 3)]
+            + [whole(t_a_up, 0), whole(t_b_dn, 0)]
         )
-        two_.third()
-        two_.last([one_map(t_a, n) for n in range(3)] + [one_map(t_b, n) for n in range(3)])
+        mid.last([one_map(t_a, 3), one_map(t_b, 3), one_map(t_a, 0), one_map(t_b, 0)])
+        two_.last([one_map(t_a, 1), one_map(t_b, 1), one_map(t_a, 2), one_map(t_b, 2)])
 
     like = jax.ShapeDtypeStruct
     bufs_one, sems_one = TableSum.scratch(n_fs, first_units, piece, count)
+    bufs_mid, sems_mid = TableSum.scratch(n_fs, last_units, piece, count)
     bufs_two, sems_two = TableSum.scratch(n_fs, last_units, piece, count)
     dma = pltpu.SemaphoreType.DMA
     return pl.pallas_call(
@@ -1070,7 +1111,7 @@
             like((adapters, RANK, hidden), BF),
             like((adapters, RANK, width), BF),
         ],
-        in_specs=[WHOLE] * 12 + [ANY] * 7,
+        in_specs=[WHOLE] * 9 + [ANY] * 7,
         out_specs=[WHOLE] * 8,
         scratch_shapes=[
             pltpu.VMEM((rows, 3 * width), BF),
@@ -1088,9 +1129,11 @@
             pltpu.VMEM((groups, prompt_len, 2 * half), BF),
             pltpu.VMEM((PIECES,) + hot.shape, BF),
         ]
-        + bufs_one
+        + bufs_one[1:]
+        + bufs_mid
         + bufs_two
         + sems_one
+        + sems_mid
         + sems_two
         + [dma((6,)), dma((2, 2)), dma((groups, 2)), dma((groups, 2)), dma((groups,)), dma((groups,))]
         + [dma((PIECES,)), dma((PIECES,))],
@@ -1099,7 +1142,7 @@
         ),
         name="back",
     )(
-        grad_attn, mixed, low_o, lows, gain, a_ext, b_ext, hot, *mid,
+        grad_attn, mixed, low_o, lows, gain, a_ext, b_ext, hot, packed,
         qkv, kp, x_p, x_c, normed, grad_resid, w_all,
     )
 
@@ -1180,7 +1223,7 @@
             grad_resid,
             grad_attn,
             low_o,
-            *mid,
+            packed,
         ) = forward_call(
             x_p,
             x_c,
@@ -1201,7 +1244,7 @@
             a_ext,
             b_ext,
             hot,
-            mid,
+            packed,
             qkv,
             kp,
             x_p,

time: 534 us -> 504 us (0.944)
  Pallas kernels: 517 us -> 488 us
    pallas_call x1, Pallas kernels: 422 us -> 400 us  [forward_call(): pl.pallas_call(kernel, out_shape=[like((count, n_shard, shard_rows, PART)...]
    pallas_call x1, Pallas kernels: 92.1 us -> 84.1 us  [back_call(): pl.pallas_call(kernel, out_shape=[like(x_p.shape, BF), like(x_c.shape, BF...]
where the time goes in v5:
time: 504 us; the launch traced here: 503 us
  Pallas kernels  488 us (97%)
  other arithmetic  9.92 us (2%)
    pallas_call x1, Pallas kernels, forward_call(): pl.pallas_call(kernel, out_shape=[like((count, n_shard, shard_rows, PART)...  400 us
    pallas_call x1, Pallas kernels, back_call(): pl.pallas_call(kernel, out_shape=[like(x_p.shape, BF), like(x_c.shape, BF...  84.1 us

profile of v5, /device:TPU:0, one launch (start us, length us, event | category | flops | bytes accessed | tf_op | source)
XLA Modules:
  0.0 503.1 jit_solution(9655152357481384782)
XLA Ops:
  1.9 0.6 broadcast_multiply_fusion
  2.5 0.1 broadcast_in_dim.21
  2.6 0.1 mul.18
  2.7 0.7 fusion.refs_7_
  3.4 3.4 select.3
  6.7 400.0 %forward.1 = (bf16[96,16,128,256]{3,2,1,0:T(8,128)(2,1)}, bf16[384,6144]{1,0:T(8,128)(2,1)}, bf16[4,128,4096]{2,1,0:T(8,128)(2,1)}, bf16[384,2048]{1,0:T(8,128)(...) custom-call(bf16[128,2048]{1,0:T(8,128)(2,1)} %bitcast.27, ...), custom_call_target="tpu_custom_call" | custom-call | tf_op jit(solution)/shard_map/forward/pallas_call | solution.py:620
  406.8 84.1 %back.1 = (bf16[128,2048]{1,0:T(8,128)(2,1)}, bf16[256,2048]{1,0:T(8,128)(2,1)}, bf16[2,4,16,2048]{3,2,1,0:T(8,128)(2,1)}, bf16[2,4,16,2048]{3,2,1,0:T(8,128)(2,...) custom-call(bf16[384,2048]{1,0:T(8,128)(2,1)} %get-tuple-element.44., ...), custom_call_target="tpu_custom_call" | custom-call | tf_op jit(solution)/shard_map/back/pallas_call | solution.py:1102
  490.9 0.0 copy-start.4
  490.9 0.0 copy-start.3
  490.9 1.7 convert_bitcast_fusion.2
  492.6 1.6 convert_element_type.18
  494.2 0.0 copy-start.2
  494.2 2.2 convert_bitcast_fusion.1
  496.4 0.0 copy-done.4
  496.4 0.0 copy-start.5
  496.4 1.1 convert_element_type.16
  497.5 0.0 copy-done.3
  497.5 0.0 copy-start
  497.5 1.0 convert_element_type.17
  498.5 0.0 copy-done.2
  498.5 0.0 copy-start.6
  498.5 1.0 convert_bitcast_fusion
  499.6 0.0 copy-done.5
  499.6 0.0 copy-start.1
  499.6 0.8 copy.36
  500.4 0.0 copy-done
  500.4 1.0 copy.37
  501.3 0.0 copy-done.6
  501.3 0.8 copy.38
  502.1 0.0 copy-done.1
  502.1 1.0 copy.39
  (1 shorter events, 0.0 us)
Async XLA Ops:
  490.9 5.5 %copy-start.4 = (bf16[2,4,16,2048]{3,2,1,0:T(8,128)(2,1)S(1)}, bf16[2,4,16,2048]{3,2,1,0:T(8,128)(2,1)}, u32[]{:S(2)}) copy-start(bf16[2,4,16,2048]{3,2,1,0:T(8,128)(2,1)} %get-tuple-element.57) | copy-start | bytes 1572868
  490.9 6.6 %copy-start.3 = (bf16[2,16,8192]{2,1,0:T(8,128)(2,1)S(1)}, bf16[2,16,8192]{2,1,0:T(8,128)(2,1)}, u32[]{:S(2)}) copy-start(bf16[2,16,8192]{2,1,0:T(8,128)(2,1)} %get-tuple-element.59) | copy-start | bytes 1572868
  494.2 4.3 copy-start.2
  496.4 3.2 copy-start.5
  497.5 2.9 copy-start
  498.5 2.8 copy-start.6
  499.6 2.6 copy-start.1

commit v6 on v5

--- a/solution.py
+++ b/solution.py
@@ -386,9 +386,8 @@
     per = width // BLOCK
     piece = width // PIECES
     lag = 2
-    t_share = n_qkv + lag * (n_fs + 2) + 1
-    t_onward = t_share + 10
-    t_head = t_onward + 1
+    t_onward, t_low = 6, 12
+    t_head = n_qkv + lag * (n_fs + 2) + 1
     t_out = t_head + heads
     t_norm = t_out + per
 
@@ -398,7 +397,7 @@
         (dst, qkv_out, kp_out, normed_out, mixed_out), refs = refs[:5], refs[5:]
         (lows, res_p, res_c, resid_back, grad_attn, low_o), refs = refs[:6], refs[6:]
         packed, refs = refs[0], refs[1:]
-        (qkv, kp, normed_one, normed, mixed, cot, resid, out_acc), refs = refs[:8], refs[8:]
+        (qkv, kp, group, low_group, normed_one, normed, mixed, cot, resid, out_acc), refs = refs[:10], refs[10:]
         (low_up, dlow_dn, low_dn, dlow_up, wbuf, dbuf), refs = refs[:6], refs[6:]
         (wsem, dsem, ksend, krecv, lsem), sems = refs[:5], refs[5:]
         own, rest = slice(0, prompt_len), slice(prompt_len, None)
@@ -424,8 +423,8 @@
 
         def pass_on(n, whose, to):
             return pltpu.make_async_remote_copy(
-                kp.at[whose],
-                kp.at[whose],
+                group.at[whose],
+                group.at[whose],
                 ksend.at[n],
                 krecv.at[n],
                 device_id={"grp": to},
@@ -433,7 +432,7 @@
             )
 
         def landed(n, whose):
-            return pltpu.make_async_copy(kp.at[whose], kp.at[whose], krecv.at[n])
+            return pltpu.make_async_copy(group.at[whose], group.at[whose], krecv.at[n])
 
         to_row = pass_on(0, grp, engine.far_row)
         to_core = pass_on(1, grp, engine.far_core)
@@ -448,33 +447,36 @@
                 for x, part in ((x_p, own), (x_c, rest)):
                     hat, _ = norm_stats(x[...].astype(F32))
                     normed_one[part] = (hat * gain_one[...] + bias_one[...]).astype(BF)
+                    if part == own:
+                        group[grp] = normed_one[part]
+                        to_row.start()
+                        to_core.start()
                 for n in range(3):
                     lows[n] = low_of(mm_nt(normed_one[...], a_ext[n]), prompt_len)
                 for copy in loads:
                     copy.wait()
                 dlow_dn[...] = low_of(mm_nt(cot[...], b_dn[...]), prompt_len)
 
-            @pl.when(t == t_share)
-            def _():
-                kp[grp] = qkv[:prompt_len, width:]
-                to_row.start()
-                to_core.start()
-                stores[0].start()
-                stores[2].start()
-
             @pl.when(t == t_onward)
             def _():
                 landed(0, engine.far_row).wait()
                 onward.start()
 
-            @pl.when(t == t_head)
+            @pl.when(t == t_low)
             def _():
                 landed(1, engine.far_core).wait()
                 landed(2, diagonal).wait()
                 to_row.wait_send()
                 to_core.wait_send()
                 onward.wait_send()
-                stores[1].start()
+                for n in range(2):
+                    low = mm_nt(group[...].reshape(-1, width), a_ext[1 + n, :RANK])
+                    low_group[n] = low.astype(BF)
+
+            @pl.when(t == t_head)
+            def _():
+                for n in range(3):
+                    stores[n].start()
 
             @pl.when((t >= t_head) & (t < t_out))
             def _():
@@ -564,8 +566,20 @@
                 m = i // per
                 inside = pl.ds(pl.multiple_of(lax.rem(i, per) * BLOCK, BLOCK), BLOCK)
                 cols = pl.ds(pl.multiple_of(i * BLOCK, BLOCK), BLOCK)
-                extra = mm(lows[m], b_ext[m, :, inside])
-                qkv[:, cols] = (mm(normed_one[...], w) + extra).astype(BF)
+
+                @pl.when(m == 0)
+                def _():
+                    extra = mm(lows[0], b_ext[0, :, inside])
+                    qkv[:, cols] = (mm(normed_one[...], w) + extra).astype(BF)
+
+                @pl.when(m > 0)
+                def _():
+                    extra = mm(lows[m, rest], b_ext[m, :, inside])
+                    qkv[rest, cols] = (mm(normed_one[rest], w) + extra).astype(BF)
+                    extra = mm(low_group[m - 1], b_ext[m, :RANK, inside])
+                    shared = (mm(group[...].reshape(-1, width), w) + extra).astype(BF)
+                    there = pl.ds(pl.multiple_of((i - per) * BLOCK, BLOCK), BLOCK)
+                    kp[:, :, there] = shared.reshape(n_grp, prompt_len, BLOCK)
 
             @pl.when((n > 0) & (lax.rem(j, 2) == 0))
             def _():
@@ -638,6 +652,8 @@
         scratch_shapes=[
             pltpu.VMEM((rows, 3 * width), BF),
             pltpu.VMEM(share, BF),
+            pltpu.VMEM((n_grp, prompt_len, width), BF),
+            pltpu.VMEM((2, n_grp * prompt_len, RANK), BF),
             pltpu.VMEM((rows, width), BF),
             pltpu.VMEM((rows, width), BF),
             pltpu.VMEM((rows, width), BF),
@@ -1147,6 +1163,33 @@
     )
 
 
+def finish_call(rows, tables):
+    steps = (2, 4)
+
+    def kernel(*refs):
+        for src, dst in zip(refs[: len(refs) // 2], refs[len(refs) // 2 :]):
+            dst[...] = src[...].astype(dst.dtype)
+
+    def row_spec(v):
+        return pl.BlockSpec((v.shape[0] // 8, v.shape[1]), lambda a, n: (a * 4 + n, 0))
+
+    def table_spec(v):
+        if v.ndim == 4:
+            return pl.BlockSpec((1, 1) + v.shape[2:], lambda a, n: (a, n, 0, 0))
+        return pl.BlockSpec((1, v.shape[1], v.shape[2] // 4), lambda a, n: (a, 0, n))
+
+    specs = [row_spec(v) for v in rows] + [table_spec(v) for v in tables]
+    return pl.pallas_call(
+        kernel,
+        grid=steps,
+        in_specs=specs,
+        out_specs=specs,
+        out_shape=[jax.ShapeDtypeStruct(v.shape, BF) for v in rows]
+        + [jax.ShapeDtypeStruct(v.shape, F32) for v in tables],
+        name="finish",
+    )(*rows, *tables)
+
+
 def make_body(sizes):
     n_rep, n_grp, n_fs = sizes
     n_shard = n_grp * n_fs
@@ -1157,7 +1200,7 @@
             far = lax.ppermute(v, "rep", [(i, i ^ step) for i in range(n_rep)])
             v = (v.astype(F32) + far.astype(F32)).astype(BF)
             step *= 2
-        return v.astype(F32)
+        return v
 
     def body(
         prompt_input_rows,
@@ -1185,7 +1228,7 @@
         count = adapter_up_input.shape[0]
         hidden = frozen_up_weight.shape[1]
         shard_rows = frozen_query_key_value.shape[0]
-        assert n_grp == 4 and hidden == n_shard * BLOCK
+        assert n_grp == 4 and hidden == n_shard * BLOCK and count // n_fs == 2
         assert frozen_down_weight.shape[0] == BLOCK and BLOCK % shard_rows == 0
 
         def flat(v):
@@ -1255,17 +1298,21 @@
             n_fs,
             count,
         )
+        tables = [other_pairs(t) for t in (t_a, t_b, t_a_up, t_b_up, t_a_dn, t_b_dn)]
+        res_p, res_c, grad_p, grad_c, t_a, t_b, t_a_up, t_b_up, t_a_dn, t_b_dn = finish_call(
+            [res_p, res_c, grad_p, grad_c], tables
+        )
         return (
             res_p.reshape(prompt_input_rows.shape),
             res_c.reshape(continuation_input.shape),
             grad_p.reshape(prompt_input_rows.shape),
             grad_c.reshape(continuation_input.shape),
-            other_pairs(t_a).swapaxes(2, 3),
-            other_pairs(t_b),
-            other_pairs(t_a_up).swapaxes(1, 2),
-            other_pairs(t_b_up),
-            other_pairs(t_a_dn).swapaxes(1, 2),
-            other_pairs(t_b_dn),
+            t_a.swapaxes(2, 3),
+            t_b,
+            t_a_up.swapaxes(1, 2),
+            t_b_up,
+            t_a_dn.swapaxes(1, 2),
+            t_b_dn,
         )
 
     return body

time: 504 us -> 487 us (0.966)
  other arithmetic: 9.92 us -> 1.27 us
    pallas_call x1, Pallas kernels: 400 us -> 389 us  [forward_call(): pl.pallas_call(kernel, out_shape=[like((count, n_shard, shard_rows, PART)...]
    pallas_call x0 -> x1, Pallas kernels: none -> 7.49 us  [finish_call(): pl.pallas_call(kernel, grid=steps, in_specs=specs, out_specs=specs, out_s...]
where the time goes in v6:
time: 487 us
  Pallas kernels  483 us (99%)
    pallas_call x1, Pallas kernels, forward_call(): pl.pallas_call(kernel, out_shape=[like((count, n_shard, shard_rows, PART)...  389 us
    pallas_call x1, Pallas kernels, back_call(): pl.pallas_call(kernel, out_shape=[like(x_p.shape, BF), like(x_c.shape, BF...  83.4 us

profile of v6, /device:TPU:0, one launch (start us, length us, event | category | flops | bytes accessed | tf_op | source)
XLA Modules:
  0.0 486.6 jit_solution(8720483437384868999)
XLA Ops:
  1.9 0.6 broadcast_multiply_fusion
  2.5 0.1 broadcast_in_dim.21
  2.6 0.1 mul.18
  2.7 0.7 fusion.refs_7_
  3.4 3.4 select.3
  6.7 388.8 %forward.1 = (bf16[96,16,128,256]{3,2,1,0:T(8,128)(2,1)}, bf16[384,6144]{1,0:T(8,128)(2,1)}, bf16[4,128,4096]{2,1,0:T(8,128)(2,1)}, bf16[384,2048]{1,0:T(8,128)(...) custom-call(bf16[128,2048]{1,0:T(8,128)(2,1)} %bitcast.24, ...), custom_call_target="tpu_custom_call" | custom-call | tf_op jit(solution)/shard_map/forward/pallas_call | solution.py:634
  395.5 83.4 %back.1 = (bf16[128,2048]{1,0:T(8,128)(2,1)}, bf16[256,2048]{1,0:T(8,128)(2,1)}, bf16[2,4,16,2048]{3,2,1,0:T(8,128)(2,1)}, bf16[2,4,16,2048]{3,2,1,0:T(8,128)(2,...) custom-call(bf16[384,2048]{1,0:T(8,128)(2,1)} %get-tuple-element.54., ...), custom_call_target="tpu_custom_call" | custom-call | tf_op jit(solution)/shard_map/back/pallas_call | solution.py:1118
  478.9 7.5 %finish.1 = (bf16[128,2048]{1,0:T(8,128)(2,1)}, bf16[256,2048]{1,0:T(8,128)(2,1)}, bf16[128,2048]{1,0:T(8,128)(2,1)}, bf16[256,2048]{1,0:T(8,128)(2,1)}, f32[2,4...) custom-call(bf16[128,2048]{1,0:T(8,128)(2,1)} %get-tuple-element.52., ...), custom_call_target="tpu_custom_call" | custom-call | tf_op jit(solution)/shard_map/finish/pallas_call | solution.py:1182
  (1 shorter events, 0.0 us)

commit v7 on v6

--- a/solution.py
+++ b/solution.py
@@ -12,8 +12,8 @@
 RANK = 16
 BLOCK = 512
 PART = 256
-AWAY = (40, 48)
-ALONG = 40
+AWAY = (32, 48)
+ALONG = 16
 SCALE = HDIM ** (-0.5)
 NEG_FILL = -1e30
 BF = jnp.bfloat16

time: 487 us -> 480 us (0.986)
  Pallas kernels: 483 us -> 476 us
    pallas_call x1, Pallas kernels: 389 us -> 380 us  [forward_call(): pl.pallas_call(kernel, out_shape=[like((count, n_shard, shard_rows, PART)...]
where the time goes in v7:
time: 480 us; the launch traced here: 479 us
  Pallas kernels  476 us (99%)
    pallas_call x1, Pallas kernels, forward_call(): pl.pallas_call(kernel, out_shape=[like((count, n_shard, shard_rows, PART)...  380 us
    pallas_call x1, Pallas kernels, back_call(): pl.pallas_call(kernel, out_shape=[like(x_p.shape, BF), like(x_c.shape, BF...  84.3 us

profile of v7, /device:TPU:0, one launch (start us, length us, event | category | flops | bytes accessed | tf_op | source)
XLA Modules:
  0.0 479.1 jit_solution(12371923299931745135)
XLA Ops:
  1.9 0.6 broadcast_multiply_fusion
  2.5 0.1 broadcast_in_dim.21
  2.6 0.1 mul.18
  2.7 0.7 fusion.refs_7_
  3.4 3.4 select.3
  6.7 380.3 %forward.1 = (bf16[96,16,128,256]{3,2,1,0:T(8,128)(2,1)}, bf16[384,6144]{1,0:T(8,128)(2,1)}, bf16[4,128,4096]{2,1,0:T(8,128)(2,1)}, bf16[384,2048]{1,0:T(8,128)(...) custom-call(bf16[128,2048]{1,0:T(8,128)(2,1)} %bitcast.24, ...), custom_call_target="tpu_custom_call" | custom-call | tf_op jit(solution)/shard_map/forward/pallas_call | solution.py:634
  387.1 84.3 %back.1 = (bf16[128,2048]{1,0:T(8,128)(2,1)}, bf16[256,2048]{1,0:T(8,128)(2,1)}, bf16[2,4,16,2048]{3,2,1,0:T(8,128)(2,1)}, bf16[2,4,16,2048]{3,2,1,0:T(8,128)(2,...) custom-call(bf16[384,2048]{1,0:T(8,128)(2,1)} %get-tuple-element.54., ...), custom_call_target="tpu_custom_call" | custom-call | tf_op jit(solution)/shard_map/back/pallas_call | solution.py:1118
  471.4 7.5 %finish.1 = (bf16[128,2048]{1,0:T(8,128)(2,1)}, bf16[256,2048]{1,0:T(8,128)(2,1)}, bf16[128,2048]{1,0:T(8,128)(2,1)}, bf16[256,2048]{1,0:T(8,128)(2,1)}, f32[2,4...) custom-call(bf16[128,2048]{1,0:T(8,128)(2,1)} %get-tuple-element.52., ...), custom_call_target="tpu_custom_call" | custom-call | tf_op jit(solution)/shard_map/finish/pallas_call | solution.py:1182
  (1 shorter events, 0.0 us)

commit v8 on v7

--- a/solution.py
+++ b/solution.py
@@ -851,7 +851,7 @@
     n_qkv = 3 * per
     piece = width // PIECES
     adapters = count // n_fs
-    groups = 4
+    groups = 8
     group_heads = heads // groups
     half = group_heads * HDIM
     two = 2 * RANK

time: 480 us -> 478 us (level)
  no operation moved by 1% of the time
where the time goes in v8:
time: 478 us
  Pallas kernels  474 us (99%)
    pallas_call x1, Pallas kernels, forward_call(): pl.pallas_call(kernel, out_shape=[like((count, n_shard, shard_rows, PART)...  380 us
    pallas_call x1, Pallas kernels, back_call(): pl.pallas_call(kernel, out_shape=[like(x_p.shape, BF), like(x_c.shape, BF...  83 us

profile of v8, /device:TPU:0, one launch (start us, length us, event | category | flops | bytes accessed | tf_op | source)
XLA Modules:
  0.0 477.8 jit_solution(17111713079367851343)
XLA Ops:
  1.9 0.6 broadcast_multiply_fusion
  2.5 0.1 broadcast_in_dim.21
  2.6 0.1 mul.18
  2.7 0.7 fusion.refs_7_
  3.4 3.4 select.3
  6.7 380.3 %forward.1 = (bf16[96,16,128,256]{3,2,1,0:T(8,128)(2,1)}, bf16[384,6144]{1,0:T(8,128)(2,1)}, bf16[4,128,4096]{2,1,0:T(8,128)(2,1)}, bf16[384,2048]{1,0:T(8,128)(...) custom-call(bf16[128,2048]{1,0:T(8,128)(2,1)} %bitcast.24, ...), custom_call_target="tpu_custom_call" | custom-call | tf_op jit(solution)/shard_map/forward/pallas_call | solution.py:634
  387.1 83.0 %back.1 = (bf16[128,2048]{1,0:T(8,128)(2,1)}, bf16[256,2048]{1,0:T(8,128)(2,1)}, bf16[2,4,16,2048]{3,2,1,0:T(8,128)(2,1)}, bf16[2,4,16,2048]{3,2,1,0:T(8,128)(2,...) custom-call(bf16[384,2048]{1,0:T(8,128)(2,1)} %get-tuple-element.54., ...), custom_call_target="tpu_custom_call" | custom-call | tf_op jit(solution)/shard_map/back/pallas_call | solution.py:1118
  470.1 7.5 %finish.1 = (bf16[128,2048]{1,0:T(8,128)(2,1)}, bf16[256,2048]{1,0:T(8,128)(2,1)}, bf16[128,2048]{1,0:T(8,128)(2,1)}, bf16[256,2048]{1,0:T(8,128)(2,1)}, f32[2,4...) custom-call(bf16[128,2048]{1,0:T(8,128)(2,1)} %get-tuple-element.52., ...), custom_call_target="tpu_custom_call" | custom-call | tf_op jit(solution)/shard_map/finish/pallas_call | solution.py:1182
  (1 shorter events, 0.0 us)
